TPU v7x, 32 devices: a whole 2x2x4 slice. The times are simulated.
32 devices in a mesh: dev: 32 (over z, y, x, core).
Axes of the slice: x: 2, y: 2, z: 4, core: 2. Of those that a mesh axis runs over, the one named last changes fastest.
Arguments:
- runs_field: float32 [512, 256, 256], P('dev'), may hold values from -6 to 6
- spectral_filter: float32 [256, 129], replicated, may hold values from 0.3 to 3, as said below
- block_inverses: float32 [2, 256, 256], replicated, may hold values from -1.5 to 1.5, as said below
- factor_panels: float32 [2, 512, 256], P(None, 'dev'), may hold values from -0.375 to 0.375
Outputs:
- solved: float32 [512, 65536], P(None, 'dev')
Inputs may be any that keep to these rules, and one draw needn't show every extreme that they name: `spectral_filter`: symmetric under the first frequency index k -> (256 - k) mod 256 in columns 0 and 128. `block_inverses`: each block is lower triangular with diagonal entries from 0.7 to 1.4.
All inputs are finite; a program needn't handle non-finite values.
Results may differ from a plain program's by a relative error of at most 0.000076.
Values sent between devices are 32-bit elements; how exact they have to be, the bound alone decides.
No kernel may reach another device: no remote copies, remote signals or barrier semaphores. Data moves between devices by JAX's collectives and lax.ppermute only.
A program may use at most 64 MiB of HBM per device.

v0:
```python
import functools, math
LANES = 128
import numpy as np
import jax, jax.numpy as jnp
from jax import lax
from jax.experimental import pallas as pl
from jax.experimental.pallas import tpu as pltpu
from jax.sharding import PartitionSpec as P

def basis(length):
    half = length // 2
    slot = np.arange(length)
    freq = np.where(slot <= half, slot, slot - half)
    phase = np.outer(np.arange(length), freq) % length
    angle = phase * (2.0 * math.pi / length)
    table = np.where(slot[None, :] <= half, np.cos(angle), np.sin(angle))
    hi = table.astype(jnp.bfloat16)
    lo = (table - hi.astype(np.float64)).astype(jnp.bfloat16)
    return hi, lo

def split(x):
    hi = x.astype(jnp.bfloat16)
    lo = (x - hi.astype(jnp.float32)).astype(jnp.bfloat16)
    return hi, lo

def mm(a, b):
    return lax.dot_general(a, b, (((1,), (0,)), ((), ())), preferred_element_type=jnp.float32)

def gains(filter_t, length):
    half = length // 2
    row = lax.broadcasted_iota(jnp.int32, (length, length), 0)
    col = lax.broadcasted_iota(jnp.int32, (length, length), 1)
    freq = jnp.where(row <= half, row, row - half)
    edge = (freq == 0) | (freq == half)
    plus = (col == freq).astype(jnp.float32)
    minus = (col == length - freq).astype(jnp.float32)
    minus = jnp.where(edge, 0.0, minus)
    plus_only = jnp.where(edge, 0.0, plus)
    sums = (plus + minus).astype(jnp.bfloat16)
    diffs = (plus_only - minus).astype(jnp.bfloat16)
    low = filter_t[:half]
    k = lax.broadcasted_iota(jnp.int32, (half, length), 0)
    high = jnp.where(k == 0, jnp.broadcast_to(filter_t[half:half + 1], (half, length)), low)
    def pick(sel, table):
        out = None
        rest = table
        for _ in range(3):
            piece = rest.astype(jnp.bfloat16)
            rest = rest - piece.astype(jnp.float32)
            part = lax.dot_general(sel, piece, (((1,), (1,)), ((), ())), preferred_element_type=jnp.float32)
            out = part if out is None else out + part
        return out
    tab = jnp.concatenate([low, high], axis=0)
    s = pick(sums, tab)
    d = pick(diffs, tab)
    kk = jnp.where(col <= half, col, col - half)
    kedge = (kk == 0) | (kk == half)
    scale = 1.0 / float(length * length)
    s = s * jnp.where(kedge, scale, 2.0 * scale)
    same = (row < half) == (col < half)
    d = d * jnp.where(kedge, 0.0, jnp.where(same, -2.0 * scale, 2.0 * scale))
    return s, d

def whiten_kernel(x_ref, ft_ref, fh_ref, fl_ref, th_ref, tl_ref, o_ref, g1_ref, g2_ref, *, rb, groups):
    length = x_ref.shape[1]
    half = length // 2
    @pl.when(pl.program_id(0) == 0)
    def _():
        s, d = gains(ft_ref[...], length)
        g1_ref[...] = s
        g2_ref[...] = d
    fh = fh_ref[...]; fl = fl_ref[...]; th = th_ref[...]; tl = tl_ref[...]
    def right(x, h, l):
        xh, xl = split(x)
        return mm(xh, h) + mm(xh, l) + mm(xl, h)
    def left(h, l, x):
        xh, xl = split(x)
        return mm(h, xh) + mm(l, xh) + mm(h, xl)
    z = right(x_ref[...].reshape(rb * length, length), fh, fl)
    vs = []
    for r in range(rb):
        t = left(th, tl, z[r * length:(r + 1) * length])
        sw = jnp.concatenate([
            jnp.concatenate([t[half:, half:], t[half:, :half]], axis=1),
            jnp.concatenate([t[:half, half:], t[:half, :half]], axis=1)], axis=0)
        t = g1_ref[...] * t + g2_ref[...] * sw
        vs.append(left(fh, fl, t))
    y = right(jnp.concatenate(vs, axis=0), th, tl)
    rows = length // groups
    for r in range(rb):
        for part in range(o_ref.shape[2]):
            o_ref[:, r, part] = y[r * length:(r + 1) * length, part * LANES:(part + 1) * LANES].reshape(groups, rows, LANES)

def whiten(x, spectral_filter, groups, start=0, count=None, rb=2):
    runs, length, _ = x.shape
    count = runs if count is None else count
    rows = length // groups
    fh, fl = basis(length)
    const = lambda shape: pl.BlockSpec(shape, lambda i: (0,) * len(shape), pipeline_mode=pl.Buffered(1))
    off = start // rb
    return pl.pallas_call(
        functools.partial(whiten_kernel, rb=rb, groups=groups),
        grid=(count // rb,),
        in_specs=[pl.BlockSpec((rb, length, length), lambda i: (i + off, 0, 0)),
                  const((spectral_filter.shape[1], length))] + [const((length, length))] * 4,
        out_specs=pl.BlockSpec((groups, rb, length // LANES, rows, LANES), lambda i: (0, i, 0, 0, 0)),
        out_shape=jax.ShapeDtypeStruct((groups, count, length // LANES, rows, LANES), jnp.float32),
        scratch_shapes=[pltpu.VMEM((length, length), jnp.float32)] * 2,
        name="whiten",
    )(x, spectral_filter.T, fh, fl, fh.T, fl.T)

def solve_kernel(w_ref, mh_ref, ml_ref, *rest, rows, acc):
    a_ref, o_ref = rest if acc else (None, rest[0])
    k = mh_ref.shape[1]
    i = pl.program_id(0)
    parts = w_ref.shape[0] // (k * rows)
    w = jnp.concatenate([w_ref[pl.ds(i + p * rows, k, stride=rows * parts), :] for p in range(parts)], axis=1)
    wh, wl = split(w)
    mh = mh_ref[...]; ml = ml_ref[...]
    out = mm(mh, wh) + mm(mh, wl) + mm(ml, wh)
    o_ref[...] = out + a_ref[...] if acc else out

def solve(w, mh, ml, acc=None):
    src, runs, parts, rows, lanes = w.shape
    length = parts * lanes
    q, k = mh.shape
    const = lambda shape: pl.BlockSpec(shape, lambda i: (0,) * len(shape), pipeline_mode=pl.Buffered(1))
    tile = pl.BlockSpec((q, length), lambda i: (0, i))
    w = w.reshape(src * runs * parts * rows, lanes)
    args = (w, mh, ml) + (() if acc is None else (acc,))
    return pl.pallas_call(
        functools.partial(solve_kernel, rows=rows, acc=acc is not None),
        grid=(rows,),
        in_specs=[const(w.shape), const((q, k)), const((q, k))] + ([] if acc is None else [tile]),
        out_specs=tile,
        out_shape=jax.ShapeDtypeStruct((q, rows * length), jnp.float32),
        input_output_aliases={} if acc is None else {3: 0},
        name="solve",
    )(*args)


def precise_dot(a, b):
    return jnp.dot(a, b, precision=lax.Precision.HIGHEST, preferred_element_type=jnp.float32)


def split_outside(x):
    hi = lax.reduce_precision(x, 8, 7)
    return hi.astype(jnp.bfloat16), (x - hi).astype(jnp.bfloat16)


def gather_panels(mine):
    groups = lax.axis_size("dev")
    me = lax.axis_index("dev")
    held = mine[None]
    bit = groups // 2
    while bit:
        pairs = [(i, i ^ bit) for i in range(groups)]
        held = jnp.concatenate([held, lax.ppermute(held, "dev", pairs)], axis=0)
        bit //= 2
    order = np.zeros(1, np.int32)
    bit = groups // 2
    while bit:
        order = np.concatenate([order, order ^ bit])
        bit //= 2
    place = np.argsort(order).astype(np.int32)
    held = jnp.take(held, jnp.asarray(place)[jnp.arange(groups) ^ me], axis=0)
    return jnp.moveaxis(held, 0, 1).reshape(mine.shape[0], -1, mine.shape[2])


def mixing(block_inverses, panels, total):
    width = block_inverses.shape[1]
    first, second = block_inverses[0], block_inverses[1]
    below = -precise_dot(second, precise_dot(panels[0, width : 2 * width], first))
    top = jnp.concatenate([first, jnp.zeros_like(first)], axis=1)
    rows = [top, jnp.concatenate([below, second], axis=1)]
    if total > 2 * width:
        left, right = panels[0, 2 * width :], panels[1, 2 * width :]
        rows.append(
            -jnp.concatenate(
                [precise_dot(left, first) + precise_dot(right, below), precise_dot(right, second)],
                axis=1,
            )
        )
    return jnp.concatenate(rows, axis=0)


def per_device(runs_field, spectral_filter, block_inverses, factor_panels):
    groups = lax.axis_size("dev")
    local, length, _ = runs_field.shape
    total = local * groups
    width = block_inverses.shape[1]
    pieces = whiten(runs_field, spectral_filter, groups, rb=4)
    arrived = lax.all_to_all(pieces, "dev", 0, 0, tiled=True)
    needed = 1 if total == 2 * width else 2
    panels = gather_panels(factor_panels[:needed])
    high, low = split_outside(mixing(block_inverses, panels, total))
    used = 2 * width // local
    out = solve(arrived[:used], high, low)
    if total > 2 * width:
        rest = jnp.moveaxis(arrived[used:], 2, 3).reshape(total - 2 * width, -1)
        out = jnp.concatenate([out[: 2 * width], out[2 * width :] + rest], axis=0)
    return out


def solution(mesh):
    return jax.shard_map(
        per_device,
        mesh=mesh,
        in_specs=(P("dev", None, None), P(), P(), P(None, "dev", None)),
        out_specs=P(None, "dev"),
        check_vma=False,
    )
```

profile of v0, /device:TPU:0, one launch (start us, length us, event | category | flops | bytes accessed | tf_op | source)
XLA Modules:
  0.0 142.3 jit_solution(15582166441925268551)
XLA Ops:
  0.0 13.9 %whiten.1 = f32[32,16,2,8,128]{4,3,2,1,0:T(8,128)} custom-call(f32[16,256,256]{2,1,0:T(8,128)} %x_ref.1, f32[129,256]{1,0:T(8,128)} %bitcast.32, bf16[256,256]{1,0:T(8,128)(2,1)} %constant.34.clone.fh_ref, bf16[256,256]{1,0:T(8,128)(2,1)} %constant.35.clone.fl_ref, bf16[256,256]{1,0:T(8,128)(2,1)} %constant.36.clone.th_ref, ...), custom_call_target="tpu_custom_call" | custom-call | tf_op jit(solution)/shard_map/whiten/pallas_call | solution.py:101
  13.9 0.0 copy-start.2
  13.9 0.0 copy-start
  13.9 0.0 copy-start.1
  13.9 7.5 %all-to-all-start = ((f32[32,16,2,8,128]{4,3,2,1,0:T(8,128)}), f32[32,16,2,8,128]{4,3,2,1,0:T(8,128)}, u32[]{:S(2)}, u32[]{:S(2)}) async-start(f32[32,16,2,8,128]{4,3,2,1,0:T(8,128)} %whiten.1), calls=%async_computation | async-start | bytes 8388608 | tf_op jit(solution)/shard_map/all_to_all | solution.py:193
  21.4 0.0 copy-done.2
  21.4 2.7 %collective-permute-start = (f32[1,1,16,256]{3,2,1,0:T(8,128)S(1)}, f32[1,1,16,256]{3,2,1,0:T(8,128)S(1)}, u32[]{:S(2)}, u32[]{:S(2)}) collective-permute-start(f32[1,1,16,256]{3,2,1,0:T(8,128)S(1)} %slice_bitcast_fusion.2), channel_id=1, source_target_pairs={{0,16},{1,17},{2,18},{3,19},{4,20},{5,21},{6,22},{7,23},{8,24},{9,... | collective-permute-start | bytes 49160 | tf_op jit(solution)/shard_map/ppermute | solution.py:158
  24.1 0.0 copy-done
  24.1 0.7 gather_fusion
  24.8 90.9 %collective-permute-done = f32[1,1,16,256]{3,2,1,0:T(8,128)S(1)} collective-permute-done((f32[1,1,16,256]{3,2,1,0:T(8,128)S(1)}, f32[1,1,16,256]{3,2,1,0:T(8,128)S(1)}, u32[]{:S(2)}, u32[]{:S(2)}) %collective-permute-start) | collective-permute-done | bytes 16416 | tf_op jit(solution)/shard_map/ppermute | solution.py:158
  115.7 0.0 collective-permute-start.1
  115.7 3.9 %collective-permute-done.1 = f32[2,1,16,256]{3,2,1,0:T(8,128)S(1)} collective-permute-done((f32[2,1,16,256]{3,2,1,0:T(8,128)S(1)}, f32[2,1,16,256]{3,2,1,0:T(8,128)S(1)}, u32[]{:S(2)}, u32[]{:S(2)}) %collective-permute-start.1) | collective-permute-done | bytes 32800 | tf_op jit(solution)/shard_map/ppermute | solution.py:158
  119.6 1.4 collective-permute-start.2
  121.0 2.9 %collective-permute-done.2 = f32[4,1,16,256]{3,2,1,0:T(8,128)S(1)} collective-permute-done((f32[4,1,16,256]{3,2,1,0:T(8,128)S(1)}, f32[4,1,16,256]{3,2,1,0:T(8,128)S(1)}, u32[]{:S(2)}, u32[]{:S(2)}) %collective-permute-start.2) | collective-permute-done | bytes 65568 | tf_op jit(solution)/shard_map/ppermute | solution.py:158
  123.9 1.5 %collective-permute-start.3 = (f32[8,1,16,256]{3,2,1,0:T(8,128)S(1)}, f32[8,1,16,256]{3,2,1,0:T(8,128)S(1)}, u32[]{:S(2)}, u32[]{:S(2)}) collective-permute-start(f32[8,1,16,256]{3,2,1,0:T(8,128)S(1)} %pad_maximum_fusion), channel_id=1, source_target_pairs={{0,2},{1,3},{2,0},{3,1},{4,6},{5,7},{6,4},{7,5},{8,10},{9,11},{10,... | collective-permute-start | bytes 393224 | tf_op jit(solution)/shard_map/ppermute | solution.py:158
  125.4 3.5 %collective-permute-done.3 = f32[8,1,16,256]{3,2,1,0:T(8,128)S(1)} collective-permute-done((f32[8,1,16,256]{3,2,1,0:T(8,128)S(1)}, f32[8,1,16,256]{3,2,1,0:T(8,128)S(1)}, u32[]{:S(2)}, u32[]{:S(2)}) %collective-permute-start.3) | collective-permute-done | bytes 131104 | tf_op jit(solution)/shard_map/ppermute | solution.py:158
  129.0 0.1 collective-permute-start.4
  129.1 0.1 broadcast_in_dim.19
  129.1 0.1 broadcast_in_dim.20
  129.2 0.0 copy-done.1
  129.3 1.3 collective-permute-done.4
  130.6 0.6 gather_fusion.1
  131.2 0.4 fusion.3
  131.6 0.4 fusion
  132.0 1.1 fusion.1
  133.1 0.0 all-to-all-done
  133.1 9.2 %solve.1 = f32[512,2048]{1,0:T(8,128)} custom-call(f32[8192,128]{1,0:T(8,128)} %bitcast.1.w_ref, bf16[512,512]{1,0:T(8,128)(2,1)} %get-tuple-element.6.mh_ref, bf16[512,512]{1,0:T(8,128)(2,1)} %get-tuple-element.5.ml_ref), custom_call_target="tpu_custom_call" | custom-call | tf_op jit(solution)/shard_map/solve/pallas_call | solution.py:131
  (17 shorter events, 0.2 us)
Async XLA Ops:
  13.9 7.5 %copy-start.2 = (f32[2,16,256]{2,1,0:T(8,128)S(1)}, f32[2,16,256]{2,1,0:T(8,128)}, u32[]{:S(2)}) copy-start(f32[2,16,256]{2,1,0:T(8,128)} %param.12) | copy-start | bytes 98308
  13.9 10.2 %copy-start = (s32[32]{0:T(128)S(1)}, s32[32]{0:T(128)}, u32[]{:S(2)}) copy-start(s32[32]{0:T(128)} %constant.38.clone) | copy-start | bytes 388
  13.9 115.3 %copy-start.1 = (f32[2,256,256]{2,1,0:T(8,128)S(1)}, f32[2,256,256]{2,1,0:T(8,128)}, u32[]{:S(2)}) copy-start(f32[2,256,256]{2,1,0:T(8,128)} %param.11) | copy-start | bytes 1572868
  13.9 119.2 %all-to-all-start = ((f32[32,16,2,8,128]{4,3,2,1,0:T(8,128)}), f32[32,16,2,8,128]{4,3,2,1,0:T(8,128)}, u32[]{:S(2)}, u32[]{:S(2)}) async-start(f32[32,16,2,8,128]{4,3,2,1,0:T(8,128)} %whiten.1), calls=%async_computation | async-start | bytes 8388608 | tf_op jit(solution)/shard_map/all_to_all | solution.py:193
  21.4 94.3 %collective-permute-start = (f32[1,1,16,256]{3,2,1,0:T(8,128)S(1)}, f32[1,1,16,256]{3,2,1,0:T(8,128)S(1)}, u32[]{:S(2)}, u32[]{:S(2)}) collective-permute-start(f32[1,1,16,256]{3,2,1,0:T(8,128)S(1)} %slice_bitcast_fusion.2), channel_id=1, source_target_pairs={{0,16},{1,17},{2,18},{3,19},{4,20},{5,21},{6,22},{7,23},{8,24},{9,... | collective-permute-start | bytes 49160 | tf_op jit(solution)/shard_map/ppermute | solution.py:158
  115.7 3.9 %collective-permute-start.1 = (f32[2,1,16,256]{3,2,1,0:T(8,128)S(1)}, f32[2,1,16,256]{3,2,1,0:T(8,128)S(1)}, u32[]{:S(2)}, u32[]{:S(2)}) collective-permute-start(f32[2,1,16,256]{3,2,1,0:T(8,128)S(1)} %pad_maximum_fusion.2), channel_id=1, source_target_pairs={{0,8},{1,9},{2,10},{3,11},{4,12},{5,13},{6,14},{7,15},{8,0},{9,1},... | collective-permute-start | bytes 98312 | tf_op jit(solution)/shard_map/ppermute | solution.py:158
  119.6 4.3 %collective-permute-start.2 = (f32[4,1,16,256]{3,2,1,0:T(8,128)S(1)}, f32[4,1,16,256]{3,2,1,0:T(8,128)S(1)}, u32[]{:S(2)}, u32[]{:S(2)}) collective-permute-start(f32[4,1,16,256]{3,2,1,0:T(8,128)S(1)} %pad_maximum_fusion.1), channel_id=1, source_target_pairs={{0,4},{1,5},{2,6},{3,7},{4,0},{5,1},{6,2},{7,3},{8,12},{9,13},{10,... | collective-permute-start | bytes 196616 | tf_op jit(solution)/shard_map/ppermute | solution.py:158
  123.9 5.0 %collective-permute-start.3 = (f32[8,1,16,256]{3,2,1,0:T(8,128)S(1)}, f32[8,1,16,256]{3,2,1,0:T(8,128)S(1)}, u32[]{:S(2)}, u32[]{:S(2)}) collective-permute-start(f32[8,1,16,256]{3,2,1,0:T(8,128)S(1)} %pad_maximum_fusion), channel_id=1, source_target_pairs={{0,2},{1,3},{2,0},{3,1},{4,6},{5,7},{6,4},{7,5},{8,10},{9,11},{10,... | collective-permute-start | bytes 393224 | tf_op jit(solution)/shard_map/ppermute | solution.py:158
  129.0 1.6 %collective-permute-start.4 = (f32[16,1,16,256]{3,2,1,0:T(8,128)S(1)}, f32[16,1,16,256]{3,2,1,0:T(8,128)S(1)}, u32[]{:S(2)}, u32[]{:S(2)}) collective-permute-start(f32[16,1,16,256]{3,2,1,0:T(8,128)S(1)} %get-tuple-element.9), channel_id=1, source_target_pairs={{0,1},{1,0},{2,3},{3,2},{4,5},{5,4},{6,7},{7,6},{8,9},{9,8},{10,11... | collective-permute-start | bytes 786440 | tf_op jit(solution)/shard_map/ppermute | solution.py:158
where the time goes:
time: 142 us
  waiting for transfers between devices  102 us (72%)
  Pallas kernels  23.1 us (16%)
  starting transfers between devices  13.1 us (9%)
  local copies, waits for them, and re-layouts  1.57 us (1%)
    ppermute x5, waiting for transfers between devices, gather_panels(): held = jnp.concatenate([held, lax.ppermute(held, 'dev', pairs)], axis=0)  102 us
    pallas_call x1, Pallas kernels, whiten(): pl.pallas_call(functools.partial(whiten_kernel, rb=rb, groups=groups), gr...  13.9 us
    pallas_call x1, Pallas kernels, solve(): pl.pallas_call(functools.partial(solve_kernel, rows=rows, acc=acc is not...  9.17 us
    all_to_all x1, starting transfers between devices, per_device(): arrived = lax.all_to_all(pieces, 'dev', 0, 0, tiled=True)  7.46 us
    ppermute x5, starting transfers between devices, gather_panels(): held = jnp.concatenate([held, lax.ppermute(held, 'dev', pairs)], axis=0)  5.62 us
  transfers between devices with their start and end apart: 6, of which 5 were waited for; matrix products, arithmetic and copies ran while one was open for 2% of the time, Pallas kernels for 0%

commit v1 on v0

v1 whole, which is shorter than its diff:
```python
import functools, math
LANES = 128
import numpy as np
import jax, jax.numpy as jnp
from jax import lax
from jax.experimental import pallas as pl
from jax.experimental.pallas import tpu as pltpu
from jax.sharding import PartitionSpec as P


def basis(length):
    half = length // 2
    slot = np.arange(length)
    freq = np.where(slot <= half, slot, slot - half)
    phase = np.outer(np.arange(length), freq) % length
    angle = phase * (2.0 * math.pi / length)
    table = np.where(slot[None, :] <= half, np.cos(angle), np.sin(angle))
    hi = table.astype(jnp.bfloat16)
    lo = (table - hi.astype(np.float64)).astype(jnp.bfloat16)
    return hi, lo


def split(x):
    hi = x.astype(jnp.bfloat16)
    lo = (x - hi.astype(jnp.float32)).astype(jnp.bfloat16)
    return hi, lo


def mm(a, b):
    return lax.dot_general(a, b, (((1,), (0,)), ((), ())), preferred_element_type=jnp.float32)


def gains(filter_t, length):
    half = length // 2
    row = lax.broadcasted_iota(jnp.int32, (length, length), 0)
    col = lax.broadcasted_iota(jnp.int32, (length, length), 1)
    freq = jnp.where(row <= half, row, row - half)
    edge = (freq == 0) | (freq == half)
    plus = (col == freq).astype(jnp.float32)
    minus = (col == length - freq).astype(jnp.float32)
    minus = jnp.where(edge, 0.0, minus)
    plus_only = jnp.where(edge, 0.0, plus)
    sums = (plus + minus).astype(jnp.bfloat16)
    diffs = (plus_only - minus).astype(jnp.bfloat16)
    low = filter_t[:half]
    k = lax.broadcasted_iota(jnp.int32, (half, length), 0)
    high = jnp.where(k == 0, jnp.broadcast_to(filter_t[half:half + 1], (half, length)), low)

    def pick(sel, table):
        out = None
        rest = table
        for _ in range(3):
            piece = rest.astype(jnp.bfloat16)
            rest = rest - piece.astype(jnp.float32)
            part = lax.dot_general(sel, piece, (((1,), (1,)), ((), ())), preferred_element_type=jnp.float32)
            out = part if out is None else out + part
        return out

    tab = jnp.concatenate([low, high], axis=0)
    s = pick(sums, tab)
    d = pick(diffs, tab)
    kk = jnp.where(col <= half, col, col - half)
    kedge = (kk == 0) | (kk == half)
    scale = 1.0 / float(length * length)
    s = s * jnp.where(kedge, scale, 2.0 * scale)
    same = (row < half) == (col < half)
    d = d * jnp.where(kedge, 0.0, jnp.where(same, -2.0 * scale, 2.0 * scale))
    return s, d


def whiten_kernel(me_ref, x_ref, ft_ref, fh_ref, fl_ref, th_ref, tl_ref, *rest, rb, groups, outs):
    o_refs, (g1_ref, g2_ref), stage = rest[:outs], rest[outs:outs + 2], rest[outs + 2:]
    length = x_ref.shape[1]
    half = length // 2

    @pl.when(pl.program_id(0) == 0)
    def _():
        s, d = gains(ft_ref[...], length)
        g1_ref[...] = s
        g2_ref[...] = d

    fh, fl, th, tl = fh_ref[...], fl_ref[...], th_ref[...], tl_ref[...]

    def right(x, h, l):
        xh, xl = split(x)
        return mm(xh, h) + mm(xh, l) + mm(xl, h)

    def left(h, l, x):
        xh, xl = split(x)
        return mm(h, xh) + mm(l, xh) + mm(h, xl)

    z = right(x_ref[...].reshape(rb * length, length), fh, fl)
    vs = []
    for r in range(rb):
        t = left(th, tl, z[r * length:(r + 1) * length])
        sw = jnp.concatenate([
            jnp.concatenate([t[half:, half:], t[half:, :half]], axis=1),
            jnp.concatenate([t[:half, half:], t[:half, :half]], axis=1)], axis=0)
        t = g1_ref[...] * t + g2_ref[...] * sw
        vs.append(left(fh, fl, t))
    y = right(jnp.concatenate(vs, axis=0), th, tl)
    rows = length // groups
    target = stage[0] if stage else o_refs[0]
    for r in range(rb):
        for part in range(length // LANES):
            target[:, r, part] = y[r * length:(r + 1) * length, part * LANES:(part + 1) * LANES].reshape(groups, rows, LANES)
    if stage:
        chip = me_ref[0] // 2
        for k, o_ref in enumerate(o_refs):
            o_ref[...] = target[pl.ds(2 * (chip ^ k), 2)]


def whiten(me, x, spectral_filter, groups, start, count, rb, spread):
    length = x.shape[1]
    rows, parts = length // groups, length // LANES
    fh, fl = basis(length)
    const = lambda shape: pl.BlockSpec(shape, lambda i, me: (0,) * len(shape), pipeline_mode=pl.Buffered(1))
    off = start // rb
    outs, lead = (groups // 2, 2) if spread else (1, groups)
    scratch = [pltpu.VMEM((length, length), jnp.float32)] * 2
    if spread:
        scratch.append(pltpu.VMEM((groups, rb, parts, rows, LANES), jnp.float32))
    return pl.pallas_call(
        functools.partial(whiten_kernel, rb=rb, groups=groups, outs=outs),
        grid_spec=pltpu.PrefetchScalarGridSpec(
            num_scalar_prefetch=1,
            grid=(count // rb,),
            in_specs=[pl.BlockSpec((rb, length, length), lambda i, me: (i + off, 0, 0)),
                      const((spectral_filter.shape[1], length))] + [const((length, length))] * 4,
            out_specs=[pl.BlockSpec((lead, rb, parts, rows, LANES), lambda i, me: (0, i, 0, 0, 0))] * outs,
            scratch_shapes=scratch,
        ),
        out_shape=[jax.ShapeDtypeStruct((lead, count, parts, rows, LANES), jnp.float32)] * outs,
        name="whiten",
    )(me, x, spectral_filter.T, fh, fl, fh.T, fl.T)


def solve_kernel(me_ref, *refs, rows, parts, sizes, acc):
    n = len(sizes)
    w_refs, (mh_ref, ml_ref) = refs[:n], refs[n:n + 2]
    o_ref = refs[-1]
    i = pl.program_id(0)
    pieces = [
        jnp.concatenate([w_ref[pl.ds(p * rows + i, k, stride=rows * parts), :] for p in range(parts)], axis=1)
        for w_ref, k in zip(w_refs, sizes)
    ]
    wh, wl = split(jnp.concatenate(pieces, axis=0) if n > 1 else pieces[0])
    mh, ml = mh_ref[...], ml_ref[...]
    out = mm(mh, wh) + mm(mh, wl) + mm(ml, wh)
    o_ref[...] = out + refs[n + 2][...] if acc else out


def solve(me, pieces, mh, ml, rows, parts, acc=None):
    q = mh.shape[0]
    const = lambda shape: pl.BlockSpec(shape, lambda i, me: (0,) * len(shape), pipeline_mode=pl.Buffered(1))
    each = rows * parts
    specs, args, sizes = [], [], []
    for array, runs, paired in pieces:
        sizes.append(runs)
        args.append(array)
        if paired:
            specs.append(pl.BlockSpec((None, runs * each, LANES), lambda i, me: (me[0] % 2, 0, 0), pipeline_mode=pl.Buffered(1)))
        else:
            specs.append(const((runs * each, LANES)))
    tile = pl.BlockSpec((q, parts * LANES), lambda i, me: (0, i))
    specs += [const(mh.shape), const(ml.shape)]
    args += [mh, ml]
    if acc is not None:
        specs.append(tile)
        args.append(acc)
    return pl.pallas_call(
        functools.partial(solve_kernel, rows=rows, parts=parts, sizes=tuple(sizes), acc=acc is not None),
        grid_spec=pltpu.PrefetchScalarGridSpec(
            num_scalar_prefetch=1, grid=(rows,), in_specs=specs, out_specs=tile),
        out_shape=jax.ShapeDtypeStruct((q, each * LANES), jnp.float32),
        input_output_aliases={} if acc is None else {len(args): 0},
        name="solve",
    )(me, *args)


def precise_dot(a, b):
    return jnp.dot(a, b, precision=lax.Precision.HIGHEST, preferred_element_type=jnp.float32)


def split_outside(x):
    hi = lax.reduce_precision(x, 8, 7)
    return hi.astype(jnp.bfloat16), (x - hi).astype(jnp.bfloat16)


def mixing(block_inverses, panels, total):
    width = block_inverses.shape[1]
    first, second = block_inverses[0], block_inverses[1]
    below = -precise_dot(second, precise_dot(panels[0, width : 2 * width], first))
    top = jnp.concatenate([first, jnp.zeros_like(first)], axis=1)
    rows = [top, jnp.concatenate([below, second], axis=1)]
    if total > 2 * width:
        left, right = panels[0, 2 * width :], panels[1, 2 * width :]
        rows.append(
            -jnp.concatenate(
                [precise_dot(left, first) + precise_dot(right, below), precise_dot(right, second)],
                axis=1,
            )
        )
    return jnp.concatenate(rows, axis=0)


HEAD = 4
LATE = 3


def exchange(x, offset):
    pairs = [(i, i ^ offset) for i in range(lax.axis_size("dev"))]
    return lax.ppermute(x, "dev", pairs)


def whole_order(me, head, got, early, late, load, final, ways, mix, rows, parts, front):
    groups, _ = head.shape[:2]
    each = rows * parts
    rest = final.shape[0] // (len(late) * each)
    core = me[0] % 2

    def mine(k):
        return lax.dynamic_slice_in_dim(got[k], core, 1, 0)[0, : rest * each]

    tail = [mine(k) for k in early] + [load[: len(early) * rest * each]] + [mine(k) for k in late] + [final]
    tail = jnp.concatenate(tail, axis=0).reshape(groups, rest, parts, rows, LANES)
    spot = jnp.asarray(np.argsort(ways).astype(np.int32))
    tail = jnp.take(tail, spot[jnp.arange(groups) ^ me[0]], axis=0)
    runs = jnp.concatenate([head, tail], axis=1).reshape(-1, parts, rows, LANES)
    out = solve(me, [(runs[:front].reshape(-1, LANES), front, False)], *split_outside(mix), rows, parts)
    below = jnp.moveaxis(runs[front:], 1, 2).reshape(out.shape[0] - front, -1)
    return jnp.concatenate([out[:front], out[front:] + below], axis=0)


def per_device(runs_field, spectral_filter, block_inverses, factor_panels):
    groups = lax.axis_size("dev")
    place = lax.axis_index("dev")
    local, length, _ = runs_field.shape
    total = local * groups
    width = block_inverses.shape[1]
    rows, parts = length // groups, length // LANES
    each = rows * parts
    chips, top = groups // 2, groups // 2
    rest = local - HEAD
    core = place % 2
    me = place.astype(jnp.int32).reshape(1)
    needed = 1 if total == 2 * width else 2

    def other(x):
        return lax.dynamic_slice_in_dim(x, 1 - core, 1, 0)

    mine = factor_panels[:needed]
    held = jnp.stack([mine, exchange(mine, top)])
    (head,) = whiten(me, runs_field, spectral_filter, groups, 0, HEAD, HEAD, False)
    head = lax.all_to_all(head, "dev", 0, 0, tiled=True)
    outs = whiten(me, runs_field, spectral_filter, groups, HEAD, rest, HEAD, True)
    outs = [o.reshape(2, rest * each, LANES) for o in outs]
    carried = held.reshape(2, -1, LANES)
    got = {0: outs[0]}
    papers = {0: carried}
    near = list(range(1, chips // 2))
    far = list(range(chips // 2, chips))
    for k in far:
        got[k] = exchange(outs[k], 2 * k)
    for k in near:
        got[k] = exchange(jnp.concatenate([outs[k], carried], axis=1), 2 * k)
        papers[k] = got[k][:, rest * each:]
    early = [0] + near + far[:-LATE]
    late = far[-LATE:]
    book = jnp.concatenate([papers[k].reshape(1, -1, LANES) for k in [0] + near], axis=1)
    load = jnp.concatenate([other(got[k])[:, : rest * each] for k in early] + [book], axis=1)
    load = exchange(load[0], 1)
    first_count = len(early) * rest
    theirs = load[first_count * each :]
    pages = jnp.concatenate([book[0], theirs], axis=0)
    pages = pages.reshape(2, chips // 2, 2, needed, local, width)
    pages = jnp.transpose(pages, (2, 1, 0, 3, 4, 5)).reshape(groups, needed, local, width)
    ways = np.array([[h * top + 2 * k + c for k in [0] + near for c in range(2)] for h in range(2)]).reshape(-1)
    spot = np.argsort(ways).astype(np.int32)
    pages = jnp.take(pages, jnp.asarray(spot)[jnp.arange(groups) ^ place], axis=0)
    panels = jnp.moveaxis(pages, 0, 1).reshape(needed, total, width)
    mix = mixing(block_inverses, panels, total)
    ways = [2 * k for k in early] + [2 * k + 1 for k in early] + [2 * k for k in late] + [2 * k + 1 for k in late]
    cut = 2 * first_count

    if total == 2 * width:
        table = mix.T.reshape(groups, local, total)
        tail = jnp.take(table[:, HEAD:], jnp.asarray(np.array(ways, np.int32)) ^ place, axis=0)
        tail = tail.reshape(-1, total)
        soon = split_outside(jnp.concatenate([table[:, :HEAD].reshape(-1, total), tail[:cut]], axis=0).T)
        last = split_outside(tail[cut:].T)
    final = exchange(jnp.concatenate([other(got[k])[0] for k in late], axis=0), 1)
    if total > 2 * width:
        return whole_order(me, head, got, early, late, load, final, ways, mix, rows, parts, 2 * width)
    pieces = [(head.reshape(-1, LANES), groups * HEAD, False)]
    pieces += [(got[k], rest, True) for k in early]
    pieces.append((load, first_count, False))
    out = solve(me, pieces, *soon, rows, parts)
    pieces = [(got[k], rest, True) for k in late] + [(final, len(late) * rest, False)]
    out = solve(me, pieces, *last, rows, parts, out)
    return out


def solution(mesh):
    return jax.shard_map(
        per_device,
        mesh=mesh,
        in_specs=(P("dev", None, None), P(), P(), P(None, "dev", None)),
        out_specs=P(None, "dev"),
        check_vma=False,
    )
```

time: 142 us -> 163 us (1.15)
  waiting for transfers between devices: 102 us -> 48.2 us
  local copies, waits for them, and re-layouts: 1.57 us -> 32.4 us
  starting transfers between devices: 13.1 us -> 40.8 us
  Pallas kernels: 23.1 us -> 34.5 us
  other arithmetic: 1.15 us -> 5.39 us
    ppermute x5 -> x18, waiting for transfers between devices: 102 us -> 48.2 us  [exchange(): return lax.ppermute(x, 'dev', pairs)]
    ppermute x5 -> x18, starting transfers between devices: 5.62 us -> 36.9 us  [exchange(): return lax.ppermute(x, 'dev', pairs)]
    unnamed x10 -> x67, local copies, waits for them, and re-layouts: 0.03 us -> 17.5 us
    pallas_call x2 -> x4, Pallas kernels: 23.1 us -> 34.5 us  [the longest x2 17.5 us: solve(): pl.pallas_call(functools.partial(solve_kernel, rows=rows, parts=parts, si...]
    reshape x0 -> x4, local copies, waits for them, and re-layouts: none -> 4.06 us  [the longest x2 3.84 us: per_device(): pages = pages.reshape(2, chips // 2, 2, needed, local, width)]
    all_to_all x1, starting transfers between devices: 7.46 us -> 3.83 us  [per_device(): head = lax.all_to_all(head, 'dev', 0, 0, tiled=True)]
    slice x0 -> x17, local copies, waits for them, and re-layouts: none -> 3.52 us  [the longest x3 2.33 us: per_device(): tail[:cut]]
    concatenate x3 -> x4, other arithmetic: 0.02 us -> 3.33 us  [the longest x1 1.56 us: per_device(): got[k] = exchange(jnp.concatenate([outs[k], carried], axis=1), 2 * k)]
  transfers between devices with their start and end apart: 6 -> 19, of which waited for: 5 -> 9; matrix products, arithmetic and copies ran while one was open for 2% -> 22% of each run, Pallas kernels for 0% -> 16%
where the time goes in v1:
time: 163 us
  waiting for transfers between devices  48.2 us (30%)
  starting transfers between devices  40.8 us (25%)
  Pallas kernels  34.5 us (21%)
  local copies, waits for them, and re-layouts  32.4 us (20%)
  other arithmetic  5.39 us (3%)
    ppermute x18, waiting for transfers between devices, exchange(): return lax.ppermute(x, 'dev', pairs)  48.2 us
    ppermute x18, starting transfers between devices, exchange(): return lax.ppermute(x, 'dev', pairs)  36.9 us
    unnamed x67, local copies, waits for them, and re-layouts  17.5 us
    pallas_call x2, Pallas kernels, solve(): pl.pallas_call(functools.partial(solve_kernel, rows=rows, parts=parts, si...  17.5 us
    pallas_call x2, Pallas kernels, whiten(): pl.pallas_call(functools.partial(whiten_kernel, rb=rb, groups=groups, out...  17.1 us
    reshape x2, local copies, waits for them, and re-layouts, per_device(): pages = pages.reshape(2, chips // 2, 2, needed, local, width)  3.84 us
    all_to_all x1, starting transfers between devices, per_device(): head = lax.all_to_all(head, 'dev', 0, 0, tiled=True)  3.83 us
  transfers between devices with their start and end apart: 19, of which 9 were waited for; matrix products, arithmetic and copies ran while one was open for 22% of the time, Pallas kernels for 16%

profile of v1, /device:TPU:0, one launch (start us, length us, event | category | flops | bytes accessed | tf_op | source)
XLA Modules:
  0.0 162.7 jit_solution(12847174991928761618)
XLA Ops:
  0.7 4.1 %collective-permute-start.4 = (f32[1,16,256]{2,1,0:T(8,128)S(1)}, f32[1,16,256]{2,1,0:T(8,128)S(1)}, u32[]{:S(2)}, u32[]{:S(2)}) collective-permute-start(f32[1,16,256]{2,1,0:T(8,128)S(1)} %get-tuple-element.62), channel_id=1, source_target_pairs={{0,16},{1,17},{2,18},{3,19},{4,20},{5,21},{6,22},{7,23},{8,24},{9,... | collective-permute-start | bytes 49160 | tf_op jit(solution)/shard_map/ppermute | solution.py:213
  4.8 5.5 %whiten.3 = f32[32,4,2,8,128]{4,3,2,1,0:T(8,128)} custom-call(s32[1]{0:T(128)} %bitcast.me_ref, f32[16,256,256]{2,1,0:T(8,128)} %x_ref.3, f32[129,256]{1,0:T(8,128)} %bitcast.105, bf16[256,256]{1,0:T(8,128)(2,1)} %constant.64.clone.fh_ref, bf16[256,256]{1,0:T(8,128)(2,1)} %constant.65.clone.fl_ref, bf16[256,256]{1,0:T(8,128)(2,1)} %constant.66.clone.th_ref, ...), custom_call_target="tpu_custom_call" | custom-call | tf_op jit(solution)/shard_map/whiten/pallas_call | solution.py:123
  10.2 3.8 %all-to-all-start = ((f32[32,4,2,8,128]{4,3,2,1,0:T(8,128)}), f32[32,4,2,8,128]{4,3,2,1,0:T(8,128)S(1)}, u32[]{:S(2)}, u32[]{:S(2)}) async-start(f32[32,4,2,8,128]{4,3,2,1,0:T(8,128)} %whiten.3), calls=%async_computation | async-start | bytes 2097152 | tf_op jit(solution)/shard_map/all_to_all | solution.py:255
  14.1 11.6 %whiten.2 = (f32[2,12,2,8,128]{4,3,2,1,0:T(8,128)}, f32[2,12,2,8,128]{4,3,2,1,0:T(8,128)}, f32[2,12,2,8,128]{4,3,2,1,0:T(8,128)}, f32[2,12,2,8,128]{4,3,2,1,0:T(...) custom-call(s32[1]{0:T(128)} %bitcast.me_ref, ...), custom_call_target="tpu_custom_call" | custom-call | tf_op jit(solution)/shard_map/whiten/pallas_call | solution.py:123
  25.7 4.6 %collective-permute-start.1 = (f32[2,192,128]{2,1,0:T(8,128)}, f32[2,192,128]{2,1,0:T(8,128)}, u32[]{:S(2)}, u32[]{:S(2)}) collective-permute-start(f32[2,192,128]{2,1,0:T(8,128)} %bitcast.128), channel_id=1, source_target_pairs={{0,28},{1,29},{2,30},{3,31},{4,24},{5,25},{6,26},{7,27},{8,20},{9,... | collective-permute-start | bytes 589832 | tf_op jit(solution)/shard_map/ppermute | solution.py:213
  30.3 1.4 collective-permute-start
  31.7 1.6 pad_maximum_fusion
  34.8 2.7 %collective-permute-start.7 = (f32[2,224,128]{2,1,0:T(8,128)S(1)}, f32[2,224,128]{2,1,0:T(8,128)S(1)}, u32[]{:S(2)}, u32[]{:S(2)}) collective-permute-start(f32[2,224,128]{2,1,0:T(8,128)S(1)} %get-tuple-element.65), channel_id=1, source_target_pairs={{0,6},{1,7},{2,4},{3,5},{4,2},{5,3},{6,0},{7,1},{8,14},{9,15},{10,... | collective-permute-start | bytes 688136 | tf_op jit(solution)/shard_map/ppermute | solution.py:213
  37.5 9.5 %collective-permute-done.5.refs_2_ = f32[2,224,128]{2,1,0:T(8,128)S(1)} collective-permute-done((f32[2,224,128]{2,1,0:T(8,128)S(1)}, f32[2,224,128]{2,1,0:T(8,128)S(1)}, u32[]{:S(2)}, u32[]{:S(2)}) %collective-permute-start.5) | collective-permute-done | bytes 229408 | tf_op jit(solution)/shard_map/ppermute | solution.py:213
  47.8 3.9 %collective-permute-done.6.refs_3_ = f32[2,224,128]{2,1,0:T(8,128)S(1)} collective-permute-done((f32[2,224,128]{2,1,0:T(8,128)S(1)}, f32[2,224,128]{2,1,0:T(8,128)S(1)}, u32[]{:S(2)}, u32[]{:S(2)}) %collective-permute-start.6) | collective-permute-done | bytes 229408 | tf_op jit(solution)/shard_map/ppermute | solution.py:213
  52.3 2.7 %collective-permute-start.10 = (f32[2,224,128]{2,1,0:T(8,128)S(1)}, f32[2,224,128]{2,1,0:T(8,128)S(1)}, u32[]{:S(2)}, u32[]{:S(2)}) collective-permute-start(f32[2,224,128]{2,1,0:T(8,128)S(1)} %get-tuple-element.68), channel_id=1, source_target_pairs={{0,12},{1,13},{2,14},{3,15},{4,8},{5,9},{6,10},{7,11},{8,4},{9,5},... | collective-permute-start | bytes 688136 | tf_op jit(solution)/shard_map/ppermute | solution.py:213
  57.1 3.9 %collective-permute-done.9.refs_6_ = f32[2,224,128]{2,1,0:T(8,128)S(1)} collective-permute-done((f32[2,224,128]{2,1,0:T(8,128)S(1)}, f32[2,224,128]{2,1,0:T(8,128)S(1)}, u32[]{:S(2)}, u32[]{:S(2)}) %collective-permute-start.9) | collective-permute-done | bytes 229408 | tf_op jit(solution)/shard_map/ppermute | solution.py:213
  61.0 3.2 %collective-permute-start.2 = (f32[2,192,128]{2,1,0:T(8,128)}, f32[2,192,128]{2,1,0:T(8,128)}, u32[]{:S(2)}, u32[]{:S(2)}) collective-permute-start(f32[2,192,128]{2,1,0:T(8,128)} %bitcast.126), channel_id=1, source_target_pairs={{0,30},{1,31},{2,28},{3,29},{4,26},{5,27},{6,24},{7,25},{8,22},{9,... | collective-permute-start | bytes 589832 | tf_op jit(solution)/shard_map/ppermute | solution.py:213
  64.9 3.3 %collective-permute-done.10.refs_7_ = f32[2,224,128]{2,1,0:T(8,128)S(1)} collective-permute-done((f32[2,224,128]{2,1,0:T(8,128)S(1)}, f32[2,224,128]{2,1,0:T(8,128)S(1)}, u32[]{:S(2)}, u32[]{:S(2)}) %collective-permute-start.10) | collective-permute-done | bytes 229408 | tf_op jit(solution)/shard_map/ppermute | solution.py:213
  68.9 4.2 %collective-permute-done.11.refs_8_ = f32[2,224,128]{2,1,0:T(8,128)S(1)} collective-permute-done((f32[2,224,128]{2,1,0:T(8,128)S(1)}, f32[2,224,128]{2,1,0:T(8,128)S(1)}, u32[]{:S(2)}, u32[]{:S(2)}) %collective-permute-start.11) | collective-permute-done | bytes 229408 | tf_op jit(solution)/shard_map/ppermute | solution.py:213
  73.9 10.3 %collective-permute-done.12.refs_9_ = f32[2,192,128]{2,1,0:T(8,128)S(1)} collective-permute-done((f32[2,192,128]{2,1,0:T(8,128)}, f32[2,192,128]{2,1,0:T(8,128)S(1)}, u32[]{:S(2)}, u32[]{:S(2)}) %collective-permute-start.12) | collective-permute-done | bytes 196640 | tf_op jit(solution)/shard_map/ppermute | solution.py:213
  84.2 9.7 %collective-permute-start.14 = (f32[2,192,128]{2,1,0:T(8,128)}, f32[2,192,128]{2,1,0:T(8,128)S(1)}, u32[]{:S(2)}, u32[]{:S(2)}) collective-permute-start(f32[2,192,128]{2,1,0:T(8,128)} %bitcast.131), channel_id=1, source_target_pairs={{0,20},{1,21},{2,22},{3,23},{4,16},{5,17},{6,18},{7,19},{8,28},{9,... | collective-permute-start | bytes 589832 | tf_op jit(solution)/shard_map/ppermute | solution.py:213
  94.5 6.8 %collective-permute-start.15 = (f32[2,192,128]{2,1,0:T(8,128)S(1)}, f32[2,192,128]{2,1,0:T(8,128)S(1)}, u32[]{:S(2)}, u32[]{:S(2)}) collective-permute-start(f32[2,192,128]{2,1,0:T(8,128)S(1)} %bitcast.130), channel_id=1, source_target_pairs={{0,22},{1,23},{2,20},{3,21},{4,18},{5,19},{6,16},{7,17},{8,30},{9,... | collective-permute-start | bytes 589832 | tf_op jit(solution)/shard_map/ppermute | solution.py:213
  101.9 7.0 %collective-permute-done.14.refs_11_ = f32[2,192,128]{2,1,0:T(8,128)S(1)} collective-permute-done((f32[2,192,128]{2,1,0:T(8,128)}, f32[2,192,128]{2,1,0:T(8,128)S(1)}, u32[]{:S(2)}, u32[]{:S(2)}) %collective-permute-start.14) | collective-permute-done | bytes 196640 | tf_op jit(solution)/shard_map/ppermute | solution.py:213
  109.6 4.6 %collective-permute-done.15.refs_12_ = f32[2,192,128]{2,1,0:T(8,128)S(1)} collective-permute-done((f32[2,192,128]{2,1,0:T(8,128)S(1)}, f32[2,192,128]{2,1,0:T(8,128)S(1)}, u32[]{:S(2)}, u32[]{:S(2)}) %collective-permute-start.15) | collective-permute-done | bytes 196640 | tf_op jit(solution)/shard_map/ppermute | solution.py:213
  115.0 1.5 collective-permute-done.16.refs_13_
  124.5 1.1 copy.26
  125.6 1.8 %copy.25 = f32[1,256,256]{1,2,0:T(8,128)} copy(f32[1,256,256]{2,1,0:T(8,128)} %get-tuple-element.42) | data formatting | bytes 524288
  127.4 0.9 dynamic-slice_bitcast_fusion.1
  131.9 2.0 %reshape.192 = f32[2,8,2,1,16,256]{5,4,2,1,0,3:T(8,128)} reshape(f32[1024,128]{1,0:T(8,128)} %pad_maximum_fusion.7) | data formatting | bytes 1048576 | tf_op jit(solution)/shard_map/reshape | solution.py:276
  133.9 1.9 %copy.20 = f32[2,8,2,1,16,256]{5,4,0,1,2,3:T(8,128)} copy(f32[2,8,2,1,16,256]{5,4,2,1,0,3:T(8,128)} %reshape.192) | data formatting | bytes 1048576 | tf_op jit(solution)/shard_map/reshape | solution.py:276
  135.7 1.7 %gather_fusion.1 = f32[32,16,256]{2,1,0:T(8,128)S(1)} fusion(f32[32,16,256]{2,1,0:T(8,128)} %bitcast.101, s32[1024]{0:T(1024)S(1)} %get-tuple-element.71), kind=kCustom, calls=%fused_computation.1 | custom fusion | bytes 1048704 | tf_op jit(solution)/shard_map/jit(_take)/gather | solution.py:280
  140.8 1.3 copy.24
  142.1 1.1 fusion.1
  144.2 1.0 copy-done
  145.2 9.5 %solve.2.refs_6_ = f32[512,2048]{1,0:T(8,128)} custom-call(s32[1]{0:T(128)} %bitcast.me_ref, f32[2048,128]{1,0:T(8,128)} %bitcast.100, f32[2,192,128]{2,1,0:T(8,128)} %bitcast.107, f32[2,224,128]{2,1,0:T(8,128)} %copy-done.4, f32[2,224,128]{2,1,0:T(8,128)} %copy-done.5, f32[2,224,128]{2,1,0:T(8,128)} %copy-done.6, f32[2,224,128]{2,1,0:T(8,128)} %copy-done.7, ...), custom_call_target="tpu_custom_call" | custom-call | tf_op jit(solution)/shard_map/solve/pallas_call | solution.py:171
  154.7 8.0 %solve.3 = f32[512,2048]{1,0:T(8,128)} custom-call(s32[1]{0:T(128)} %bitcast.me_ref, f32[2,192,128]{2,1,0:T(8,128)} %collective-permute-done.refs_0_, f32[2,192,128]{2,1,0:T(8,128)} %collective-permute-done.1.refs_1_, f32[2,192,128]{2,1,0:T(8,128)} %collective-permute-done.2.refs_2_, ...), custom_call_target="tpu_custom_call", output_to_operand_aliasing={{}: (7, {})} | custom-call | tf_op jit(solution)/shard_map/solve/pallas_call | solution.py:171
  (130 shorter events, 26.4 us)
Async XLA Ops:
  0.7 31.0 %collective-permute-start.4 = (f32[1,16,256]{2,1,0:T(8,128)S(1)}, f32[1,16,256]{2,1,0:T(8,128)S(1)}, u32[]{:S(2)}, u32[]{:S(2)}) collective-permute-start(f32[1,16,256]{2,1,0:T(8,128)S(1)} %get-tuple-element.62), channel_id=1, source_target_pairs={{0,16},{1,17},{2,18},{3,19},{4,20},{5,21},{6,22},{7,23},{8,24},{9,... | collective-permute-start | bytes 49160 | tf_op jit(solution)/shard_map/ppermute | solution.py:213
  10.2 133.9 %all-to-all-start = ((f32[32,4,2,8,128]{4,3,2,1,0:T(8,128)}), f32[32,4,2,8,128]{4,3,2,1,0:T(8,128)S(1)}, u32[]{:S(2)}, u32[]{:S(2)}) async-start(f32[32,4,2,8,128]{4,3,2,1,0:T(8,128)} %whiten.3), calls=%async_computation | async-start | bytes 2097152 | tf_op jit(solution)/shard_map/all_to_all | solution.py:255
  25.7 101.7 %collective-permute-start.1 = (f32[2,192,128]{2,1,0:T(8,128)}, f32[2,192,128]{2,1,0:T(8,128)}, u32[]{:S(2)}, u32[]{:S(2)}) collective-permute-start(f32[2,192,128]{2,1,0:T(8,128)} %bitcast.128), channel_id=1, source_target_pairs={{0,28},{1,29},{2,30},{3,31},{4,24},{5,25},{6,26},{7,27},{8,20},{9,... | collective-permute-start | bytes 589832 | tf_op jit(solution)/shard_map/ppermute | solution.py:213
  30.3 98.1 %collective-permute-start = (f32[2,192,128]{2,1,0:T(8,128)}, f32[2,192,128]{2,1,0:T(8,128)}, u32[]{:S(2)}, u32[]{:S(2)}) collective-permute-start(f32[2,192,128]{2,1,0:T(8,128)} %bitcast.127), channel_id=1, source_target_pairs={{0,26},{1,27},{2,24},{3,25},{4,30},{5,31},{6,28},{7,29},{8,18},{9,... | collective-permute-start | bytes 589832 | tf_op jit(solution)/shard_map/ppermute | solution.py:213
  33.3 13.8 %collective-permute-start.5 = (f32[2,224,128]{2,1,0:T(8,128)S(1)}, f32[2,224,128]{2,1,0:T(8,128)S(1)}, u32[]{:S(2)}, u32[]{:S(2)}) collective-permute-start(f32[2,224,128]{2,1,0:T(8,128)S(1)} %get-tuple-element.69), channel_id=1, source_target_pairs={{0,2},{1,3},{2,0},{3,1},{4,6},{5,7},{6,4},{7,5},{8,10},{9,11},{10,... | collective-permute-start | bytes 688136 | tf_op jit(solution)/shard_map/ppermute | solution.py:213
  34.6 17.1 %collective-permute-start.6 = (f32[2,224,128]{2,1,0:T(8,128)S(1)}, f32[2,224,128]{2,1,0:T(8,128)S(1)}, u32[]{:S(2)}, u32[]{:S(2)}) collective-permute-start(f32[2,224,128]{2,1,0:T(8,128)S(1)} %get-tuple-element.64), channel_id=1, source_target_pairs={{0,4},{1,5},{2,6},{3,7},{4,0},{5,1},{6,2},{7,3},{8,12},{9,13},{10,... | collective-permute-start | bytes 688136 | tf_op jit(solution)/shard_map/ppermute | solution.py:213
  34.8 17.5 %collective-permute-start.7 = (f32[2,224,128]{2,1,0:T(8,128)S(1)}, f32[2,224,128]{2,1,0:T(8,128)S(1)}, u32[]{:S(2)}, u32[]{:S(2)}) collective-permute-start(f32[2,224,128]{2,1,0:T(8,128)S(1)} %get-tuple-element.65), channel_id=1, source_target_pairs={{0,6},{1,7},{2,4},{3,5},{4,2},{5,3},{6,0},{7,1},{8,14},{9,15},{10,... | collective-permute-start | bytes 688136 | tf_op jit(solution)/shard_map/ppermute | solution.py:213
  37.5 57.0 %copy-start.21 = (f32[2,12,2,8,128]{4,3,2,1,0:T(8,128)S(1)}, f32[2,12,2,8,128]{4,3,2,1,0:T(8,128)}, u32[]{:S(2)}) copy-start(f32[2,12,2,8,128]{4,3,2,1,0:T(8,128)} %get-tuple-element.35) | copy-start | bytes 589828
  37.5 71.4 %copy-start.20 = (f32[2,12,2,8,128]{4,3,2,1,0:T(8,128)S(1)}, f32[2,12,2,8,128]{4,3,2,1,0:T(8,128)}, u32[]{:S(2)}) copy-start(f32[2,12,2,8,128]{4,3,2,1,0:T(8,128)} %get-tuple-element.36) | copy-start | bytes 589828
  47.1 73.2 %copy-start.4 = (f32[2,224,128]{2,1,0:T(8,128)}, f32[2,224,128]{2,1,0:T(8,128)S(1)}, u32[]{:S(2)}) copy-start(f32[2,224,128]{2,1,0:T(8,128)S(1)} %collective-permute-done.5.refs_2_) | copy-start | bytes 688132
  47.1 8.6 %collective-permute-start.8 = (f32[2,224,128]{2,1,0:T(8,128)S(1)}, f32[2,224,128]{2,1,0:T(8,128)S(1)}, u32[]{:S(2)}, u32[]{:S(2)}) collective-permute-start(f32[2,224,128]{2,1,0:T(8,128)S(1)} %get-tuple-element.66), channel_id=1, source_target_pairs={{0,8},{1,9},{2,10},{3,11},{4,12},{5,13},{6,14},{7,15},{8,0},{9,1},... | collective-permute-start | bytes 688136 | tf_op jit(solution)/shard_map/ppermute | solution.py:213
  51.6 69.2 %copy-start.5 = (f32[2,224,128]{2,1,0:T(8,128)}, f32[2,224,128]{2,1,0:T(8,128)S(1)}, u32[]{:S(2)}) copy-start(f32[2,224,128]{2,1,0:T(8,128)S(1)} %collective-permute-done.6.refs_3_) | copy-start | bytes 688132
  51.6 9.4 %collective-permute-start.9 = (f32[2,224,128]{2,1,0:T(8,128)S(1)}, f32[2,224,128]{2,1,0:T(8,128)S(1)}, u32[]{:S(2)}, u32[]{:S(2)}) collective-permute-start(f32[2,224,128]{2,1,0:T(8,128)S(1)} %get-tuple-element.67), channel_id=1, source_target_pairs={{0,10},{1,11},{2,8},{3,9},{4,14},{5,15},{6,12},{7,13},{8,2},{9,3},... | collective-permute-start | bytes 688136 | tf_op jit(solution)/shard_map/ppermute | solution.py:213
  52.3 69.1 %copy-start.6 = (f32[2,224,128]{2,1,0:T(8,128)}, f32[2,224,128]{2,1,0:T(8,128)S(1)}, u32[]{:S(2)}) copy-start(f32[2,224,128]{2,1,0:T(8,128)S(1)} %collective-permute-done.7.refs_4_) | copy-start | bytes 688132
  52.3 15.9 %collective-permute-start.10 = (f32[2,224,128]{2,1,0:T(8,128)S(1)}, f32[2,224,128]{2,1,0:T(8,128)S(1)}, u32[]{:S(2)}, u32[]{:S(2)}) collective-permute-start(f32[2,224,128]{2,1,0:T(8,128)S(1)} %get-tuple-element.68), channel_id=1, source_target_pairs={{0,12},{1,13},{2,14},{3,15},{4,8},{5,9},{6,10},{7,11},{8,4},{9,5},... | collective-permute-start | bytes 688136 | tf_op jit(solution)/shard_map/ppermute | solution.py:213
  55.7 66.4 %copy-start.7 = (f32[2,224,128]{2,1,0:T(8,128)}, f32[2,224,128]{2,1,0:T(8,128)S(1)}, u32[]{:S(2)}) copy-start(f32[2,224,128]{2,1,0:T(8,128)S(1)} %collective-permute-done.8.refs_5_) | copy-start | bytes 688132
  55.7 17.4 %collective-permute-start.11 = (f32[2,224,128]{2,1,0:T(8,128)S(1)}, f32[2,224,128]{2,1,0:T(8,128)S(1)}, u32[]{:S(2)}, u32[]{:S(2)}) collective-permute-start(f32[2,224,128]{2,1,0:T(8,128)S(1)} %get-tuple-element.63), channel_id=1, source_target_pairs={{0,14},{1,15},{2,12},{3,13},{4,10},{5,11},{6,8},{7,9},{8,6},{9,7},... | collective-permute-start | bytes 688136 | tf_op jit(solution)/shard_map/ppermute | solution.py:213
  61.0 61.1 %copy-start.8 = (f32[2,224,128]{2,1,0:T(8,128)}, f32[2,224,128]{2,1,0:T(8,128)S(1)}, u32[]{:S(2)}) copy-start(f32[2,224,128]{2,1,0:T(8,128)S(1)} %collective-permute-done.9.refs_6_) | copy-start | bytes 688132
  61.0 68.3 %collective-permute-start.2 = (f32[2,192,128]{2,1,0:T(8,128)}, f32[2,192,128]{2,1,0:T(8,128)}, u32[]{:S(2)}, u32[]{:S(2)}) collective-permute-start(f32[2,192,128]{2,1,0:T(8,128)} %bitcast.126), channel_id=1, source_target_pairs={{0,30},{1,31},{2,28},{3,29},{4,26},{5,27},{6,24},{7,25},{8,22},{9,... | collective-permute-start | bytes 589832 | tf_op jit(solution)/shard_map/ppermute | solution.py:213
  68.2 53.9 %copy-start.9 = (f32[2,224,128]{2,1,0:T(8,128)}, f32[2,224,128]{2,1,0:T(8,128)S(1)}, u32[]{:S(2)}) copy-start(f32[2,224,128]{2,1,0:T(8,128)S(1)} %collective-permute-done.10.refs_7_) | copy-start | bytes 688132
  68.2 16.0 %collective-permute-start.12 = (f32[2,192,128]{2,1,0:T(8,128)}, f32[2,192,128]{2,1,0:T(8,128)S(1)}, u32[]{:S(2)}, u32[]{:S(2)}) collective-permute-start(f32[2,192,128]{2,1,0:T(8,128)} %bitcast.133), channel_id=1, source_target_pairs={{0,16},{1,17},{2,18},{3,19},{4,20},{5,21},{6,22},{7,23},{8,24},{9,... | collective-permute-start | bytes 589832 | tf_op jit(solution)/shard_map/ppermute | solution.py:213
  68.9 54.6 %copy-start.19 = (s32[32]{0:T(128)S(1)}, s32[32]{0:T(128)}, u32[]{:S(2)}) copy-start(s32[32]{0:T(128)} %constant.68.clone) | copy-start | bytes 388
  68.9 54.6 %copy-start.2 = (f32[2,256,256]{2,1,0:T(8,128)S(1)}, f32[2,256,256]{2,1,0:T(8,128)}, u32[]{:S(2)}) copy-start(f32[2,256,256]{2,1,0:T(8,128)} %param.16) | copy-start | bytes 1572868
  73.1 49.0 %copy-start.10 = (f32[2,224,128]{2,1,0:T(8,128)}, f32[2,224,128]{2,1,0:T(8,128)S(1)}, u32[]{:S(2)}) copy-start(f32[2,224,128]{2,1,0:T(8,128)S(1)} %collective-permute-done.11.refs_8_) | copy-start | bytes 688132
  73.1 21.4 %collective-permute-start.13 = (f32[2,192,128]{2,1,0:T(8,128)}, f32[2,192,128]{2,1,0:T(8,128)S(1)}, u32[]{:S(2)}, u32[]{:S(2)}) collective-permute-start(f32[2,192,128]{2,1,0:T(8,128)} %bitcast.132), channel_id=1, source_target_pairs={{0,18},{1,19},{2,16},{3,17},{4,22},{5,23},{6,20},{7,21},{8,26},{9,... | collective-permute-start | bytes 589832 | tf_op jit(solution)/shard_map/ppermute | solution.py:213
  84.2 38.0 %copy-start.12 = (f32[2,192,128]{2,1,0:T(8,128)}, f32[2,192,128]{2,1,0:T(8,128)S(1)}, u32[]{:S(2)}) copy-start(f32[2,192,128]{2,1,0:T(8,128)S(1)} %collective-permute-done.12.refs_9_) | copy-start | bytes 589828
  84.2 24.8 %collective-permute-start.14 = (f32[2,192,128]{2,1,0:T(8,128)}, f32[2,192,128]{2,1,0:T(8,128)S(1)}, u32[]{:S(2)}, u32[]{:S(2)}) collective-permute-start(f32[2,192,128]{2,1,0:T(8,128)} %bitcast.131), channel_id=1, source_target_pairs={{0,20},{1,21},{2,22},{3,23},{4,16},{5,17},{6,18},{7,19},{8,28},{9,... | collective-permute-start | bytes 589832 | tf_op jit(solution)/shard_map/ppermute | solution.py:213
  94.5 27.7 %copy-start.13 = (f32[2,192,128]{2,1,0:T(8,128)}, f32[2,192,128]{2,1,0:T(8,128)S(1)}, u32[]{:S(2)}) copy-start(f32[2,192,128]{2,1,0:T(8,128)S(1)} %collective-permute-done.13.refs_10_) | copy-start | bytes 589828
  94.5 19.8 %collective-permute-start.15 = (f32[2,192,128]{2,1,0:T(8,128)S(1)}, f32[2,192,128]{2,1,0:T(8,128)S(1)}, u32[]{:S(2)}, u32[]{:S(2)}) collective-permute-start(f32[2,192,128]{2,1,0:T(8,128)S(1)} %bitcast.130), channel_id=1, source_target_pairs={{0,22},{1,23},{2,20},{3,21},{4,18},{5,19},{6,16},{7,17},{8,30},{9,... | collective-permute-start | bytes 589832 | tf_op jit(solution)/shard_map/ppermute | solution.py:213
  108.9 7.5 %collective-permute-start.16 = (f32[2,192,128]{2,1,0:T(8,128)S(1)}, f32[2,192,128]{2,1,0:T(8,128)S(1)}, u32[]{:S(2)}, u32[]{:S(2)}) collective-permute-start(f32[2,192,128]{2,1,0:T(8,128)S(1)} %bitcast.129), channel_id=1, source_target_pairs={{0,24},{1,25},{2,26},{3,27},{4,28},{5,29},{6,30},{7,31},{8,16},{9,... | collective-permute-start | bytes 589832 | tf_op jit(solution)/shard_map/ppermute | solution.py:213
  122.1 8.8 %collective-permute-start.17 = (f32[3008,128]{1,0:T(8,128)}, f32[3008,128]{1,0:T(8,128)S(1)}, u32[]{:S(2)}, u32[]{:S(2)}) collective-permute-start(f32[3008,128]{1,0:T(8,128)} %bitcast.125), channel_id=1, source_target_pairs={{0,1},{1,0},{2,3},{3,2},{4,5},{5,4},{6,7},{7,6},{8,9},{9,8},{10,11... | collective-permute-start | bytes 4620296 | tf_op jit(solution)/shard_map/ppermute | solution.py:213
  130.9 23.7 %collective-permute-start.3 = (f32[576,128]{1,0:T(8,128)}, f32[576,128]{1,0:T(8,128)}, u32[]{:S(2)}, u32[]{:S(2)}) collective-permute-start(f32[576,128]{1,0:T(8,128)} %pad_maximum_fusion.8), channel_id=1, source_target_pairs={{0,1},{1,0},{2,3},{3,2},{4,5},{5,4},{6,7},{7,6},{8,9},{9,8},{10,11... | collective-permute-start | bytes 884744 | tf_op jit(solution)/shard_map/ppermute | solution.py:213
  (9 other events, 41.9 us)

commit v2 on v1

--- a/solution.py
+++ b/solution.py
@@ -135,45 +135,151 @@
     )(me, x, spectral_filter.T, fh, fl, fh.T, fl.T)
 
 
-def solve_kernel(me_ref, *refs, rows, parts, sizes, acc):
-    n = len(sizes)
-    w_refs, (mh_ref, ml_ref) = refs[:n], refs[n:n + 2]
-    o_ref = refs[-1]
+def plain_kernel(w_ref, mh_ref, ml_ref, o_ref, *, rows, parts):
+    k = mh_ref.shape[1]
     i = pl.program_id(0)
-    pieces = [
-        jnp.concatenate([w_ref[pl.ds(p * rows + i, k, stride=rows * parts), :] for p in range(parts)], axis=1)
-        for w_ref, k in zip(w_refs, sizes)
-    ]
-    wh, wl = split(jnp.concatenate(pieces, axis=0) if n > 1 else pieces[0])
-    mh, ml = mh_ref[...], ml_ref[...]
-    out = mm(mh, wh) + mm(mh, wl) + mm(ml, wh)
-    o_ref[...] = out + refs[n + 2][...] if acc else out
-
-
-def solve(me, pieces, mh, ml, rows, parts, acc=None):
+    w = jnp.concatenate([w_ref[pl.ds(p * rows + i, k, stride=rows * parts), :] for p in range(parts)], axis=1)
+    wh, wl = split(w)
+    o_ref[...] = mm(mh_ref[...], wh) + mm(mh_ref[...], wl) + mm(ml_ref[...], wh)
+
+
+def plain_solve(w, mh, ml, rows, parts):
     q = mh.shape[0]
-    const = lambda shape: pl.BlockSpec(shape, lambda i, me: (0,) * len(shape), pipeline_mode=pl.Buffered(1))
+    const = lambda a: pl.BlockSpec(a.shape, lambda i: (0,) * a.ndim, pipeline_mode=pl.Buffered(1))
+    return pl.pallas_call(
+        functools.partial(plain_kernel, rows=rows, parts=parts),
+        grid=(rows,),
+        in_specs=[const(w), const(mh), const(ml)],
+        out_specs=pl.BlockSpec((q, parts * LANES), lambda i: (0, i)),
+        out_shape=jax.ShapeDtypeStruct((q, rows * parts * LANES), jnp.float32),
+        name="plain",
+    )(w, mh, ml)
+
+
+def whole(shape):
+    return pl.BlockSpec(shape, lambda i, me: (0,) * len(shape), pipeline_mode=pl.Buffered(1))
+
+
+def here():
+    return pl.BlockSpec(memory_space=pltpu.VMEM)
+
+
+def bundle_kernel(me_ref, *refs):
+    size = refs[0].shape[1]
+    for j, ref in enumerate(refs[:-1]):
+        refs[-1][j * size:(j + 1) * size] = ref[1 - me_ref[0] % 2]
+
+
+def bundle(me, arrays):
+    size = arrays[0].shape[1]
+    shape = (len(arrays) * size, LANES)
+    return pl.pallas_call(
+        bundle_kernel,
+        grid_spec=pltpu.PrefetchScalarGridSpec(
+            num_scalar_prefetch=1, grid=(1,), in_specs=[here() for a in arrays], out_specs=here()),
+        out_shape=jax.ShapeDtypeStruct(shape, jnp.float32),
+        name="bundle",
+    )(me, *arrays)
+
+
+def mix_kernel(me_ref, spot_ref, mask_ref, inverse_ref, *refs, top, local):
+    papers, theirs_ref = refs[:-6], refs[-6]
+    th_ref, tl_ref, bh_ref, bl_ref, panel_ref = refs[-5:]
+    me = me_ref[0]
+    for k, ref in enumerate(papers):
+        for c in range(2):
+            at = pl.multiple_of(((me ^ (2 * k + c)) & (top - 1)) * local, local)
+            panel_ref[pl.ds(at, local), :] = theirs_ref[k * local:(k + 1) * local] if c else ref[...]
+    exact = functools.partial(jnp.dot, precision=lax.Precision.HIGHEST, preferred_element_type=jnp.float32)
+    first, second = inverse_ref[0], inverse_ref[1]
+    below = -exact(second, exact(panel_ref[...], first))
+    width = first.shape[0]
+    table = jnp.concatenate([
+        jnp.concatenate([first, jnp.zeros_like(first)], axis=1),
+        jnp.concatenate([below, second], axis=1)], axis=0)
+    run = spot_ref[...] ^ ((me * local) & mask_ref[...])
+    order = lax.broadcasted_iota(jnp.int32, table.shape, 0) == jnp.broadcast_to(run, table.shape)
+    order = order.astype(jnp.float32).astype(jnp.bfloat16)
+    left = me < top
+    for piece, t_ref, b_ref in zip(split(table), (th_ref, tl_ref), (bh_ref, bl_ref)):
+        moved = mm(piece, order)
+        b_ref[...] = moved[width:].astype(jnp.bfloat16)
+        t_ref[...] = jnp.where(left, moved[:width, :width], moved[:width, width:]).astype(jnp.bfloat16)
+
+
+def mix(me, spots, masks, inverses, papers, theirs, top, local):
+    width = inverses.shape[1]
+    shapes = [(width, width)] * 2 + [(width, 2 * width)] * 2
+    args = [spots, masks, inverses, *papers, theirs]
+    return pl.pallas_call(
+        functools.partial(mix_kernel, top=top, local=local),
+        grid_spec=pltpu.PrefetchScalarGridSpec(
+            num_scalar_prefetch=1, grid=(1,),
+            in_specs=[whole(spots.shape), whole(masks.shape), whole(inverses.shape)] + [here()] * (len(papers) + 1),
+            out_specs=[here()] * len(shapes),
+            scratch_shapes=[pltpu.VMEM((width, width), jnp.float32)]),
+        out_shape=[jax.ShapeDtypeStruct(shape, jnp.bfloat16) for shape in shapes],
+        name="mix",
+    )(me, *args)
+
+
+def solve_kernel(me_ref, *refs, rows, parts, per, near, far, top):
+    count = len(refs) - 6
+    w_refs = refs[:count]
+    th_ref, tl_ref, bh_ref, bl_ref, o_ref, held_ref = refs[count:]
+    stride = rows * parts
+    width = th_ref.shape[0]
+    left = me_ref[0] // top
+    for block, picks in enumerate((near, far)):
+        columns = []
+        for g in range(per):
+            i = pl.program_id(0) * per + g
+            for p in range(parts):
+                at = p * rows + i
+                column = []
+                for n, start, size in picks:
+                    if start is None:
+                        start = (left ^ block) * (size * stride)
+                    ref = w_refs[n]
+                    if len(ref.shape) == 3:
+                        ref = ref.at[me_ref[0] % 2]
+                    column.append(ref[pl.ds(start + at, size, stride=stride), :])
+                columns.append(jnp.concatenate(column, axis=0))
+        high, low = split(jnp.concatenate(columns, axis=1))
+        held_ref[block, 0] = high
+        held_ref[block, 1] = low
+    th, tl = th_ref[...], tl_ref[...]
+    o_ref[:width] = mm(th, held_ref[left, 0]) + mm(th, held_ref[left, 1]) + mm(tl, held_ref[left, 0])
+    out = None
+    for block in range(2):
+        bh = bh_ref[:, block * width:(block + 1) * width]
+        bl = bl_ref[:, block * width:(block + 1) * width]
+        part = mm(bh, held_ref[block, 0]) + mm(bh, held_ref[block, 1]) + mm(bl, held_ref[block, 0])
+        out = part if out is None else out + part
+    o_ref[width:] = out
+
+
+def solve(me, head, got, load, final, late, rest, tables, rows, parts, top):
+    chips = len(got)
     each = rows * parts
-    specs, args, sizes = [], [], []
-    for array, runs, paired in pieces:
-        sizes.append(runs)
-        args.append(array)
-        if paired:
-            specs.append(pl.BlockSpec((None, runs * each, LANES), lambda i, me: (me[0] % 2, 0, 0), pipeline_mode=pl.Buffered(1)))
-        else:
-            specs.append(const((runs * each, LANES)))
-    tile = pl.BlockSpec((q, parts * LANES), lambda i, me: (0, i))
-    specs += [const(mh.shape), const(ml.shape)]
-    args += [mh, ml]
-    if acc is not None:
-        specs.append(tile)
-        args.append(acc)
-    return pl.pallas_call(
-        functools.partial(solve_kernel, rows=rows, parts=parts, sizes=tuple(sizes), acc=acc is not None),
+    early = chips - late
+    per = 2 if rows % 2 == 0 else 1
+    args = [head, *got, load, final, *tables]
+    half_rows = head.shape[0] // each // 2
+    pair = lambda n, start, size: (n, start * each, size)
+    near = [(0, None, half_rows)] + [pair(1 + k, 0, rest) for k in range(chips // 2)]
+    near += [pair(1 + chips, 0, chips // 2 * rest)]
+    far = [(0, None, half_rows)] + [pair(1 + k, 0, rest) for k in range(chips // 2, chips)]
+    far += [pair(1 + chips, chips // 2 * rest, (early - chips // 2) * rest), pair(2 + chips, 0, late * rest)]
+    specs = [here()] * len(args)
+    width = tables[0].shape[0]
+    return pl.pallas_call(
+        functools.partial(solve_kernel, rows=rows, parts=parts, per=per, near=tuple(near), far=tuple(far), top=top),
         grid_spec=pltpu.PrefetchScalarGridSpec(
-            num_scalar_prefetch=1, grid=(rows,), in_specs=specs, out_specs=tile),
-        out_shape=jax.ShapeDtypeStruct((q, each * LANES), jnp.float32),
-        input_output_aliases={} if acc is None else {len(args): 0},
+            num_scalar_prefetch=1, grid=(rows // per,), in_specs=specs,
+            out_specs=pl.BlockSpec((2 * width, per * parts * LANES), lambda i, me: (0, i)),
+            scratch_shapes=[pltpu.VMEM((2, 2, width, per * parts * LANES), jnp.bfloat16)]),
+        out_shape=jax.ShapeDtypeStruct((2 * width, each * LANES), jnp.float32),
         name="solve",
     )(me, *args)
 
@@ -213,92 +319,74 @@
     return lax.ppermute(x, "dev", pairs)
 
 
-def whole_order(me, head, got, early, late, load, final, ways, mix, rows, parts, front):
-    groups, _ = head.shape[:2]
-    each = rows * parts
-    rest = final.shape[0] // (len(late) * each)
-    core = me[0] % 2
-
-    def mine(k):
-        return lax.dynamic_slice_in_dim(got[k], core, 1, 0)[0, : rest * each]
-
-    tail = [mine(k) for k in early] + [load[: len(early) * rest * each]] + [mine(k) for k in late] + [final]
-    tail = jnp.concatenate(tail, axis=0).reshape(groups, rest, parts, rows, LANES)
-    spot = jnp.asarray(np.argsort(ways).astype(np.int32))
-    tail = jnp.take(tail, spot[jnp.arange(groups) ^ me[0]], axis=0)
-    runs = jnp.concatenate([head, tail], axis=1).reshape(-1, parts, rows, LANES)
-    out = solve(me, [(runs[:front].reshape(-1, LANES), front, False)], *split_outside(mix), rows, parts)
-    below = jnp.moveaxis(runs[front:], 1, 2).reshape(out.shape[0] - front, -1)
-    return jnp.concatenate([out[:front], out[front:] + below], axis=0)
+def general(me, runs_field, spectral_filter, block_inverses, factor_panels):
+    groups = lax.axis_size("dev")
+    local, length, _ = runs_field.shape
+    total = local * groups
+    front = 2 * block_inverses.shape[1]
+    rows, parts = length // groups, length // LANES
+    (pieces,) = whiten(me, runs_field, spectral_filter, groups, 0, local, HEAD, False)
+    runs = lax.all_to_all(pieces, "dev", 0, 0, tiled=True).reshape(total, parts, rows, LANES)
+    panels = lax.all_gather(factor_panels, "dev", axis=1, tiled=True)
+    tables = split_outside(mixing(block_inverses, panels, total))
+    out = plain_solve(runs[:front].reshape(-1, LANES), *tables, rows, parts)
+    if total > front:
+        below = jnp.moveaxis(runs[front:], 1, 2).reshape(total - front, -1)
+        out = jnp.concatenate([out[:front], out[front:] + below], axis=0)
+    return out
+
+
+def places(groups, local, early, late):
+    top = groups // 2
+    rest = range(HEAD, local)
+    spots, masks = [], []
+    for far in range(2):
+        for source in range(top):
+            spots += [(source + far * top) * local + r for r in range(HEAD)]
+            masks += [top * local] * HEAD
+        mine = [k for k in early + late if (2 * k >= top) == bool(far)]
+        ways = [2 * k for k in mine]
+        ways += [2 * k + 1 for k in mine]
+        for way in ways:
+            spots += [way * local + r for r in rest]
+            masks += [-1] * len(rest)
+    return np.array([spots], np.int32), np.array([masks], np.int32)
 
 
 def per_device(runs_field, spectral_filter, block_inverses, factor_panels):
     groups = lax.axis_size("dev")
     place = lax.axis_index("dev")
     local, length, _ = runs_field.shape
-    total = local * groups
     width = block_inverses.shape[1]
     rows, parts = length // groups, length // LANES
-    each = rows * parts
     chips, top = groups // 2, groups // 2
+    me = place.astype(jnp.int32).reshape(1)
+    if local * groups != 2 * width:
+        return general(me, runs_field, spectral_filter, block_inverses, factor_panels)
     rest = local - HEAD
-    core = place % 2
-    me = place.astype(jnp.int32).reshape(1)
-    needed = 1 if total == 2 * width else 2
-
-    def other(x):
-        return lax.dynamic_slice_in_dim(x, 1 - core, 1, 0)
-
-    mine = factor_panels[:needed]
-    held = jnp.stack([mine, exchange(mine, top)])
+    near = list(range(1, chips // 2))
+    far = list(range(chips // 2, chips))
+    early, late = [0] + near + far[:-LATE], far[-LATE:]
+    mine = factor_panels[0]
+    mine = jnp.where(place < top, exchange(mine, top), mine)
     (head,) = whiten(me, runs_field, spectral_filter, groups, 0, HEAD, HEAD, False)
     head = lax.all_to_all(head, "dev", 0, 0, tiled=True)
     outs = whiten(me, runs_field, spectral_filter, groups, HEAD, rest, HEAD, True)
-    outs = [o.reshape(2, rest * each, LANES) for o in outs]
-    carried = held.reshape(2, -1, LANES)
-    got = {0: outs[0]}
-    papers = {0: carried}
-    near = list(range(1, chips // 2))
-    far = list(range(chips // 2, chips))
-    for k in far:
+    outs = [o.reshape(2, -1, LANES) for o in outs]
+    got = [outs[0]] + [None] * (chips - 1)
+    papers = [mine]
+    for k in near:
+        papers.append(exchange(mine, 2 * k))
+    for k in near + far:
         got[k] = exchange(outs[k], 2 * k)
-    for k in near:
-        got[k] = exchange(jnp.concatenate([outs[k], carried], axis=1), 2 * k)
-        papers[k] = got[k][:, rest * each:]
-    early = [0] + near + far[:-LATE]
-    late = far[-LATE:]
-    book = jnp.concatenate([papers[k].reshape(1, -1, LANES) for k in [0] + near], axis=1)
-    load = jnp.concatenate([other(got[k])[:, : rest * each] for k in early] + [book], axis=1)
-    load = exchange(load[0], 1)
-    first_count = len(early) * rest
-    theirs = load[first_count * each :]
-    pages = jnp.concatenate([book[0], theirs], axis=0)
-    pages = pages.reshape(2, chips // 2, 2, needed, local, width)
-    pages = jnp.transpose(pages, (2, 1, 0, 3, 4, 5)).reshape(groups, needed, local, width)
-    ways = np.array([[h * top + 2 * k + c for k in [0] + near for c in range(2)] for h in range(2)]).reshape(-1)
-    spot = np.argsort(ways).astype(np.int32)
-    pages = jnp.take(pages, jnp.asarray(spot)[jnp.arange(groups) ^ place], axis=0)
-    panels = jnp.moveaxis(pages, 0, 1).reshape(needed, total, width)
-    mix = mixing(block_inverses, panels, total)
-    ways = [2 * k for k in early] + [2 * k + 1 for k in early] + [2 * k for k in late] + [2 * k + 1 for k in late]
-    cut = 2 * first_count
-
-    if total == 2 * width:
-        table = mix.T.reshape(groups, local, total)
-        tail = jnp.take(table[:, HEAD:], jnp.asarray(np.array(ways, np.int32)) ^ place, axis=0)
-        tail = tail.reshape(-1, total)
-        soon = split_outside(jnp.concatenate([table[:, :HEAD].reshape(-1, total), tail[:cut]], axis=0).T)
-        last = split_outside(tail[cut:].T)
-    final = exchange(jnp.concatenate([other(got[k])[0] for k in late], axis=0), 1)
-    if total > 2 * width:
-        return whole_order(me, head, got, early, late, load, final, ways, mix, rows, parts, 2 * width)
-    pieces = [(head.reshape(-1, LANES), groups * HEAD, False)]
-    pieces += [(got[k], rest, True) for k in early]
-    pieces.append((load, first_count, False))
-    out = solve(me, pieces, *soon, rows, parts)
-    pieces = [(got[k], rest, True) for k in late] + [(final, len(late) * rest, False)]
-    out = solve(me, pieces, *last, rows, parts, out)
-    return out
+    theirs = exchange(jnp.concatenate(papers, axis=0), 1)
+    spots, masks = places(groups, local, early, late)
+    tables = mix(me, spots, masks, block_inverses, papers, theirs, top, local)
+    load = bundle(me, [got[k] for k in early])
+    load = exchange(load, 1)
+    final = bundle(me, [got[k] for k in late])
+    final = exchange(final, 1)
+    return solve(me, head.reshape(-1, LANES), got, load, final, LATE, rest, tables, rows, parts, top)
 
 
 def solution(mesh):

time: 163 us -> 153 us (0.939)
  local copies, waits for them, and re-layouts: 32.4 us -> 4.18 us
  starting transfers between devices: 40.8 us -> 55.4 us
  waiting for transfers between devices: 48.2 us -> 57.3 us
  other arithmetic: 5.39 us -> 0.01 us
    unnamed x67 -> x62, local copies, waits for them, and re-layouts: 17.5 us -> 4.18 us
    ppermute x18 -> x26, starting transfers between devices: 36.9 us -> 48.1 us  [exchange(): return lax.ppermute(x, 'dev', pairs)]
    ppermute x18 -> x26, waiting for transfers between devices: 48.2 us -> 57.3 us  [exchange(): return lax.ppermute(x, 'dev', pairs)]
    reshape x4 -> x0, local copies, waits for them, and re-layouts: 4.06 us -> none  [the longest x2 3.84 us: per_device(): pages = pages.reshape(2, chips // 2, 2, needed, local, width)]
    slice x18 -> x0, local copies, waits for them, and re-layouts: 3.53 us -> none  [the longest x3 2.33 us: per_device(): tail[:cut]]
    all_to_all x1, starting transfers between devices: 3.83 us -> 7.32 us  [per_device(): head = lax.all_to_all(head, 'dev', 0, 0, tiled=True)]
    concatenate x4 -> x0, other arithmetic: 3.33 us -> none  [the longest x1 1.56 us: per_device(): got[k] = exchange(jnp.concatenate([outs[k], carried], axis=1), 2 * k)]
    gather x3 -> x0, local copies, waits for them, and re-layouts: 2.98 us -> none  [the longest x1 1.66 us: per_device(): jnp.take(pages, jnp.asarray(spot)[jnp.arange(groups) ^ place], axis=0)]
  transfers between devices with their start and end apart: 19 -> 27, of which waited for: 9 -> 14; matrix products, arithmetic and copies ran while one was open for 22% -> 0% of each run, Pallas kernels for 16% -> 13%
where the time goes in v2:
time: 153 us
  waiting for transfers between devices  57.3 us (37%)
  starting transfers between devices  55.4 us (36%)
  Pallas kernels  35.3 us (23%)
  local copies, waits for them, and re-layouts  4.18 us (3%)
    ppermute x26, waiting for transfers between devices, exchange(): return lax.ppermute(x, 'dev', pairs)  57.3 us
    ppermute x26, starting transfers between devices, exchange(): return lax.ppermute(x, 'dev', pairs)  48.1 us
    pallas_call x2, Pallas kernels, whiten(): pl.pallas_call(functools.partial(whiten_kernel, rb=rb, groups=groups, out...  17.1 us
    pallas_call x1, Pallas kernels, solve(): pl.pallas_call(functools.partial(solve_kernel, rows=rows, parts=parts, pe...  9.86 us
    all_to_all x1, starting transfers between devices, per_device(): head = lax.all_to_all(head, 'dev', 0, 0, tiled=True)  7.32 us
    pallas_call x2, Pallas kernels, bundle(): pl.pallas_call(bundle_kernel, grid_spec=pltpu.PrefetchScalarGridSpec(num_...  4.74 us
    unnamed x62, local copies, waits for them, and re-layouts  4.18 us
    pallas_call x1, Pallas kernels, mix(): pl.pallas_call(functools.partial(mix_kernel, top=top, local=local), grid_...  3.66 us
  transfers between devices with their start and end apart: 27, of which 14 were waited for; matrix products, arithmetic and copies ran while one was open for 0% of the time, Pallas kernels for 13%

profile of v2, /device:TPU:0, one launch (start us, length us, event | category | flops | bytes accessed | tf_op | source)
XLA Modules:
  0.0 152.5 jit_solution(16811232512892644859)
XLA Ops:
  0.0 5.5 %whiten.2 = f32[32,4,2,8,128]{4,3,2,1,0:T(8,128)} custom-call(s32[1]{0:T(128)} %bitcast.me_ref, f32[16,256,256]{2,1,0:T(8,128)} %x_ref.3, f32[129,256]{1,0:T(8,128)} %bitcast.27, bf16[256,256]{1,0:T(8,128)(2,1)} %constant.18.clone.fh_ref, bf16[256,256]{1,0:T(8,128)(2,1)} %constant.19.clone.fl_ref, bf16[256,256]{1,0:T(8,128)(2,1)} %constant.20.clone.th_ref, ...), custom_call_target="tpu_custom_call" | custom-call | tf_op jit(solution)/shard_map/whiten/pallas_call | solution.py:123
  5.5 7.3 %all-to-all-start = ((f32[32,4,2,8,128]{4,3,2,1,0:T(8,128)}), f32[32,4,2,8,128]{4,3,2,1,0:T(8,128)S(1)}, u32[]{:S(2)}, u32[]{:S(2)}) async-start(f32[32,4,2,8,128]{4,3,2,1,0:T(8,128)} %whiten.2), calls=%async_computation | async-start | bytes 2097152 | tf_op jit(solution)/shard_map/all_to_all | solution.py:373
  12.8 11.6 %whiten.3 = (f32[2,12,2,8,128]{4,3,2,1,0:T(8,128)}, f32[2,12,2,8,128]{4,3,2,1,0:T(8,128)}, f32[2,12,2,8,128]{4,3,2,1,0:T(8,128)}, f32[2,12,2,8,128]{4,3,2,1,0:T(...) custom-call(s32[1]{0:T(128)} %bitcast.me_ref, ...), custom_call_target="tpu_custom_call" | custom-call | tf_op jit(solution)/shard_map/whiten/pallas_call | solution.py:123
  24.4 1.8 %collective-permute-start = (f32[2,192,128]{2,1,0:T(8,128)}, f32[2,192,128]{2,1,0:T(8,128)S(1)}, u32[]{:S(2)}, u32[]{:S(2)}) collective-permute-start(f32[2,192,128]{2,1,0:T(8,128)} %bitcast.43), channel_id=1, source_target_pairs={{0,2},{1,3},{2,0},{3,1},{4,6},{5,7},{6,4},{7,5},{8,10},{9,11},{10,... | collective-permute-start | bytes 589832 | tf_op jit(solution)/shard_map/ppermute | solution.py:319
  28.0 1.8 %collective-permute-start.3 = (f32[2,192,128]{2,1,0:T(8,128)}, f32[2,192,128]{2,1,0:T(8,128)S(1)}, u32[]{:S(2)}, u32[]{:S(2)}) collective-permute-start(f32[2,192,128]{2,1,0:T(8,128)} %bitcast.40), channel_id=1, source_target_pairs={{0,8},{1,9},{2,10},{3,11},{4,12},{5,13},{6,14},{7,15},{8,0},{9,1},... | collective-permute-start | bytes 589832 | tf_op jit(solution)/shard_map/ppermute | solution.py:319
  31.2 2.3 %collective-permute-done.refs_1_.refs_2_ = f32[2,192,128]{2,1,0:T(8,128)S(1)} collective-permute-done((f32[2,192,128]{2,1,0:T(8,128)}, f32[2,192,128]{2,1,0:T(8,128)S(1)}, u32[]{:S(2)}, u32[]{:S(2)}) %collective-permute-start) | collective-permute-done | bytes 196640 | tf_op jit(solution)/shard_map/ppermute | solution.py:319
  33.5 2.7 %collective-permute-start.5 = (f32[2,192,128]{2,1,0:T(8,128)}, f32[2,192,128]{2,1,0:T(8,128)S(1)}, u32[]{:S(2)}, u32[]{:S(2)}) collective-permute-start(f32[2,192,128]{2,1,0:T(8,128)} %bitcast.38), channel_id=1, source_target_pairs={{0,12},{1,13},{2,14},{3,15},{4,8},{5,9},{6,10},{7,11},{8,4},{9,5},... | collective-permute-start | bytes 589832 | tf_op jit(solution)/shard_map/ppermute | solution.py:319
  36.2 3.9 %collective-permute-done.1.refs_2_.refs_3_ = f32[2,192,128]{2,1,0:T(8,128)S(1)} collective-permute-done((f32[2,192,128]{2,1,0:T(8,128)}, f32[2,192,128]{2,1,0:T(8,128)S(1)}, u32[]{:S(2)}, u32[]{:S(2)}) %collective-permute-start.1) | collective-permute-done | bytes 196640 | tf_op jit(solution)/shard_map/ppermute | solution.py:319
  40.2 8.9 %collective-permute-start.7 = (f32[2,192,128]{2,1,0:T(8,128)}, f32[2,192,128]{2,1,0:T(8,128)S(1)}, u32[]{:S(2)}, u32[]{:S(2)}) collective-permute-start(f32[2,192,128]{2,1,0:T(8,128)} %bitcast.36), channel_id=1, source_target_pairs={{0,16},{1,17},{2,18},{3,19},{4,20},{5,21},{6,22},{7,23},{8,24},{9,... | collective-permute-start | bytes 589832 | tf_op jit(solution)/shard_map/ppermute | solution.py:319
  49.5 2.3 %collective-permute-start.9 = (f32[2,192,128]{2,1,0:T(8,128)}, f32[2,192,128]{2,1,0:T(8,128)S(1)}, u32[]{:S(2)}, u32[]{:S(2)}) collective-permute-start(f32[2,192,128]{2,1,0:T(8,128)} %bitcast.34), channel_id=1, source_target_pairs={{0,20},{1,21},{2,22},{3,23},{4,16},{5,17},{6,18},{7,19},{8,28},{9,... | collective-permute-start | bytes 589832 | tf_op jit(solution)/shard_map/ppermute | solution.py:319
  51.9 3.6 %collective-permute-start.10 = (f32[2,192,128]{2,1,0:T(8,128)}, f32[2,192,128]{2,1,0:T(8,128)S(1)}, u32[]{:S(2)}, u32[]{:S(2)}) collective-permute-start(f32[2,192,128]{2,1,0:T(8,128)} %bitcast.33), channel_id=1, source_target_pairs={{0,22},{1,23},{2,20},{3,21},{4,18},{5,19},{6,16},{7,17},{8,30},{9,... | collective-permute-start | bytes 589832 | tf_op jit(solution)/shard_map/ppermute | solution.py:319
  55.5 4.2 %collective-permute-done.6.refs_7_.refs_8_ = f32[2,192,128]{2,1,0:T(8,128)S(1)} collective-permute-done((f32[2,192,128]{2,1,0:T(8,128)}, f32[2,192,128]{2,1,0:T(8,128)S(1)}, u32[]{:S(2)}, u32[]{:S(2)}) %collective-permute-start.6) | collective-permute-done | bytes 196640 | tf_op jit(solution)/shard_map/ppermute | solution.py:319
  60.0 14.5 %collective-permute-done.7.refs_8_.refs_9_ = f32[2,192,128]{2,1,0:T(8,128)S(1)} collective-permute-done((f32[2,192,128]{2,1,0:T(8,128)}, f32[2,192,128]{2,1,0:T(8,128)S(1)}, u32[]{:S(2)}, u32[]{:S(2)}) %collective-permute-start.7) | collective-permute-done | bytes 196640 | tf_op jit(solution)/shard_map/ppermute | solution.py:319
  74.6 6.1 %collective-permute-done.8.refs_9_.refs_10_ = f32[2,192,128]{2,1,0:T(8,128)S(1)} collective-permute-done((f32[2,192,128]{2,1,0:T(8,128)}, f32[2,192,128]{2,1,0:T(8,128)S(1)}, u32[]{:S(2)}, u32[]{:S(2)}) %collective-permute-start.8) | collective-permute-done | bytes 196640 | tf_op jit(solution)/shard_map/ppermute | solution.py:319
  80.7 5.1 %collective-permute-done.9.refs_10_.refs_11_ = f32[2,192,128]{2,1,0:T(8,128)S(1)} collective-permute-done((f32[2,192,128]{2,1,0:T(8,128)}, f32[2,192,128]{2,1,0:T(8,128)S(1)}, u32[]{:S(2)}, u32[]{:S(2)}) %collective-permute-start.9) | collective-permute-done | bytes 196640 | tf_op jit(solution)/shard_map/ppermute | solution.py:319
  85.8 2.6 %collective-permute-done.10.refs_11_.refs_12_ = f32[2,192,128]{2,1,0:T(8,128)S(1)} collective-permute-done((f32[2,192,128]{2,1,0:T(8,128)}, f32[2,192,128]{2,1,0:T(8,128)S(1)}, u32[]{:S(2)}, u32[]{:S(2)}) %collective-permute-start.10) | collective-permute-done | bytes 196640 | tf_op jit(solution)/shard_map/ppermute | solution.py:319
  89.1 2.9 %bundle.2 = f32[2496,128]{1,0:T(8,128)} custom-call(s32[1]{0:T(128)} %bitcast.me_ref, f32[2,192,128]{2,1,0:T(8,128)} %bitcast.25, f32[2,192,128]{2,1,0:T(8,128)} %copy-done.2, f32[2,192,128]{2,1,0:T(8,128)} %copy-done.3, f32[2,192,128]{2,1,0:T(8,128)} %copy-done.4, f32[2,192,128]{2,1,0:T(8,128)} %copy-done.5, f32[2,192,128]{2,1,0:T(8,128)} %copy-done.6, ...), custom_call_target="tpu_custom_call" | custom-call | tf_op jit(solution)/shard_map/bundle/pallas_call | solution.py:176
  92.0 3.1 %collective-permute-start.17 = (f32[16,256]{1,0:T(8,128)S(1)}, f32[16,256]{1,0:T(8,128)S(1)}, u32[]{:S(2)}, u32[]{:S(2)}) collective-permute-start(f32[16,256]{1,0:T(8,128)S(1)} %slice_bitcast_fusion), channel_id=1, source_target_pairs={{0,16},{1,17},{2,18},{3,19},{4,20},{5,21},{6,22},{7,23},{8,24},{9,... | collective-permute-start | bytes 49160 | tf_op jit(solution)/shard_map/ppermute | solution.py:319
  95.1 1.7 %collective-permute-done.17 = f32[16,256]{1,0:T(8,128)S(1)} collective-permute-done((f32[16,256]{1,0:T(8,128)S(1)}, f32[16,256]{1,0:T(8,128)S(1)}, u32[]{:S(2)}, u32[]{:S(2)}) %collective-permute-start.17) | collective-permute-done | bytes 16416 | tf_op jit(solution)/shard_map/ppermute | solution.py:319
  96.9 2.2 %collective-permute-start.18 = (f32[16,256]{1,0:T(8,128)S(1)}, f32[16,256]{1,0:T(8,128)S(1)}, u32[]{:S(2)}, u32[]{:S(2)}) collective-permute-start(f32[16,256]{1,0:T(8,128)S(1)} %get-tuple-element.46.refs_0_), channel_id=1, source_target_pairs={{0,2},{1,3},{2,0},{3,1},{4,6},{5,7},{6,4},{7,5},{8,10},{9,11},{10,... | collective-permute-start | bytes 49160 | tf_op jit(solution)/shard_map/ppermute | solution.py:319
  99.0 1.6 %collective-permute-start.12 = (f32[2,192,128]{2,1,0:T(8,128)}, f32[2,192,128]{2,1,0:T(8,128)S(1)}, u32[]{:S(2)}, u32[]{:S(2)}) collective-permute-start(f32[2,192,128]{2,1,0:T(8,128)} %bitcast.31), channel_id=1, source_target_pairs={{0,26},{1,27},{2,24},{3,25},{4,30},{5,31},{6,28},{7,29},{8,18},{9,... | collective-permute-start | bytes 589832 | tf_op jit(solution)/shard_map/ppermute | solution.py:319
  100.7 3.1 %collective-permute-start.13 = (f32[2,192,128]{2,1,0:T(8,128)}, f32[2,192,128]{2,1,0:T(8,128)S(1)}, u32[]{:S(2)}, u32[]{:S(2)}) collective-permute-start(f32[2,192,128]{2,1,0:T(8,128)} %bitcast.30), channel_id=1, source_target_pairs={{0,28},{1,29},{2,30},{3,31},{4,24},{5,25},{6,26},{7,27},{8,20},{9,... | collective-permute-start | bytes 589832 | tf_op jit(solution)/shard_map/ppermute | solution.py:319
  103.7 3.0 %collective-permute-start.14 = (f32[2,192,128]{2,1,0:T(8,128)}, f32[2,192,128]{2,1,0:T(8,128)S(1)}, u32[]{:S(2)}, u32[]{:S(2)}) collective-permute-start(f32[2,192,128]{2,1,0:T(8,128)} %bitcast.29), channel_id=1, source_target_pairs={{0,30},{1,31},{2,28},{3,29},{4,26},{5,27},{6,24},{7,25},{8,22},{9,... | collective-permute-start | bytes 589832 | tf_op jit(solution)/shard_map/ppermute | solution.py:319
  106.8 3.9 %collective-permute-done.19.refs_2_ = f32[16,256]{1,0:T(8,128)S(1)} collective-permute-done((f32[16,256]{1,0:T(8,128)S(1)}, f32[16,256]{1,0:T(8,128)S(1)}, u32[]{:S(2)}, u32[]{:S(2)}) %collective-permute-start.19) | collective-permute-done | bytes 16416 | tf_op jit(solution)/shard_map/ppermute | solution.py:319
  110.7 7.4 %collective-permute-start.20 = (f32[16,256]{1,0:T(8,128)S(1)}, f32[16,256]{1,0:T(8,128)S(1)}, u32[]{:S(2)}, u32[]{:S(2)}) collective-permute-start(f32[16,256]{1,0:T(8,128)S(1)} %get-tuple-element.46.refs_0_), channel_id=1, source_target_pairs={{0,6},{1,7},{2,4},{3,5},{4,2},{5,3},{6,0},{7,1},{8,14},{9,15},{10,... | collective-permute-start | bytes 49160 | tf_op jit(solution)/shard_map/ppermute | solution.py:319
  118.1 1.7 %collective-permute-done.20.refs_3_ = f32[16,256]{1,0:T(8,128)S(1)} collective-permute-done((f32[16,256]{1,0:T(8,128)S(1)}, f32[16,256]{1,0:T(8,128)S(1)}, u32[]{:S(2)}, u32[]{:S(2)}) %collective-permute-start.20) | collective-permute-done | bytes 16416 | tf_op jit(solution)/shard_map/ppermute | solution.py:319
  119.8 3.7 %collective-permute-done.21.refs_4_ = f32[16,256]{1,0:T(8,128)S(1)} collective-permute-done((f32[16,256]{1,0:T(8,128)S(1)}, f32[16,256]{1,0:T(8,128)S(1)}, u32[]{:S(2)}, u32[]{:S(2)}) %collective-permute-start.21) | collective-permute-done | bytes 16416 | tf_op jit(solution)/shard_map/ppermute | solution.py:319
  123.5 4.6 %collective-permute-done.22.refs_5_ = f32[16,256]{1,0:T(8,128)S(1)} collective-permute-done((f32[16,256]{1,0:T(8,128)S(1)}, f32[16,256]{1,0:T(8,128)S(1)}, u32[]{:S(2)}, u32[]{:S(2)}) %collective-permute-start.22) | collective-permute-done | bytes 16416 | tf_op jit(solution)/shard_map/ppermute | solution.py:319
  128.2 1.7 %collective-permute-start.23 = (f32[16,256]{1,0:T(8,128)S(1)}, f32[16,256]{1,0:T(8,128)S(1)}, u32[]{:S(2)}, u32[]{:S(2)}) collective-permute-start(f32[16,256]{1,0:T(8,128)S(1)} %get-tuple-element.46.refs_0_), channel_id=1, source_target_pairs={{0,12},{1,13},{2,14},{3,15},{4,8},{5,9},{6,10},{7,11},{8,4},{9,5},... | collective-permute-start | bytes 49160 | tf_op jit(solution)/shard_map/ppermute | solution.py:319
  132.0 1.9 %bundle.3 = f32[576,128]{1,0:T(8,128)} custom-call(s32[1]{0:T(128)} %bitcast.me_ref, f32[2,192,128]{2,1,0:T(8,128)} %copy-done.14, f32[2,192,128]{2,1,0:T(8,128)} %copy-done.15, f32[2,192,128]{2,1,0:T(8,128)} %copy-done.16), custom_call_target="tpu_custom_call" | custom-call | tf_op jit(solution)/shard_map/bundle/pallas_call | solution.py:176
  137.5 3.7 %mix.1 = (bf16[256,256]{1,0:T(8,128)(2,1)}, bf16[256,256]{1,0:T(8,128)(2,1)}, bf16[256,512]{1,0:T(8,128)(2,1)}, bf16[256,512]{1,0:T(8,128)(2,1)}) custom-call(s32[1]{0:T(128)} %bitcast.me_ref, s32[1,512]{1,0:T(1,128)} %constant.22.clone.spot_ref, s32[1,512]{1,0:T(1,128)} %constant.23.clone.mask_ref, f32[2,256,256]{2,1,0:T(8,128)} %inverse_ref.1, ...), custom_call_target="tpu_custom_call" | custom-call | tf_op jit(solution)/shard_map/mix/pallas_call | solution.py:214
  142.7 9.9 %solve.1 = f32[512,2048]{1,0:T(8,128)} custom-call(s32[1]{0:T(128)} %bitcast.me_ref, f32[2048,128]{1,0:T(8,128)} %bitcast.24, f32[2,192,128]{2,1,0:T(8,128)} %bitcast.26, f32[2,192,128]{2,1,0:T(8,128)} %copy-done.2, f32[2,192,128]{2,1,0:T(8,128)} %copy-done.3, f32[2,192,128]{2,1,0:T(8,128)} %copy-done.4, f32[2,192,128]{2,1,0:T(8,128)} %copy-done.5, ...), custom_call_target="tpu_custom_call" | custom-call | tf_op jit(solution)/shard_map/solve/pallas_call | solution.py:276
  (93 shorter events, 12.0 us)
Async XLA Ops:
  5.5 135.7 %all-to-all-start = ((f32[32,4,2,8,128]{4,3,2,1,0:T(8,128)}), f32[32,4,2,8,128]{4,3,2,1,0:T(8,128)S(1)}, u32[]{:S(2)}, u32[]{:S(2)}) async-start(f32[32,4,2,8,128]{4,3,2,1,0:T(8,128)} %whiten.2), calls=%async_computation | async-start | bytes 2097152 | tf_op jit(solution)/shard_map/all_to_all | solution.py:373
  12.8 79.2 %copy-start.27 = (f32[2,16,256]{2,1,0:T(8,128)S(1)}, f32[2,16,256]{2,1,0:T(8,128)}, u32[]{:S(2)}) copy-start(f32[2,16,256]{2,1,0:T(8,128)} %param.17) | copy-start | bytes 98308
  24.4 9.1 %collective-permute-start = (f32[2,192,128]{2,1,0:T(8,128)}, f32[2,192,128]{2,1,0:T(8,128)S(1)}, u32[]{:S(2)}, u32[]{:S(2)}) collective-permute-start(f32[2,192,128]{2,1,0:T(8,128)} %bitcast.43), channel_id=1, source_target_pairs={{0,2},{1,3},{2,0},{3,1},{4,6},{5,7},{6,4},{7,5},{8,10},{9,11},{10,... | collective-permute-start | bytes 589832 | tf_op jit(solution)/shard_map/ppermute | solution.py:319
  26.3 13.9 %collective-permute-start.1 = (f32[2,192,128]{2,1,0:T(8,128)}, f32[2,192,128]{2,1,0:T(8,128)S(1)}, u32[]{:S(2)}, u32[]{:S(2)}) collective-permute-start(f32[2,192,128]{2,1,0:T(8,128)} %bitcast.42), channel_id=1, source_target_pairs={{0,4},{1,5},{2,6},{3,7},{4,0},{5,1},{6,2},{7,3},{8,12},{9,13},{10,... | collective-permute-start | bytes 589832 | tf_op jit(solution)/shard_map/ppermute | solution.py:319
  27.7 12.4 %collective-permute-start.2 = (f32[2,192,128]{2,1,0:T(8,128)}, f32[2,192,128]{2,1,0:T(8,128)S(1)}, u32[]{:S(2)}, u32[]{:S(2)}) collective-permute-start(f32[2,192,128]{2,1,0:T(8,128)} %bitcast.41), channel_id=1, source_target_pairs={{0,6},{1,7},{2,4},{3,5},{4,2},{5,3},{6,0},{7,1},{8,14},{9,15},{10,... | collective-permute-start | bytes 589832 | tf_op jit(solution)/shard_map/ppermute | solution.py:319
  28.0 21.0 %collective-permute-start.3 = (f32[2,192,128]{2,1,0:T(8,128)}, f32[2,192,128]{2,1,0:T(8,128)S(1)}, u32[]{:S(2)}, u32[]{:S(2)}) collective-permute-start(f32[2,192,128]{2,1,0:T(8,128)} %bitcast.40), channel_id=1, source_target_pairs={{0,8},{1,9},{2,10},{3,11},{4,12},{5,13},{6,14},{7,15},{8,0},{9,1},... | collective-permute-start | bytes 589832 | tf_op jit(solution)/shard_map/ppermute | solution.py:319
  29.8 19.8 %collective-permute-start.4 = (f32[2,192,128]{2,1,0:T(8,128)}, f32[2,192,128]{2,1,0:T(8,128)S(1)}, u32[]{:S(2)}, u32[]{:S(2)}) collective-permute-start(f32[2,192,128]{2,1,0:T(8,128)} %bitcast.39), channel_id=1, source_target_pairs={{0,10},{1,11},{2,8},{3,9},{4,14},{5,15},{6,12},{7,13},{8,2},{9,3},... | collective-permute-start | bytes 589832 | tf_op jit(solution)/shard_map/ppermute | solution.py:319
  33.5 54.8 %copy-start.2 = (f32[2,192,128]{2,1,0:T(8,128)}, f32[2,192,128]{2,1,0:T(8,128)S(1)}, u32[]{:S(2)}) copy-start(f32[2,192,128]{2,1,0:T(8,128)S(1)} %collective-permute-done.refs_1_.refs_2_) | copy-start | bytes 589828
  33.5 18.3 %collective-permute-start.5 = (f32[2,192,128]{2,1,0:T(8,128)}, f32[2,192,128]{2,1,0:T(8,128)S(1)}, u32[]{:S(2)}, u32[]{:S(2)}) collective-permute-start(f32[2,192,128]{2,1,0:T(8,128)} %bitcast.38), channel_id=1, source_target_pairs={{0,12},{1,13},{2,14},{3,15},{4,8},{5,9},{6,10},{7,11},{8,4},{9,5},... | collective-permute-start | bytes 589832 | tf_op jit(solution)/shard_map/ppermute | solution.py:319
  40.1 48.2 %copy-start.3 = (f32[2,192,128]{2,1,0:T(8,128)}, f32[2,192,128]{2,1,0:T(8,128)S(1)}, u32[]{:S(2)}) copy-start(f32[2,192,128]{2,1,0:T(8,128)S(1)} %collective-permute-done.1.refs_2_.refs_3_) | copy-start | bytes 589828
  40.1 19.5 %collective-permute-start.6 = (f32[2,192,128]{2,1,0:T(8,128)}, f32[2,192,128]{2,1,0:T(8,128)S(1)}, u32[]{:S(2)}, u32[]{:S(2)}) collective-permute-start(f32[2,192,128]{2,1,0:T(8,128)} %bitcast.37), channel_id=1, source_target_pairs={{0,14},{1,15},{2,12},{3,13},{4,10},{5,11},{6,8},{7,9},{8,6},{9,7},... | collective-permute-start | bytes 589832 | tf_op jit(solution)/shard_map/ppermute | solution.py:319
  40.2 48.2 %copy-start.4 = (f32[2,192,128]{2,1,0:T(8,128)}, f32[2,192,128]{2,1,0:T(8,128)S(1)}, u32[]{:S(2)}) copy-start(f32[2,192,128]{2,1,0:T(8,128)S(1)} %collective-permute-done.2.refs_3_.refs_4_) | copy-start | bytes 589828
  40.2 34.4 %collective-permute-start.7 = (f32[2,192,128]{2,1,0:T(8,128)}, f32[2,192,128]{2,1,0:T(8,128)S(1)}, u32[]{:S(2)}, u32[]{:S(2)}) collective-permute-start(f32[2,192,128]{2,1,0:T(8,128)} %bitcast.36), channel_id=1, source_target_pairs={{0,16},{1,17},{2,18},{3,19},{4,20},{5,21},{6,22},{7,23},{8,24},{9,... | collective-permute-start | bytes 589832 | tf_op jit(solution)/shard_map/ppermute | solution.py:319
  49.0 31.7 %collective-permute-start.8 = (f32[2,192,128]{2,1,0:T(8,128)}, f32[2,192,128]{2,1,0:T(8,128)S(1)}, u32[]{:S(2)}, u32[]{:S(2)}) collective-permute-start(f32[2,192,128]{2,1,0:T(8,128)} %bitcast.35), channel_id=1, source_target_pairs={{0,18},{1,19},{2,16},{3,17},{4,22},{5,23},{6,20},{7,21},{8,26},{9,... | collective-permute-start | bytes 589832 | tf_op jit(solution)/shard_map/ppermute | solution.py:319
  49.5 36.2 %collective-permute-start.9 = (f32[2,192,128]{2,1,0:T(8,128)}, f32[2,192,128]{2,1,0:T(8,128)S(1)}, u32[]{:S(2)}, u32[]{:S(2)}) collective-permute-start(f32[2,192,128]{2,1,0:T(8,128)} %bitcast.34), channel_id=1, source_target_pairs={{0,20},{1,21},{2,22},{3,23},{4,16},{5,17},{6,18},{7,19},{8,28},{9,... | collective-permute-start | bytes 589832 | tf_op jit(solution)/shard_map/ppermute | solution.py:319
  51.9 36.5 %collective-permute-start.10 = (f32[2,192,128]{2,1,0:T(8,128)}, f32[2,192,128]{2,1,0:T(8,128)S(1)}, u32[]{:S(2)}, u32[]{:S(2)}) collective-permute-start(f32[2,192,128]{2,1,0:T(8,128)} %bitcast.33), channel_id=1, source_target_pairs={{0,22},{1,23},{2,20},{3,21},{4,18},{5,19},{6,16},{7,17},{8,30},{9,... | collective-permute-start | bytes 589832 | tf_op jit(solution)/shard_map/ppermute | solution.py:319
  59.7 28.7 %collective-permute-start.11 = (f32[2,192,128]{2,1,0:T(8,128)}, f32[2,192,128]{2,1,0:T(8,128)S(1)}, u32[]{:S(2)}, u32[]{:S(2)}) collective-permute-start(f32[2,192,128]{2,1,0:T(8,128)} %bitcast.32), channel_id=1, source_target_pairs={{0,24},{1,25},{2,26},{3,27},{4,28},{5,29},{6,30},{7,31},{8,16},{9,... | collective-permute-start | bytes 589832 | tf_op jit(solution)/shard_map/ppermute | solution.py:319
  92.0 49.2 %collective-permute-start.15 = (f32[2496,128]{1,0:T(8,128)}, f32[2496,128]{1,0:T(8,128)S(1)}, u32[]{:S(2)}, u32[]{:S(2)}) collective-permute-start(f32[2496,128]{1,0:T(8,128)} %bundle.2), channel_id=1, source_target_pairs={{0,1},{1,0},{2,3},{3,2},{4,5},{5,4},{6,7},{7,6},{8,9},{9,8},{10,11... | collective-permute-start | bytes 3833864 | tf_op jit(solution)/shard_map/ppermute | solution.py:319
  92.0 4.8 %collective-permute-start.17 = (f32[16,256]{1,0:T(8,128)S(1)}, f32[16,256]{1,0:T(8,128)S(1)}, u32[]{:S(2)}, u32[]{:S(2)}) collective-permute-start(f32[16,256]{1,0:T(8,128)S(1)} %slice_bitcast_fusion), channel_id=1, source_target_pairs={{0,16},{1,17},{2,18},{3,19},{4,20},{5,21},{6,22},{7,23},{8,24},{9,... | collective-permute-start | bytes 49160 | tf_op jit(solution)/shard_map/ppermute | solution.py:319
  96.8 40.0 %copy-start.26 = (f32[16,256]{1,0:T(8,128)}, f32[16,256]{1,0:T(8,128)S(1)}, u32[]{:S(2)}) copy-start(f32[16,256]{1,0:T(8,128)S(1)} %get-tuple-element.46.refs_0_) | copy-start | bytes 49156
  96.9 9.9 %collective-permute-start.18 = (f32[16,256]{1,0:T(8,128)S(1)}, f32[16,256]{1,0:T(8,128)S(1)}, u32[]{:S(2)}, u32[]{:S(2)}) collective-permute-start(f32[16,256]{1,0:T(8,128)S(1)} %get-tuple-element.46.refs_0_), channel_id=1, source_target_pairs={{0,2},{1,3},{2,0},{3,1},{4,6},{5,7},{6,4},{7,5},{8,10},{9,11},{10,... | collective-permute-start | bytes 49160 | tf_op jit(solution)/shard_map/ppermute | solution.py:319
  99.0 30.8 %collective-permute-start.12 = (f32[2,192,128]{2,1,0:T(8,128)}, f32[2,192,128]{2,1,0:T(8,128)S(1)}, u32[]{:S(2)}, u32[]{:S(2)}) collective-permute-start(f32[2,192,128]{2,1,0:T(8,128)} %bitcast.31), channel_id=1, source_target_pairs={{0,26},{1,27},{2,24},{3,25},{4,30},{5,31},{6,28},{7,29},{8,18},{9,... | collective-permute-start | bytes 589832 | tf_op jit(solution)/shard_map/ppermute | solution.py:319
  100.7 30.0 %collective-permute-start.13 = (f32[2,192,128]{2,1,0:T(8,128)}, f32[2,192,128]{2,1,0:T(8,128)S(1)}, u32[]{:S(2)}, u32[]{:S(2)}) collective-permute-start(f32[2,192,128]{2,1,0:T(8,128)} %bitcast.30), channel_id=1, source_target_pairs={{0,28},{1,29},{2,30},{3,31},{4,24},{5,25},{6,26},{7,27},{8,20},{9,... | collective-permute-start | bytes 589832 | tf_op jit(solution)/shard_map/ppermute | solution.py:319
  103.7 26.9 %collective-permute-start.14 = (f32[2,192,128]{2,1,0:T(8,128)}, f32[2,192,128]{2,1,0:T(8,128)S(1)}, u32[]{:S(2)}, u32[]{:S(2)}) collective-permute-start(f32[2,192,128]{2,1,0:T(8,128)} %bitcast.29), channel_id=1, source_target_pairs={{0,30},{1,31},{2,28},{3,29},{4,26},{5,27},{6,24},{7,25},{8,22},{9,... | collective-permute-start | bytes 589832 | tf_op jit(solution)/shard_map/ppermute | solution.py:319
  106.8 3.9 %collective-permute-start.19 = (f32[16,256]{1,0:T(8,128)S(1)}, f32[16,256]{1,0:T(8,128)S(1)}, u32[]{:S(2)}, u32[]{:S(2)}) collective-permute-start(f32[16,256]{1,0:T(8,128)S(1)} %get-tuple-element.46.refs_0_), channel_id=1, source_target_pairs={{0,4},{1,5},{2,6},{3,7},{4,0},{5,1},{6,2},{7,3},{8,12},{9,13},{10,... | collective-permute-start | bytes 49160 | tf_op jit(solution)/shard_map/ppermute | solution.py:319
  110.7 9.1 %collective-permute-start.20 = (f32[16,256]{1,0:T(8,128)S(1)}, f32[16,256]{1,0:T(8,128)S(1)}, u32[]{:S(2)}, u32[]{:S(2)}) collective-permute-start(f32[16,256]{1,0:T(8,128)S(1)} %get-tuple-element.46.refs_0_), channel_id=1, source_target_pairs={{0,6},{1,7},{2,4},{3,5},{4,2},{5,3},{6,0},{7,1},{8,14},{9,15},{10,... | collective-permute-start | bytes 49160 | tf_op jit(solution)/shard_map/ppermute | solution.py:319
  119.8 3.7 %collective-permute-start.21 = (f32[16,256]{1,0:T(8,128)S(1)}, f32[16,256]{1,0:T(8,128)S(1)}, u32[]{:S(2)}, u32[]{:S(2)}) collective-permute-start(f32[16,256]{1,0:T(8,128)S(1)} %get-tuple-element.46.refs_0_), channel_id=1, source_target_pairs={{0,8},{1,9},{2,10},{3,11},{4,12},{5,13},{6,14},{7,15},{8,0},{9,1},... | collective-permute-start | bytes 49160 | tf_op jit(solution)/shard_map/ppermute | solution.py:319
  123.5 4.6 %collective-permute-start.22 = (f32[16,256]{1,0:T(8,128)S(1)}, f32[16,256]{1,0:T(8,128)S(1)}, u32[]{:S(2)}, u32[]{:S(2)}) collective-permute-start(f32[16,256]{1,0:T(8,128)S(1)} %get-tuple-element.46.refs_0_), channel_id=1, source_target_pairs={{0,10},{1,11},{2,8},{3,9},{4,14},{5,15},{6,12},{7,13},{8,2},{9,3},... | collective-permute-start | bytes 49160 | tf_op jit(solution)/shard_map/ppermute | solution.py:319
  128.2 5.7 %collective-permute-start.23 = (f32[16,256]{1,0:T(8,128)S(1)}, f32[16,256]{1,0:T(8,128)S(1)}, u32[]{:S(2)}, u32[]{:S(2)}) collective-permute-start(f32[16,256]{1,0:T(8,128)S(1)} %get-tuple-element.46.refs_0_), channel_id=1, source_target_pairs={{0,12},{1,13},{2,14},{3,15},{4,8},{5,9},{6,10},{7,11},{8,4},{9,5},... | collective-permute-start | bytes 49160 | tf_op jit(solution)/shard_map/ppermute | solution.py:319
  129.9 5.6 %collective-permute-start.24 = (f32[16,256]{1,0:T(8,128)S(1)}, f32[16,256]{1,0:T(8,128)S(1)}, u32[]{:S(2)}, u32[]{:S(2)}) collective-permute-start(f32[16,256]{1,0:T(8,128)S(1)} %get-tuple-element.46.refs_0_), channel_id=1, source_target_pairs={{0,14},{1,15},{2,12},{3,13},{4,10},{5,11},{6,8},{7,9},{8,6},{9,7},... | collective-permute-start | bytes 49160 | tf_op jit(solution)/shard_map/ppermute | solution.py:319
  133.9 7.3 %collective-permute-start.16 = (f32[576,128]{1,0:T(8,128)}, f32[576,128]{1,0:T(8,128)S(1)}, u32[]{:S(2)}, u32[]{:S(2)}) collective-permute-start(f32[576,128]{1,0:T(8,128)} %bundle.3), channel_id=1, source_target_pairs={{0,1},{1,0},{2,3},{3,2},{4,5},{5,4},{6,7},{7,6},{8,9},{9,8},{10,11... | collective-permute-start | bytes 884744 | tf_op jit(solution)/shard_map/ppermute | solution.py:319
  135.5 1.3 collective-permute-start.25
  (23 other events, 274.9 us)

commit v3 on v2

--- a/solution.py
+++ b/solution.py
@@ -6,6 +6,8 @@
 from jax.experimental import pallas as pl
 from jax.experimental.pallas import tpu as pltpu
 from jax.sharding import PartitionSpec as P
+
+LIMIT = pltpu.CompilerParams(vmem_limit_bytes=32 << 20)
 
 
 def basis(length):
@@ -106,8 +108,10 @@
             target[:, r, part] = y[r * length:(r + 1) * length, part * LANES:(part + 1) * LANES].reshape(groups, rows, LANES)
     if stage:
         chip = me_ref[0] // 2
-        for k, o_ref in enumerate(o_refs):
+        for k, o_ref in enumerate(o_refs[:groups // 4]):
             o_ref[...] = target[pl.ds(2 * (chip ^ k), 2)]
+        for way, o_ref in enumerate(o_refs[groups // 4:], groups // 2):
+            o_ref[...] = target[pl.ds(me_ref[0] ^ way, 1)]
 
 
 def whiten(me, x, spectral_filter, groups, start, count, rb, spread):
@@ -116,21 +120,22 @@
     fh, fl = basis(length)
     const = lambda shape: pl.BlockSpec(shape, lambda i, me: (0,) * len(shape), pipeline_mode=pl.Buffered(1))
     off = start // rb
-    outs, lead = (groups // 2, 2) if spread else (1, groups)
+    leads = [2] * (groups // 4) + [1] * (groups // 2) if spread else [groups]
     scratch = [pltpu.VMEM((length, length), jnp.float32)] * 2
     if spread:
         scratch.append(pltpu.VMEM((groups, rb, parts, rows, LANES), jnp.float32))
     return pl.pallas_call(
-        functools.partial(whiten_kernel, rb=rb, groups=groups, outs=outs),
+        functools.partial(whiten_kernel, rb=rb, groups=groups, outs=len(leads)),
         grid_spec=pltpu.PrefetchScalarGridSpec(
             num_scalar_prefetch=1,
             grid=(count // rb,),
             in_specs=[pl.BlockSpec((rb, length, length), lambda i, me: (i + off, 0, 0)),
                       const((spectral_filter.shape[1], length))] + [const((length, length))] * 4,
-            out_specs=[pl.BlockSpec((lead, rb, parts, rows, LANES), lambda i, me: (0, i, 0, 0, 0))] * outs,
+            out_specs=[pl.BlockSpec((lead, rb, parts, rows, LANES), lambda i, me: (0, i, 0, 0, 0)) for lead in leads],
             scratch_shapes=scratch,
         ),
-        out_shape=[jax.ShapeDtypeStruct((lead, count, parts, rows, LANES), jnp.float32)] * outs,
+        out_shape=[jax.ShapeDtypeStruct((lead, count, parts, rows, LANES), jnp.float32) for lead in leads],
+        compiler_params=LIMIT,
         name="whiten",
     )(me, x, spectral_filter.T, fh, fl, fh.T, fl.T)
 
@@ -160,14 +165,19 @@
     return pl.BlockSpec(shape, lambda i, me: (0,) * len(shape), pipeline_mode=pl.Buffered(1))
 
 
-def here():
-    return pl.BlockSpec(memory_space=pltpu.VMEM)
+def outside(arrays):
+    return [pltpu.with_memory_space_constraint(a, pltpu.HBM) for a in arrays]
+
+
+def parity(array, flip):
+    pick = (lambda i, me: (1 - me[0] % 2, 0, 0)) if flip else (lambda i, me: (me[0] % 2, 0, 0))
+    return pl.BlockSpec((None,) + array.shape[1:], pick, pipeline_mode=pl.Buffered(1))
 
 
 def bundle_kernel(me_ref, *refs):
-    size = refs[0].shape[1]
+    size = refs[0].shape[0]
     for j, ref in enumerate(refs[:-1]):
-        refs[-1][j * size:(j + 1) * size] = ref[1 - me_ref[0] % 2]
+        refs[-1][j * size:(j + 1) * size] = ref[...]
 
 
 def bundle(me, arrays):
@@ -176,9 +186,23 @@
     return pl.pallas_call(
         bundle_kernel,
         grid_spec=pltpu.PrefetchScalarGridSpec(
-            num_scalar_prefetch=1, grid=(1,), in_specs=[here() for a in arrays], out_specs=here()),
+            num_scalar_prefetch=1, grid=(1,), in_specs=[parity(a, True) for a in arrays], out_specs=whole(shape)),
         out_shape=jax.ShapeDtypeStruct(shape, jnp.float32),
+        compiler_params=LIMIT,
         name="bundle",
+    )(me, *arrays)
+
+
+def stack(me, arrays):
+    rows, lanes = arrays[0].shape
+    shape = (len(arrays) * rows, lanes)
+    return pl.pallas_call(
+        bundle_kernel,
+        grid_spec=pltpu.PrefetchScalarGridSpec(
+            num_scalar_prefetch=1, grid=(1,), in_specs=[whole(a.shape) for a in arrays], out_specs=whole(shape)),
+        out_shape=jax.ShapeDtypeStruct(shape, jnp.float32),
+        compiler_params=LIMIT,
+        name="stack",
     )(me, *arrays)
 
 
@@ -215,10 +239,11 @@
         functools.partial(mix_kernel, top=top, local=local),
         grid_spec=pltpu.PrefetchScalarGridSpec(
             num_scalar_prefetch=1, grid=(1,),
-            in_specs=[whole(spots.shape), whole(masks.shape), whole(inverses.shape)] + [here()] * (len(papers) + 1),
-            out_specs=[here()] * len(shapes),
+            in_specs=[whole(a.shape) for a in args],
+            out_specs=[whole(shape) for shape in shapes],
             scratch_shapes=[pltpu.VMEM((width, width), jnp.float32)]),
         out_shape=[jax.ShapeDtypeStruct(shape, jnp.bfloat16) for shape in shapes],
+        compiler_params=LIMIT,
         name="mix",
     )(me, *args)
 
@@ -240,10 +265,7 @@
                 for n, start, size in picks:
                     if start is None:
                         start = (left ^ block) * (size * stride)
-                    ref = w_refs[n]
-                    if len(ref.shape) == 3:
-                        ref = ref.at[me_ref[0] % 2]
-                    column.append(ref[pl.ds(start + at, size, stride=stride), :])
+                    column.append(w_refs[n][pl.ds(start + at, size, stride=stride), :])
                 columns.append(jnp.concatenate(column, axis=0))
         high, low = split(jnp.concatenate(columns, axis=1))
         held_ref[block, 0] = high
@@ -259,19 +281,16 @@
     o_ref[width:] = out
 
 
-def solve(me, head, got, load, final, late, rest, tables, rows, parts, top):
-    chips = len(got)
+def solve(me, head, got, load, direct, rest, tables, rows, parts, top):
     each = rows * parts
-    early = chips - late
     per = 2 if rows % 2 == 0 else 1
-    args = [head, *got, load, final, *tables]
+    args = [*outside([head]), *got, load, *outside([*direct, *tables])]
+    specs = [parity(a, False) if a.ndim == 3 else whole(a.shape) for a in args]
+    pair = lambda n, size: (n, 0, size)
     half_rows = head.shape[0] // each // 2
-    pair = lambda n, start, size: (n, start * each, size)
-    near = [(0, None, half_rows)] + [pair(1 + k, 0, rest) for k in range(chips // 2)]
-    near += [pair(1 + chips, 0, chips // 2 * rest)]
-    far = [(0, None, half_rows)] + [pair(1 + k, 0, rest) for k in range(chips // 2, chips)]
-    far += [pair(1 + chips, chips // 2 * rest, (early - chips // 2) * rest), pair(2 + chips, 0, late * rest)]
-    specs = [here()] * len(args)
+    near = [(0, None, half_rows)] + [pair(1 + k, rest) for k in range(len(got))]
+    near += [pair(1 + len(got), len(got) * rest)]
+    far = [(0, None, half_rows)] + [pair(2 + len(got) + k, rest) for k in range(len(direct))]
     width = tables[0].shape[0]
     return pl.pallas_call(
         functools.partial(solve_kernel, rows=rows, parts=parts, per=per, near=tuple(near), far=tuple(far), top=top),
@@ -280,6 +299,7 @@
             out_specs=pl.BlockSpec((2 * width, per * parts * LANES), lambda i, me: (0, i)),
             scratch_shapes=[pltpu.VMEM((2, 2, width, per * parts * LANES), jnp.bfloat16)]),
         out_shape=jax.ShapeDtypeStruct((2 * width, each * LANES), jnp.float32),
+        compiler_params=LIMIT,
         name="solve",
     )(me, *args)
 
@@ -311,7 +331,6 @@
 
 
 HEAD = 4
-LATE = 3
 
 
 def exchange(x, offset):
@@ -336,18 +355,16 @@
     return out
 
 
-def places(groups, local, early, late):
+def places(groups, local):
     top = groups // 2
     rest = range(HEAD, local)
+    ways = list(range(0, top, 2)) + list(range(1, top, 2)) + list(range(top, groups))
     spots, masks = [], []
     for far in range(2):
         for source in range(top):
             spots += [(source + far * top) * local + r for r in range(HEAD)]
             masks += [top * local] * HEAD
-        mine = [k for k in early + late if (2 * k >= top) == bool(far)]
-        ways = [2 * k for k in mine]
-        ways += [2 * k + 1 for k in mine]
-        for way in ways:
+        for way in ways[far * top : (far + 1) * top]:
             spots += [way * local + r for r in rest]
             masks += [-1] * len(rest)
     return np.array([spots], np.int32), np.array([masks], np.int32)
@@ -365,28 +382,25 @@
         return general(me, runs_field, spectral_filter, block_inverses, factor_panels)
     rest = local - HEAD
     near = list(range(1, chips // 2))
-    far = list(range(chips // 2, chips))
-    early, late = [0] + near + far[:-LATE], far[-LATE:]
     mine = factor_panels[0]
     mine = jnp.where(place < top, exchange(mine, top), mine)
     (head,) = whiten(me, runs_field, spectral_filter, groups, 0, HEAD, HEAD, False)
     head = lax.all_to_all(head, "dev", 0, 0, tiled=True)
     outs = whiten(me, runs_field, spectral_filter, groups, HEAD, rest, HEAD, True)
-    outs = [o.reshape(2, -1, LANES) for o in outs]
-    got = [outs[0]] + [None] * (chips - 1)
+    got = [outs[0].reshape(2, -1, LANES)]
     papers = [mine]
     for k in near:
         papers.append(exchange(mine, 2 * k))
-    for k in near + far:
-        got[k] = exchange(outs[k], 2 * k)
-    theirs = exchange(jnp.concatenate(papers, axis=0), 1)
-    spots, masks = places(groups, local, early, late)
-    tables = mix(me, spots, masks, block_inverses, papers, theirs, top, local)
-    load = bundle(me, [got[k] for k in early])
+    for k in near:
+        got.append(exchange(outs[k].reshape(2, -1, LANES), 2 * k))
+    direct = []
+    for way in range(top, groups):
+        direct.append(exchange(outs[way - chips // 2].reshape(-1, LANES), way))
+    theirs = exchange(stack(me, papers), 1)
+    tables = mix(me, *places(groups, local), block_inverses, papers, theirs, top, local)
+    load = bundle(me, got)
     load = exchange(load, 1)
-    final = bundle(me, [got[k] for k in late])
-    final = exchange(final, 1)
-    return solve(me, head.reshape(-1, LANES), got, load, final, LATE, rest, tables, rows, parts, top)
+    return solve(me, head.reshape(-1, LANES), got, load, direct, rest, tables, rows, parts, top)
 
 
 def solution(mesh):

time: 153 us -> 156 us (1.020)
  the two profiles are of different devices: /device:TPU:0 before, /device:TPU:11 now
where the time goes in v3:
time: 156 us; the launch traced here: 155 us
  starting transfers between devices  70.7 us (45%)
  waiting for transfers between devices  39.8 us (26%)
  Pallas kernels  24.8 us (16%)
  local copies, waits for them, and re-layouts  19.1 us (12%)
    ppermute x33, starting transfers between devices, exchange(): return lax.ppermute(x, 'dev', pairs)  64.4 us
    ppermute x33, waiting for transfers between devices, exchange(): return lax.ppermute(x, 'dev', pairs)  39.8 us
    unnamed x92, local copies, waits for them, and re-layouts  18.5 us
    pallas_call x2, Pallas kernels, whiten(): pl.pallas_call(functools.partial(whiten_kernel, rb=rb, groups=groups, out...  14.1 us
    pallas_call x1, Pallas kernels, solve(): pl.pallas_call(functools.partial(solve_kernel, rows=rows, parts=parts, pe...  8.96 us
    all_to_all x1, starting transfers between devices, per_device(): head = lax.all_to_all(head, 'dev', 0, 0, tiled=True)  6.35 us
  transfers between devices with their start and end apart: 34, of which 16 were waited for; matrix products, arithmetic and copies ran while one was open for 1% of the time, Pallas kernels for 8%

profile of v3, /device:TPU:11, one launch (start us, length us, event | category | flops | bytes accessed | tf_op | source)
XLA Modules:
  0.0 155.4 jit_solution(7128135328532620715)
XLA Ops:
  0.0 2.2 %copy-done = f32[16,256,256]{2,1,0:T(8,128)S(1)} copy-done((f32[16,256,256]{2,1,0:T(8,128)S(1)}, f32[16,256,256]{2,1,0:T(8,128)}, u32[]{:S(2)}) %copy-start) | copy-done | bytes 4194328
  6.7 4.1 %whiten.2 = f32[32,4,2,8,128]{4,3,2,1,0:T(8,128)} custom-call(s32[1]{0:T(128)} %bitcast.me_ref, f32[16,256,256]{2,1,0:T(8,128)S(1)} %copy-done, f32[129,256]{1,0:T(8,128)S(1)} %bitcast.33, bf16[256,256]{1,0:T(8,128)(2,1)S(1)} %copy-done.10, bf16[256,256]{1,0:T(8,128)(2,1)S(1)} %copy-done.8, bf16[256,256]{1,0:T(8,128)(2,1)S(1)} %copy-done.6, ...), custom_call_target="tpu_custom_call" | custom-call | tf_op jit(solution)/shard_map/whiten/pallas_call | solution.py:127
  10.8 6.4 %all-to-all-start = ((f32[32,4,2,8,128]{4,3,2,1,0:T(8,128)}), f32[32,4,2,8,128]{4,3,2,1,0:T(8,128)}, u32[]{:S(2)}, u32[]{:S(2)}) async-start(f32[32,4,2,8,128]{4,3,2,1,0:T(8,128)} %whiten.2), calls=%async_computation | async-start | bytes 2097152 | tf_op jit(solution)/shard_map/all_to_all | solution.py:388
  17.2 2.2 %copy-done.1 = f32[16,256,256]{2,1,0:T(8,128)S(1)} copy-done((f32[16,256,256]{2,1,0:T(8,128)S(1)}, f32[16,256,256]{2,1,0:T(8,128)}, u32[]{:S(2)}) %copy-start.1) | copy-done | bytes 4194328
  19.4 10.0 %whiten.3 = (f32[2,12,2,8,128]{4,3,2,1,0:T(8,128)S(1)}, f32[2,12,2,8,128]{4,3,2,1,0:T(8,128)S(1)}, f32[2,12,2,8,128]{4,3,2,1,0:T(8,128)S(1)}, f32[2,12,2,8,128]{...) custom-call(s32[1]{0:T(128)} %bitcast.me_ref, ...), custom_call_target="tpu_custom_call" | custom-call | tf_op jit(solution)/shard_map/whiten/pallas_call | solution.py:127
  38.1 2.9 %collective-permute-done.refs_1_.refs_2_ = f32[2,192,128]{2,1,0:T(8,128)S(1)} collective-permute-done((f32[2,192,128]{2,1,0:T(8,128)S(1)}, f32[2,192,128]{2,1,0:T(8,128)S(1)}, u32[]{:S(2)}, u32[]{:S(2)}) %collective-permute-start) | collective-permute-done | bytes 196640 | tf_op jit(solution)/shard_map/ppermute | solution.py:338
  41.0 1.7 %collective-permute-start.5 = (f32[2,192,128]{2,1,0:T(8,128)S(1)}, f32[2,192,128]{2,1,0:T(8,128)S(1)}, u32[]{:S(2)}, u32[]{:S(2)}) collective-permute-start(f32[2,192,128]{2,1,0:T(8,128)S(1)} %bitcast.36), channel_id=1, source_target_pairs={{0,12},{1,13},{2,14},{3,15},{4,8},{5,9},{6,10},{7,11},{8,4},{9,5},... | collective-permute-start | bytes 589832 | tf_op jit(solution)/shard_map/ppermute | solution.py:338
  42.7 4.1 %collective-permute-start.6 = (f32[2,192,128]{2,1,0:T(8,128)S(1)}, f32[2,192,128]{2,1,0:T(8,128)S(1)}, u32[]{:S(2)}, u32[]{:S(2)}) collective-permute-start(f32[2,192,128]{2,1,0:T(8,128)S(1)} %bitcast.35), channel_id=1, source_target_pairs={{0,14},{1,15},{2,12},{3,13},{4,10},{5,11},{6,8},{7,9},{8,6},{9,7},... | collective-permute-start | bytes 589832 | tf_op jit(solution)/shard_map/ppermute | solution.py:338
  46.9 4.0 %collective-permute-done.2.refs_3_.refs_4_ = f32[2,192,128]{2,1,0:T(8,128)S(1)} collective-permute-done((f32[2,192,128]{2,1,0:T(8,128)S(1)}, f32[2,192,128]{2,1,0:T(8,128)S(1)}, u32[]{:S(2)}, u32[]{:S(2)}) %collective-permute-start.2) | collective-permute-done | bytes 196640 | tf_op jit(solution)/shard_map/ppermute | solution.py:338
  51.7 4.4 %collective-permute-done.6.refs_7_.refs_8_ = f32[2,192,128]{2,1,0:T(8,128)S(1)} collective-permute-done((f32[2,192,128]{2,1,0:T(8,128)S(1)}, f32[2,192,128]{2,1,0:T(8,128)S(1)}, u32[]{:S(2)}, u32[]{:S(2)}) %collective-permute-start.6) | collective-permute-done | bytes 196640 | tf_op jit(solution)/shard_map/ppermute | solution.py:338
  56.2 2.8 %collective-permute-start.7 = (f32[1536,128]{1,0:T(8,128)S(1)}, f32[1536,128]{1,0:T(8,128)S(1)}, u32[]{:S(2)}, u32[]{:S(2)}) collective-permute-start(f32[1536,128]{1,0:T(8,128)S(1)} %bundle.1), channel_id=1, source_target_pairs={{0,1},{1,0},{2,3},{3,2},{4,5},{5,4},{6,7},{7,6},{8,9},{9,8},{10,11... | collective-permute-start | bytes 2359304 | tf_op jit(solution)/shard_map/ppermute | solution.py:338
  59.6 2.5 %collective-permute-start.24 = (f32[16,256]{1,0:T(8,128)}, f32[16,256]{1,0:T(8,128)}, u32[]{:S(2)}, u32[]{:S(2)}) collective-permute-start(f32[16,256]{1,0:T(8,128)} %slice_bitcast_fusion), channel_id=1, source_target_pairs={{0,16},{1,17},{2,18},{3,19},{4,20},{5,21},{6,22},{7,23},{8,24},{9,... | collective-permute-start | bytes 49160 | tf_op jit(solution)/shard_map/ppermute | solution.py:338
  64.2 1.6 %collective-permute-start.31 = (f32[16,256]{1,0:T(8,128)S(1)}, f32[16,256]{1,0:T(8,128)S(1)}, u32[]{:S(2)}, u32[]{:S(2)}) collective-permute-start(f32[16,256]{1,0:T(8,128)S(1)} %broadcast_select_fusion.refs_0_), channel_id=1, source_target_pairs={{0,14},{1,15},{2,12},{3,13},{4,10},{5,11},{6,8},{7,9},{8,6},{9,7},... | collective-permute-start | bytes 49160 | tf_op jit(solution)/shard_map/ppermute | solution.py:338
  65.9 1.6 %collective-permute-start.30 = (f32[16,256]{1,0:T(8,128)S(1)}, f32[16,256]{1,0:T(8,128)S(1)}, u32[]{:S(2)}, u32[]{:S(2)}) collective-permute-start(f32[16,256]{1,0:T(8,128)S(1)} %broadcast_select_fusion.refs_0_), channel_id=1, source_target_pairs={{0,12},{1,13},{2,14},{3,15},{4,8},{5,9},{6,10},{7,11},{8,4},{9,5},... | collective-permute-start | bytes 49160 | tf_op jit(solution)/shard_map/ppermute | solution.py:338
  71.0 7.3 %collective-permute-start.9 = (f32[192,128]{1,0:T(8,128)}, f32[192,128]{1,0:T(8,128)S(1)}, u32[]{:S(2)}, u32[]{:S(2)}) collective-permute-start(f32[192,128]{1,0:T(8,128)} %bitcast.56), channel_id=1, source_target_pairs={{0,17},{1,16},{2,19},{3,18},{4,21},{5,20},{6,23},{7,22},{8,25},{9,... | collective-permute-start | bytes 294920 | tf_op jit(solution)/shard_map/ppermute | solution.py:338
  81.3 4.2 %collective-permute-start.11 = (f32[192,128]{1,0:T(8,128)}, f32[192,128]{1,0:T(8,128)S(1)}, u32[]{:S(2)}, u32[]{:S(2)}) collective-permute-start(f32[192,128]{1,0:T(8,128)} %bitcast.54), channel_id=1, source_target_pairs={{0,19},{1,18},{2,17},{3,16},{4,23},{5,22},{6,21},{7,20},{8,27},{9,... | collective-permute-start | bytes 294920 | tf_op jit(solution)/shard_map/ppermute | solution.py:338
  85.5 1.5 collective-permute-start.12
  89.2 5.3 %collective-permute-done.11.refs_13_ = f32[192,128]{1,0:T(8,128)S(1)} collective-permute-done((f32[192,128]{1,0:T(8,128)}, f32[192,128]{1,0:T(8,128)S(1)}, u32[]{:S(2)}, u32[]{:S(2)}) %collective-permute-start.11) | collective-permute-done | bytes 98336 | tf_op jit(solution)/shard_map/ppermute | solution.py:338
  94.5 4.5 %collective-permute-start.15 = (f32[192,128]{1,0:T(8,128)}, f32[192,128]{1,0:T(8,128)S(1)}, u32[]{:S(2)}, u32[]{:S(2)}) collective-permute-start(f32[192,128]{1,0:T(8,128)} %bitcast.50), channel_id=1, source_target_pairs={{0,23},{1,22},{2,21},{3,20},{4,19},{5,18},{6,17},{7,16},{8,31},{9,... | collective-permute-start | bytes 294920 | tf_op jit(solution)/shard_map/ppermute | solution.py:338
  99.0 3.4 %collective-permute-start.16 = (f32[192,128]{1,0:T(8,128)}, f32[192,128]{1,0:T(8,128)S(1)}, u32[]{:S(2)}, u32[]{:S(2)}) collective-permute-start(f32[192,128]{1,0:T(8,128)} %bitcast.49), channel_id=1, source_target_pairs={{0,24},{1,25},{2,26},{3,27},{4,28},{5,29},{6,30},{7,31},{8,16},{9,... | collective-permute-start | bytes 294920 | tf_op jit(solution)/shard_map/ppermute | solution.py:338
  103.0 3.0 %collective-permute-done.14.refs_16_ = f32[192,128]{1,0:T(8,128)S(1)} collective-permute-done((f32[192,128]{1,0:T(8,128)}, f32[192,128]{1,0:T(8,128)S(1)}, u32[]{:S(2)}, u32[]{:S(2)}) %collective-permute-start.14) | collective-permute-done | bytes 98336 | tf_op jit(solution)/shard_map/ppermute | solution.py:338
  106.2 1.9 %collective-permute-done.15.refs_17_ = f32[192,128]{1,0:T(8,128)S(1)} collective-permute-done((f32[192,128]{1,0:T(8,128)}, f32[192,128]{1,0:T(8,128)S(1)}, u32[]{:S(2)}, u32[]{:S(2)}) %collective-permute-start.15) | collective-permute-done | bytes 98336 | tf_op jit(solution)/shard_map/ppermute | solution.py:338
  108.1 3.8 %collective-permute-start.18 = (f32[192,128]{1,0:T(8,128)}, f32[192,128]{1,0:T(8,128)S(1)}, u32[]{:S(2)}, u32[]{:S(2)}) collective-permute-start(f32[192,128]{1,0:T(8,128)} %bitcast.47), channel_id=1, source_target_pairs={{0,26},{1,27},{2,24},{3,25},{4,30},{5,31},{6,28},{7,29},{8,18},{9,... | collective-permute-start | bytes 294920 | tf_op jit(solution)/shard_map/ppermute | solution.py:338
  111.9 2.5 %collective-permute-done.16.refs_18_ = f32[192,128]{1,0:T(8,128)S(1)} collective-permute-done((f32[192,128]{1,0:T(8,128)}, f32[192,128]{1,0:T(8,128)S(1)}, u32[]{:S(2)}, u32[]{:S(2)}) %collective-permute-start.16) | collective-permute-done | bytes 98336 | tf_op jit(solution)/shard_map/ppermute | solution.py:338
  114.7 2.4 %collective-permute-done.17.refs_19_ = f32[192,128]{1,0:T(8,128)S(1)} collective-permute-done((f32[192,128]{1,0:T(8,128)}, f32[192,128]{1,0:T(8,128)S(1)}, u32[]{:S(2)}, u32[]{:S(2)}) %collective-permute-start.17) | collective-permute-done | bytes 98336 | tf_op jit(solution)/shard_map/ppermute | solution.py:338
  117.1 8.9 %collective-permute-start.20 = (f32[192,128]{1,0:T(8,128)S(1)}, f32[192,128]{1,0:T(8,128)S(1)}, u32[]{:S(2)}, u32[]{:S(2)}) collective-permute-start(f32[192,128]{1,0:T(8,128)S(1)} %bitcast.45), channel_id=1, source_target_pairs={{0,28},{1,29},{2,30},{3,31},{4,24},{5,25},{6,26},{7,27},{8,20},{9,... | collective-permute-start | bytes 294920 | tf_op jit(solution)/shard_map/ppermute | solution.py:338
  126.0 5.1 %collective-permute-done.18.refs_20_ = f32[192,128]{1,0:T(8,128)S(1)} collective-permute-done((f32[192,128]{1,0:T(8,128)}, f32[192,128]{1,0:T(8,128)S(1)}, u32[]{:S(2)}, u32[]{:S(2)}) %collective-permute-start.18) | collective-permute-done | bytes 98336 | tf_op jit(solution)/shard_map/ppermute | solution.py:338
  131.2 3.8 %collective-permute-done.19.refs_21_ = f32[192,128]{1,0:T(8,128)S(1)} collective-permute-done((f32[192,128]{1,0:T(8,128)}, f32[192,128]{1,0:T(8,128)S(1)}, u32[]{:S(2)}, u32[]{:S(2)}) %collective-permute-start.19) | collective-permute-done | bytes 98336 | tf_op jit(solution)/shard_map/ppermute | solution.py:338
  134.9 2.8 %collective-permute-start.22 = (f32[192,128]{1,0:T(8,128)S(1)}, f32[192,128]{1,0:T(8,128)S(1)}, u32[]{:S(2)}, u32[]{:S(2)}) collective-permute-start(f32[192,128]{1,0:T(8,128)S(1)} %bitcast.43), channel_id=1, source_target_pairs={{0,30},{1,31},{2,28},{3,29},{4,26},{5,27},{6,24},{7,25},{8,22},{9,... | collective-permute-start | bytes 294920 | tf_op jit(solution)/shard_map/ppermute | solution.py:338
  137.8 1.8 %collective-permute-start.23 = (f32[192,128]{1,0:T(8,128)S(1)}, f32[192,128]{1,0:T(8,128)S(1)}, u32[]{:S(2)}, u32[]{:S(2)}) collective-permute-start(f32[192,128]{1,0:T(8,128)S(1)} %bitcast.42), channel_id=1, source_target_pairs={{0,31},{1,30},{2,29},{3,28},{4,27},{5,26},{6,25},{7,24},{8,23},{9,... | collective-permute-start | bytes 294920 | tf_op jit(solution)/shard_map/ppermute | solution.py:338
  140.7 1.7 %mix.1 = (bf16[256,256]{1,0:T(8,128)(2,1)S(1)}, bf16[256,256]{1,0:T(8,128)(2,1)S(1)}, bf16[256,512]{1,0:T(8,128)(2,1)S(1)}, bf16[256,512]{1,0:T(8,128)(2,1)S(1)}) custom-call(s32[1]{0:T(128)} %bitcast.me_ref, s32[1,512]{1,0:T(1,128)S(1)} %copy-done.18, s32[1,512]{1,0:T(1,128)S(1)} %copy-done.17, f32[2,256,256]{2,1,0:T(8,128)S(1)} %copy-done.12, ...), custom_call_target="tpu_custom_call" | custom-call | tf_op jit(solution)/shard_map/mix/pallas_call | solution.py:238
  146.4 9.0 %solve.1 = f32[512,2048]{1,0:T(8,128)} custom-call(s32[1]{0:T(128)} %bitcast.me_ref, f32[2048,128]{1,0:T(8,128)} %bitcast.2.refs_0_, f32[2,192,128]{2,1,0:T(8,128)S(1)} %bitcast.32, f32[2,192,128]{2,1,0:T(8,128)S(1)} %collective-permute-done.refs_1_.refs_2_, f32[2,192,128]{2,1,0:T(8,128)S(1)} %collective-permute-done.1.refs_2_.refs_3_, ...), custom_call_target="tpu_custom_call" | custom-call | tf_op jit(solution)/shard_map/solve/pallas_call | solution.py:295
  (136 shorter events, 31.8 us)
Async XLA Ops:
  10.8 135.6 %all-to-all-start = ((f32[32,4,2,8,128]{4,3,2,1,0:T(8,128)}), f32[32,4,2,8,128]{4,3,2,1,0:T(8,128)}, u32[]{:S(2)}, u32[]{:S(2)}) async-start(f32[32,4,2,8,128]{4,3,2,1,0:T(8,128)} %whiten.2), calls=%async_computation | async-start | bytes 2097152 | tf_op jit(solution)/shard_map/all_to_all | solution.py:388
  33.9 7.1 %collective-permute-start = (f32[2,192,128]{2,1,0:T(8,128)S(1)}, f32[2,192,128]{2,1,0:T(8,128)S(1)}, u32[]{:S(2)}, u32[]{:S(2)}) collective-permute-start(f32[2,192,128]{2,1,0:T(8,128)S(1)} %bitcast.41), channel_id=1, source_target_pairs={{0,2},{1,3},{2,0},{3,1},{4,6},{5,7},{6,4},{7,5},{8,10},{9,11},{10,... | collective-permute-start | bytes 589832 | tf_op jit(solution)/shard_map/ppermute | solution.py:338
  34.3 8.5 %collective-permute-start.1 = (f32[2,192,128]{2,1,0:T(8,128)S(1)}, f32[2,192,128]{2,1,0:T(8,128)S(1)}, u32[]{:S(2)}, u32[]{:S(2)}) collective-permute-start(f32[2,192,128]{2,1,0:T(8,128)S(1)} %bitcast.40), channel_id=1, source_target_pairs={{0,4},{1,5},{2,6},{3,7},{4,0},{5,1},{6,2},{7,3},{8,12},{9,13},{10,... | collective-permute-start | bytes 589832 | tf_op jit(solution)/shard_map/ppermute | solution.py:338
  35.4 15.5 %collective-permute-start.2 = (f32[2,192,128]{2,1,0:T(8,128)S(1)}, f32[2,192,128]{2,1,0:T(8,128)S(1)}, u32[]{:S(2)}, u32[]{:S(2)}) collective-permute-start(f32[2,192,128]{2,1,0:T(8,128)S(1)} %bitcast.39), channel_id=1, source_target_pairs={{0,6},{1,7},{2,4},{3,5},{4,2},{5,3},{6,0},{7,1},{8,14},{9,15},{10,... | collective-permute-start | bytes 589832 | tf_op jit(solution)/shard_map/ppermute | solution.py:338
  36.6 14.3 %collective-permute-start.3 = (f32[2,192,128]{2,1,0:T(8,128)S(1)}, f32[2,192,128]{2,1,0:T(8,128)S(1)}, u32[]{:S(2)}, u32[]{:S(2)}) collective-permute-start(f32[2,192,128]{2,1,0:T(8,128)S(1)} %bitcast.38), channel_id=1, source_target_pairs={{0,8},{1,9},{2,10},{3,11},{4,12},{5,13},{6,14},{7,15},{8,0},{9,1},... | collective-permute-start | bytes 589832 | tf_op jit(solution)/shard_map/ppermute | solution.py:338
  36.9 14.0 %collective-permute-start.4 = (f32[2,192,128]{2,1,0:T(8,128)S(1)}, f32[2,192,128]{2,1,0:T(8,128)S(1)}, u32[]{:S(2)}, u32[]{:S(2)}) collective-permute-start(f32[2,192,128]{2,1,0:T(8,128)S(1)} %bitcast.37), channel_id=1, source_target_pairs={{0,10},{1,11},{2,8},{3,9},{4,14},{5,15},{6,12},{7,13},{8,2},{9,3},... | collective-permute-start | bytes 589832 | tf_op jit(solution)/shard_map/ppermute | solution.py:338
  41.0 10.7 %collective-permute-start.5 = (f32[2,192,128]{2,1,0:T(8,128)S(1)}, f32[2,192,128]{2,1,0:T(8,128)S(1)}, u32[]{:S(2)}, u32[]{:S(2)}) collective-permute-start(f32[2,192,128]{2,1,0:T(8,128)S(1)} %bitcast.36), channel_id=1, source_target_pairs={{0,12},{1,13},{2,14},{3,15},{4,8},{5,9},{6,10},{7,11},{8,4},{9,5},... | collective-permute-start | bytes 589832 | tf_op jit(solution)/shard_map/ppermute | solution.py:338
  42.7 13.4 %collective-permute-start.6 = (f32[2,192,128]{2,1,0:T(8,128)S(1)}, f32[2,192,128]{2,1,0:T(8,128)S(1)}, u32[]{:S(2)}, u32[]{:S(2)}) collective-permute-start(f32[2,192,128]{2,1,0:T(8,128)S(1)} %bitcast.35), channel_id=1, source_target_pairs={{0,14},{1,15},{2,12},{3,13},{4,10},{5,11},{6,8},{7,9},{8,6},{9,7},... | collective-permute-start | bytes 589832 | tf_op jit(solution)/shard_map/ppermute | solution.py:338
  56.2 90.2 %collective-permute-start.7 = (f32[1536,128]{1,0:T(8,128)S(1)}, f32[1536,128]{1,0:T(8,128)S(1)}, u32[]{:S(2)}, u32[]{:S(2)}) collective-permute-start(f32[1536,128]{1,0:T(8,128)S(1)} %bundle.1), channel_id=1, source_target_pairs={{0,1},{1,0},{2,3},{3,2},{4,5},{5,4},{6,7},{7,6},{8,9},{9,8},{10,11... | collective-permute-start | bytes 2359304 | tf_op jit(solution)/shard_map/ppermute | solution.py:338
  59.6 3.9 %collective-permute-start.24 = (f32[16,256]{1,0:T(8,128)}, f32[16,256]{1,0:T(8,128)}, u32[]{:S(2)}, u32[]{:S(2)}) collective-permute-start(f32[16,256]{1,0:T(8,128)} %slice_bitcast_fusion), channel_id=1, source_target_pairs={{0,16},{1,17},{2,18},{3,19},{4,20},{5,21},{6,22},{7,23},{8,24},{9,... | collective-permute-start | bytes 49160 | tf_op jit(solution)/shard_map/ppermute | solution.py:338
  62.0 23.5 %collective-permute-start.8 = (f32[192,128]{1,0:T(8,128)}, f32[192,128]{1,0:T(8,128)}, u32[]{:S(2)}, u32[]{:S(2)}) collective-permute-start(f32[192,128]{1,0:T(8,128)} %bitcast.11), channel_id=1, source_target_pairs={{0,16},{1,17},{2,18},{3,19},{4,20},{5,21},{6,22},{7,23},{8,24},{9,... | collective-permute-start | bytes 294920 | tf_op jit(solution)/shard_map/ppermute | solution.py:338
  64.2 4.4 %collective-permute-start.31 = (f32[16,256]{1,0:T(8,128)S(1)}, f32[16,256]{1,0:T(8,128)S(1)}, u32[]{:S(2)}, u32[]{:S(2)}) collective-permute-start(f32[16,256]{1,0:T(8,128)S(1)} %broadcast_select_fusion.refs_0_), channel_id=1, source_target_pairs={{0,14},{1,15},{2,12},{3,13},{4,10},{5,11},{6,8},{7,9},{8,6},{9,7},... | collective-permute-start | bytes 49160 | tf_op jit(solution)/shard_map/ppermute | solution.py:338
  65.9 3.8 %collective-permute-start.30 = (f32[16,256]{1,0:T(8,128)S(1)}, f32[16,256]{1,0:T(8,128)S(1)}, u32[]{:S(2)}, u32[]{:S(2)}) collective-permute-start(f32[16,256]{1,0:T(8,128)S(1)} %broadcast_select_fusion.refs_0_), channel_id=1, source_target_pairs={{0,12},{1,13},{2,14},{3,15},{4,8},{5,9},{6,10},{7,11},{8,4},{9,5},... | collective-permute-start | bytes 49160 | tf_op jit(solution)/shard_map/ppermute | solution.py:338
  67.5 3.5 %collective-permute-start.29 = (f32[16,256]{1,0:T(8,128)S(1)}, f32[16,256]{1,0:T(8,128)S(1)}, u32[]{:S(2)}, u32[]{:S(2)}) collective-permute-start(f32[16,256]{1,0:T(8,128)S(1)} %broadcast_select_fusion.refs_0_), channel_id=1, source_target_pairs={{0,10},{1,11},{2,8},{3,9},{4,14},{5,15},{6,12},{7,13},{8,2},{9,3},... | collective-permute-start | bytes 49160 | tf_op jit(solution)/shard_map/ppermute | solution.py:338
  68.6 9.7 %collective-permute-start.28 = (f32[16,256]{1,0:T(8,128)S(1)}, f32[16,256]{1,0:T(8,128)S(1)}, u32[]{:S(2)}, u32[]{:S(2)}) collective-permute-start(f32[16,256]{1,0:T(8,128)S(1)} %broadcast_select_fusion.refs_0_), channel_id=1, source_target_pairs={{0,8},{1,9},{2,10},{3,11},{4,12},{5,13},{6,14},{7,15},{8,0},{9,1},... | collective-permute-start | bytes 49160 | tf_op jit(solution)/shard_map/ppermute | solution.py:338
  69.6 9.1 %collective-permute-start.27 = (f32[16,256]{1,0:T(8,128)S(1)}, f32[16,256]{1,0:T(8,128)S(1)}, u32[]{:S(2)}, u32[]{:S(2)}) collective-permute-start(f32[16,256]{1,0:T(8,128)S(1)} %broadcast_select_fusion.refs_0_), channel_id=1, source_target_pairs={{0,6},{1,7},{2,4},{3,5},{4,2},{5,3},{6,0},{7,1},{8,14},{9,15},{10,... | collective-permute-start | bytes 49160 | tf_op jit(solution)/shard_map/ppermute | solution.py:338
  71.0 16.0 %collective-permute-start.9 = (f32[192,128]{1,0:T(8,128)}, f32[192,128]{1,0:T(8,128)S(1)}, u32[]{:S(2)}, u32[]{:S(2)}) collective-permute-start(f32[192,128]{1,0:T(8,128)} %bitcast.56), channel_id=1, source_target_pairs={{0,17},{1,16},{2,19},{3,18},{4,21},{5,20},{6,23},{7,22},{8,25},{9,... | collective-permute-start | bytes 294920 | tf_op jit(solution)/shard_map/ppermute | solution.py:338
  80.9 7.1 %collective-permute-start.10 = (f32[192,128]{1,0:T(8,128)}, f32[192,128]{1,0:T(8,128)S(1)}, u32[]{:S(2)}, u32[]{:S(2)}) collective-permute-start(f32[192,128]{1,0:T(8,128)} %bitcast.55), channel_id=1, source_target_pairs={{0,18},{1,19},{2,16},{3,17},{4,22},{5,23},{6,20},{7,21},{8,26},{9,... | collective-permute-start | bytes 294920 | tf_op jit(solution)/shard_map/ppermute | solution.py:338
  81.3 13.2 %collective-permute-start.11 = (f32[192,128]{1,0:T(8,128)}, f32[192,128]{1,0:T(8,128)S(1)}, u32[]{:S(2)}, u32[]{:S(2)}) collective-permute-start(f32[192,128]{1,0:T(8,128)} %bitcast.54), channel_id=1, source_target_pairs={{0,19},{1,18},{2,17},{3,16},{4,23},{5,22},{6,21},{7,20},{8,27},{9,... | collective-permute-start | bytes 294920 | tf_op jit(solution)/shard_map/ppermute | solution.py:338
  85.5 13.5 %collective-permute-start.12 = (f32[192,128]{1,0:T(8,128)}, f32[192,128]{1,0:T(8,128)S(1)}, u32[]{:S(2)}, u32[]{:S(2)}) collective-permute-start(f32[192,128]{1,0:T(8,128)} %bitcast.53), channel_id=1, source_target_pairs={{0,20},{1,21},{2,22},{3,23},{4,16},{5,17},{6,18},{7,19},{8,28},{9,... | collective-permute-start | bytes 294920 | tf_op jit(solution)/shard_map/ppermute | solution.py:338
  87.0 15.4 %collective-permute-start.13 = (f32[192,128]{1,0:T(8,128)}, f32[192,128]{1,0:T(8,128)S(1)}, u32[]{:S(2)}, u32[]{:S(2)}) collective-permute-start(f32[192,128]{1,0:T(8,128)} %bitcast.52), channel_id=1, source_target_pairs={{0,21},{1,20},{2,23},{3,22},{4,17},{5,16},{6,19},{7,18},{8,29},{9,... | collective-permute-start | bytes 294920 | tf_op jit(solution)/shard_map/ppermute | solution.py:338
  88.0 18.0 %collective-permute-start.14 = (f32[192,128]{1,0:T(8,128)}, f32[192,128]{1,0:T(8,128)S(1)}, u32[]{:S(2)}, u32[]{:S(2)}) collective-permute-start(f32[192,128]{1,0:T(8,128)} %bitcast.51), channel_id=1, source_target_pairs={{0,22},{1,23},{2,20},{3,21},{4,18},{5,19},{6,16},{7,17},{8,30},{9,... | collective-permute-start | bytes 294920 | tf_op jit(solution)/shard_map/ppermute | solution.py:338
  94.5 13.6 %collective-permute-start.15 = (f32[192,128]{1,0:T(8,128)}, f32[192,128]{1,0:T(8,128)S(1)}, u32[]{:S(2)}, u32[]{:S(2)}) collective-permute-start(f32[192,128]{1,0:T(8,128)} %bitcast.50), channel_id=1, source_target_pairs={{0,23},{1,22},{2,21},{3,20},{4,19},{5,18},{6,17},{7,16},{8,31},{9,... | collective-permute-start | bytes 294920 | tf_op jit(solution)/shard_map/ppermute | solution.py:338
  99.0 15.4 %collective-permute-start.16 = (f32[192,128]{1,0:T(8,128)}, f32[192,128]{1,0:T(8,128)S(1)}, u32[]{:S(2)}, u32[]{:S(2)}) collective-permute-start(f32[192,128]{1,0:T(8,128)} %bitcast.49), channel_id=1, source_target_pairs={{0,24},{1,25},{2,26},{3,27},{4,28},{5,29},{6,30},{7,31},{8,16},{9,... | collective-permute-start | bytes 294920 | tf_op jit(solution)/shard_map/ppermute | solution.py:338
  102.5 35.3 %collective-permute-start.32 = (f32[128,256]{1,0:T(8,128)S(1)}, f32[128,256]{1,0:T(8,128)S(1)}, u32[]{:S(2)}, u32[]{:S(2)}) collective-permute-start(f32[128,256]{1,0:T(8,128)S(1)} %stack.1), channel_id=1, source_target_pairs={{0,1},{1,0},{2,3},{3,2},{4,5},{5,4},{6,7},{7,6},{8,9},{9,8},{10,11... | collective-permute-start | bytes 393224 | tf_op jit(solution)/shard_map/ppermute | solution.py:338
  106.0 11.1 %collective-permute-start.17 = (f32[192,128]{1,0:T(8,128)}, f32[192,128]{1,0:T(8,128)S(1)}, u32[]{:S(2)}, u32[]{:S(2)}) collective-permute-start(f32[192,128]{1,0:T(8,128)} %bitcast.48), channel_id=1, source_target_pairs={{0,25},{1,24},{2,27},{3,26},{4,29},{5,28},{6,31},{7,30},{8,17},{9,... | collective-permute-start | bytes 294920 | tf_op jit(solution)/shard_map/ppermute | solution.py:338
  108.1 23.1 %collective-permute-start.18 = (f32[192,128]{1,0:T(8,128)}, f32[192,128]{1,0:T(8,128)S(1)}, u32[]{:S(2)}, u32[]{:S(2)}) collective-permute-start(f32[192,128]{1,0:T(8,128)} %bitcast.47), channel_id=1, source_target_pairs={{0,26},{1,27},{2,24},{3,25},{4,30},{5,31},{6,28},{7,29},{8,18},{9,... | collective-permute-start | bytes 294920 | tf_op jit(solution)/shard_map/ppermute | solution.py:338
  114.4 20.5 %collective-permute-start.19 = (f32[192,128]{1,0:T(8,128)}, f32[192,128]{1,0:T(8,128)S(1)}, u32[]{:S(2)}, u32[]{:S(2)}) collective-permute-start(f32[192,128]{1,0:T(8,128)} %bitcast.46), channel_id=1, source_target_pairs={{0,27},{1,26},{2,25},{3,24},{4,31},{5,30},{6,29},{7,28},{8,19},{9,... | collective-permute-start | bytes 294920 | tf_op jit(solution)/shard_map/ppermute | solution.py:338
  117.1 28.0 %collective-permute-start.20 = (f32[192,128]{1,0:T(8,128)S(1)}, f32[192,128]{1,0:T(8,128)S(1)}, u32[]{:S(2)}, u32[]{:S(2)}) collective-permute-start(f32[192,128]{1,0:T(8,128)S(1)} %bitcast.45), channel_id=1, source_target_pairs={{0,28},{1,29},{2,30},{3,31},{4,24},{5,25},{6,26},{7,27},{8,20},{9,... | collective-permute-start | bytes 294920 | tf_op jit(solution)/shard_map/ppermute | solution.py:338
  131.2 13.9 %collective-permute-start.21 = (f32[192,128]{1,0:T(8,128)S(1)}, f32[192,128]{1,0:T(8,128)S(1)}, u32[]{:S(2)}, u32[]{:S(2)}) collective-permute-start(f32[192,128]{1,0:T(8,128)S(1)} %bitcast.44), channel_id=1, source_target_pairs={{0,29},{1,28},{2,31},{3,30},{4,25},{5,24},{6,27},{7,26},{8,21},{9,... | collective-permute-start | bytes 294920 | tf_op jit(solution)/shard_map/ppermute | solution.py:338
  134.9 10.2 %collective-permute-start.22 = (f32[192,128]{1,0:T(8,128)S(1)}, f32[192,128]{1,0:T(8,128)S(1)}, u32[]{:S(2)}, u32[]{:S(2)}) collective-permute-start(f32[192,128]{1,0:T(8,128)S(1)} %bitcast.43), channel_id=1, source_target_pairs={{0,30},{1,31},{2,28},{3,29},{4,26},{5,27},{6,24},{7,25},{8,22},{9,... | collective-permute-start | bytes 294920 | tf_op jit(solution)/shard_map/ppermute | solution.py:338
  137.8 7.3 %collective-permute-start.23 = (f32[192,128]{1,0:T(8,128)S(1)}, f32[192,128]{1,0:T(8,128)S(1)}, u32[]{:S(2)}, u32[]{:S(2)}) collective-permute-start(f32[192,128]{1,0:T(8,128)S(1)} %bitcast.42), channel_id=1, source_target_pairs={{0,31},{1,30},{2,29},{3,28},{4,27},{5,26},{6,25},{7,24},{8,23},{9,... | collective-permute-start | bytes 294920 | tf_op jit(solution)/shard_map/ppermute | solution.py:338
  (48 other events, 674.9 us)

commit v4 on v2

--- a/solution.py
+++ b/solution.py
@@ -160,14 +160,15 @@
     return pl.BlockSpec(shape, lambda i, me: (0,) * len(shape), pipeline_mode=pl.Buffered(1))
 
 
-def here():
-    return pl.BlockSpec(memory_space=pltpu.VMEM)
+def parity(array, flip):
+    pick = (lambda i, me: (1 - me[0] % 2, 0, 0)) if flip else (lambda i, me: (me[0] % 2, 0, 0))
+    return pl.BlockSpec((None,) + array.shape[1:], pick, pipeline_mode=pl.Buffered(1))
 
 
 def bundle_kernel(me_ref, *refs):
-    size = refs[0].shape[1]
+    size = refs[0].shape[0]
     for j, ref in enumerate(refs[:-1]):
-        refs[-1][j * size:(j + 1) * size] = ref[1 - me_ref[0] % 2]
+        refs[-1][j * size:(j + 1) * size] = ref[...]
 
 
 def bundle(me, arrays):
@@ -176,9 +177,21 @@
     return pl.pallas_call(
         bundle_kernel,
         grid_spec=pltpu.PrefetchScalarGridSpec(
-            num_scalar_prefetch=1, grid=(1,), in_specs=[here() for a in arrays], out_specs=here()),
+            num_scalar_prefetch=1, grid=(1,), in_specs=[parity(a, True) for a in arrays], out_specs=whole(shape)),
         out_shape=jax.ShapeDtypeStruct(shape, jnp.float32),
         name="bundle",
+    )(me, *arrays)
+
+
+def stack(me, arrays):
+    rows, lanes = arrays[0].shape
+    shape = (len(arrays) * rows, lanes)
+    return pl.pallas_call(
+        bundle_kernel,
+        grid_spec=pltpu.PrefetchScalarGridSpec(
+            num_scalar_prefetch=1, grid=(1,), in_specs=[whole(a.shape) for a in arrays], out_specs=whole(shape)),
+        out_shape=jax.ShapeDtypeStruct(shape, jnp.float32),
+        name="stack",
     )(me, *arrays)
 
 
@@ -215,8 +228,8 @@
         functools.partial(mix_kernel, top=top, local=local),
         grid_spec=pltpu.PrefetchScalarGridSpec(
             num_scalar_prefetch=1, grid=(1,),
-            in_specs=[whole(spots.shape), whole(masks.shape), whole(inverses.shape)] + [here()] * (len(papers) + 1),
-            out_specs=[here()] * len(shapes),
+            in_specs=[whole(a.shape) for a in args],
+            out_specs=[whole(shape) for shape in shapes],
             scratch_shapes=[pltpu.VMEM((width, width), jnp.float32)]),
         out_shape=[jax.ShapeDtypeStruct(shape, jnp.bfloat16) for shape in shapes],
         name="mix",
@@ -240,10 +253,7 @@
                 for n, start, size in picks:
                     if start is None:
                         start = (left ^ block) * (size * stride)
-                    ref = w_refs[n]
-                    if len(ref.shape) == 3:
-                        ref = ref.at[me_ref[0] % 2]
-                    column.append(ref[pl.ds(start + at, size, stride=stride), :])
+                    column.append(w_refs[n][pl.ds(start + at, size, stride=stride), :])
                 columns.append(jnp.concatenate(column, axis=0))
         high, low = split(jnp.concatenate(columns, axis=1))
         held_ref[block, 0] = high
@@ -271,7 +281,7 @@
     near += [pair(1 + chips, 0, chips // 2 * rest)]
     far = [(0, None, half_rows)] + [pair(1 + k, 0, rest) for k in range(chips // 2, chips)]
     far += [pair(1 + chips, chips // 2 * rest, (early - chips // 2) * rest), pair(2 + chips, 0, late * rest)]
-    specs = [here()] * len(args)
+    specs = [parity(a, False) if a.ndim == 3 else whole(a.shape) for a in args]
     width = tables[0].shape[0]
     return pl.pallas_call(
         functools.partial(solve_kernel, rows=rows, parts=parts, per=per, near=tuple(near), far=tuple(far), top=top),
@@ -311,7 +321,7 @@
 
 
 HEAD = 4
-LATE = 3
+LATE = 2
 
 
 def exchange(x, offset):
@@ -379,7 +389,7 @@
         papers.append(exchange(mine, 2 * k))
     for k in near + far:
         got[k] = exchange(outs[k], 2 * k)
-    theirs = exchange(jnp.concatenate(papers, axis=0), 1)
+    theirs = exchange(stack(me, papers), 1)
     spots, masks = places(groups, local, early, late)
     tables = mix(me, spots, masks, block_inverses, papers, theirs, top, local)
     load = bundle(me, [got[k] for k in early])

time: 153 us -> 155 us (1.013)
    unnamed x62 -> x54, local copies, waits for them, and re-layouts: 4.18 us -> 4.06 us
  transfers between devices with their start and end apart: 27 -> 27, of which waited for: 14 -> 14; matrix products, arithmetic and copies ran while one was open for 0% -> 0% of each run, Pallas kernels for 13% -> 14%
where the time goes in v4:
time: 155 us; the launch traced here: 154 us
  waiting for transfers between devices  58.2 us (38%)
  starting transfers between devices  55.7 us (36%)
  Pallas kernels  36 us (23%)
  local copies, waits for them, and re-layouts  4.07 us (3%)
    ppermute x26, waiting for transfers between devices, exchange(): return lax.ppermute(x, 'dev', pairs)  58.2 us
    ppermute x26, starting transfers between devices, exchange(): return lax.ppermute(x, 'dev', pairs)  48.4 us
    pallas_call x2, Pallas kernels, whiten(): pl.pallas_call(functools.partial(whiten_kernel, rb=rb, groups=groups, out...  17.1 us
    pallas_call x1, Pallas kernels, solve(): pl.pallas_call(functools.partial(solve_kernel, rows=rows, parts=parts, pe...  9.63 us
    all_to_all x1, starting transfers between devices, per_device(): head = lax.all_to_all(head, 'dev', 0, 0, tiled=True)  7.32 us
    pallas_call x2, Pallas kernels, bundle(): pl.pallas_call(bundle_kernel, grid_spec=pltpu.PrefetchScalarGridSpec(num_...  4.2 us
    unnamed x54, local copies, waits for them, and re-layouts  4.06 us
    pallas_call x1, Pallas kernels, mix(): pl.pallas_call(functools.partial(mix_kernel, top=top, local=local), grid_...  3.64 us
  transfers between devices with their start and end apart: 27, of which 14 were waited for; matrix products, arithmetic and copies ran while one was open for 0% of the time, Pallas kernels for 14%

profile of v4, /device:TPU:0, one launch (start us, length us, event | category | flops | bytes accessed | tf_op | source)
XLA Modules:
  0.0 154.2 jit_solution(4162826640063349715)
XLA Ops:
  0.0 5.5 %whiten.2 = f32[32,4,2,8,128]{4,3,2,1,0:T(8,128)} custom-call(s32[1]{0:T(128)} %bitcast.me_ref, f32[16,256,256]{2,1,0:T(8,128)} %x_ref.3, f32[129,256]{1,0:T(8,128)} %bitcast.26, bf16[256,256]{1,0:T(8,128)(2,1)} %constant.18.clone.fh_ref, bf16[256,256]{1,0:T(8,128)(2,1)} %constant.19.clone.fl_ref, bf16[256,256]{1,0:T(8,128)(2,1)} %constant.20.clone.th_ref, ...), custom_call_target="tpu_custom_call" | custom-call | tf_op jit(solution)/shard_map/whiten/pallas_call | solution.py:123
  5.5 7.3 %all-to-all-start = ((f32[32,4,2,8,128]{4,3,2,1,0:T(8,128)}), f32[32,4,2,8,128]{4,3,2,1,0:T(8,128)S(1)}, u32[]{:S(2)}, u32[]{:S(2)}) async-start(f32[32,4,2,8,128]{4,3,2,1,0:T(8,128)} %whiten.2), calls=%async_computation | async-start | bytes 2097152 | tf_op jit(solution)/shard_map/all_to_all | solution.py:383
  12.8 11.6 %whiten.3 = (f32[2,12,2,8,128]{4,3,2,1,0:T(8,128)}, f32[2,12,2,8,128]{4,3,2,1,0:T(8,128)}, f32[2,12,2,8,128]{4,3,2,1,0:T(8,128)}, f32[2,12,2,8,128]{4,3,2,1,0:T(...) custom-call(s32[1]{0:T(128)} %bitcast.me_ref, ...), custom_call_target="tpu_custom_call" | custom-call | tf_op jit(solution)/shard_map/whiten/pallas_call | solution.py:123
  24.4 1.8 %collective-permute-start = (f32[2,192,128]{2,1,0:T(8,128)}, f32[2,192,128]{2,1,0:T(8,128)S(1)}, u32[]{:S(2)}, u32[]{:S(2)}) collective-permute-start(f32[2,192,128]{2,1,0:T(8,128)} %bitcast.42), channel_id=1, source_target_pairs={{0,2},{1,3},{2,0},{3,1},{4,6},{5,7},{6,4},{7,5},{8,10},{9,11},{10,... | collective-permute-start | bytes 589832 | tf_op jit(solution)/shard_map/ppermute | solution.py:329
  26.2 1.5 collective-permute-start.1
  28.0 1.8 %collective-permute-start.3 = (f32[2,192,128]{2,1,0:T(8,128)}, f32[2,192,128]{2,1,0:T(8,128)S(1)}, u32[]{:S(2)}, u32[]{:S(2)}) collective-permute-start(f32[2,192,128]{2,1,0:T(8,128)} %bitcast.39), channel_id=1, source_target_pairs={{0,8},{1,9},{2,10},{3,11},{4,12},{5,13},{6,14},{7,15},{8,0},{9,1},... | collective-permute-start | bytes 589832 | tf_op jit(solution)/shard_map/ppermute | solution.py:329
  29.7 1.5 collective-permute-start.4
  31.2 2.3 %collective-permute-done.refs_1_.refs_2_ = f32[2,192,128]{2,1,0:T(8,128)S(1)} collective-permute-done((f32[2,192,128]{2,1,0:T(8,128)}, f32[2,192,128]{2,1,0:T(8,128)S(1)}, u32[]{:S(2)}, u32[]{:S(2)}) %collective-permute-start) | collective-permute-done | bytes 196640 | tf_op jit(solution)/shard_map/ppermute | solution.py:329
  33.5 2.7 %collective-permute-start.5 = (f32[2,192,128]{2,1,0:T(8,128)}, f32[2,192,128]{2,1,0:T(8,128)S(1)}, u32[]{:S(2)}, u32[]{:S(2)}) collective-permute-start(f32[2,192,128]{2,1,0:T(8,128)} %bitcast.37), channel_id=1, source_target_pairs={{0,12},{1,13},{2,14},{3,15},{4,8},{5,9},{6,10},{7,11},{8,4},{9,5},... | collective-permute-start | bytes 589832 | tf_op jit(solution)/shard_map/ppermute | solution.py:329
  36.2 3.9 %collective-permute-done.1.refs_2_.refs_3_ = f32[2,192,128]{2,1,0:T(8,128)S(1)} collective-permute-done((f32[2,192,128]{2,1,0:T(8,128)}, f32[2,192,128]{2,1,0:T(8,128)S(1)}, u32[]{:S(2)}, u32[]{:S(2)}) %collective-permute-start.1) | collective-permute-done | bytes 196640 | tf_op jit(solution)/shard_map/ppermute | solution.py:329
  40.1 8.8 %collective-permute-start.7 = (f32[2,192,128]{2,1,0:T(8,128)}, f32[2,192,128]{2,1,0:T(8,128)S(1)}, u32[]{:S(2)}, u32[]{:S(2)}) collective-permute-start(f32[2,192,128]{2,1,0:T(8,128)} %bitcast.35), channel_id=1, source_target_pairs={{0,16},{1,17},{2,18},{3,19},{4,20},{5,21},{6,22},{7,23},{8,24},{9,... | collective-permute-start | bytes 589832 | tf_op jit(solution)/shard_map/ppermute | solution.py:329
  49.5 2.3 %collective-permute-start.9 = (f32[2,192,128]{2,1,0:T(8,128)}, f32[2,192,128]{2,1,0:T(8,128)S(1)}, u32[]{:S(2)}, u32[]{:S(2)}) collective-permute-start(f32[2,192,128]{2,1,0:T(8,128)} %bitcast.33), channel_id=1, source_target_pairs={{0,20},{1,21},{2,22},{3,23},{4,16},{5,17},{6,18},{7,19},{8,28},{9,... | collective-permute-start | bytes 589832 | tf_op jit(solution)/shard_map/ppermute | solution.py:329
  51.9 3.6 %collective-permute-start.10 = (f32[2,192,128]{2,1,0:T(8,128)}, f32[2,192,128]{2,1,0:T(8,128)S(1)}, u32[]{:S(2)}, u32[]{:S(2)}) collective-permute-start(f32[2,192,128]{2,1,0:T(8,128)} %bitcast.32), channel_id=1, source_target_pairs={{0,22},{1,23},{2,20},{3,21},{4,18},{5,19},{6,16},{7,17},{8,30},{9,... | collective-permute-start | bytes 589832 | tf_op jit(solution)/shard_map/ppermute | solution.py:329
  55.5 4.2 %collective-permute-done.6.refs_7_.refs_8_ = f32[2,192,128]{2,1,0:T(8,128)S(1)} collective-permute-done((f32[2,192,128]{2,1,0:T(8,128)}, f32[2,192,128]{2,1,0:T(8,128)S(1)}, u32[]{:S(2)}, u32[]{:S(2)}) %collective-permute-start.6) | collective-permute-done | bytes 196640 | tf_op jit(solution)/shard_map/ppermute | solution.py:329
  60.0 16.6 %collective-permute-done.7.refs_8_.refs_9_ = f32[2,192,128]{2,1,0:T(8,128)S(1)} collective-permute-done((f32[2,192,128]{2,1,0:T(8,128)}, f32[2,192,128]{2,1,0:T(8,128)S(1)}, u32[]{:S(2)}, u32[]{:S(2)}) %collective-permute-start.7) | collective-permute-done | bytes 196640 | tf_op jit(solution)/shard_map/ppermute | solution.py:329
  76.6 6.1 %collective-permute-done.8.refs_9_.refs_10_ = f32[2,192,128]{2,1,0:T(8,128)S(1)} collective-permute-done((f32[2,192,128]{2,1,0:T(8,128)}, f32[2,192,128]{2,1,0:T(8,128)S(1)}, u32[]{:S(2)}, u32[]{:S(2)}) %collective-permute-start.8) | collective-permute-done | bytes 196640 | tf_op jit(solution)/shard_map/ppermute | solution.py:329
  82.8 6.7 %collective-permute-done.9.refs_10_.refs_11_ = f32[2,192,128]{2,1,0:T(8,128)S(1)} collective-permute-done((f32[2,192,128]{2,1,0:T(8,128)}, f32[2,192,128]{2,1,0:T(8,128)S(1)}, u32[]{:S(2)}, u32[]{:S(2)}) %collective-permute-start.9) | collective-permute-done | bytes 196640 | tf_op jit(solution)/shard_map/ppermute | solution.py:329
  89.5 3.1 %collective-permute-done.10.refs_11_.refs_12_ = f32[2,192,128]{2,1,0:T(8,128)S(1)} collective-permute-done((f32[2,192,128]{2,1,0:T(8,128)}, f32[2,192,128]{2,1,0:T(8,128)S(1)}, u32[]{:S(2)}, u32[]{:S(2)}) %collective-permute-start.10) | collective-permute-done | bytes 196640 | tf_op jit(solution)/shard_map/ppermute | solution.py:329
  93.3 2.6 %bundle.2 = f32[2688,128]{1,0:T(8,128)} custom-call(s32[1]{0:T(128)} %bitcast.me_ref, f32[2,192,128]{2,1,0:T(8,128)} %bitcast.24, f32[2,192,128]{2,1,0:T(8,128)} %copy-done.2, f32[2,192,128]{2,1,0:T(8,128)} %copy-done.3, f32[2,192,128]{2,1,0:T(8,128)} %copy-done.4, f32[2,192,128]{2,1,0:T(8,128)} %copy-done.5, f32[2,192,128]{2,1,0:T(8,128)} %copy-done.6, ...), custom_call_target="tpu_custom_call" | custom-call | tf_op jit(solution)/shard_map/bundle/pallas_call | solution.py:177
  97.3 5.0 %collective-permute-start.14 = (f32[2,192,128]{2,1,0:T(8,128)}, f32[2,192,128]{2,1,0:T(8,128)S(1)}, u32[]{:S(2)}, u32[]{:S(2)}) collective-permute-start(f32[2,192,128]{2,1,0:T(8,128)} %bitcast.28), channel_id=1, source_target_pairs={{0,30},{1,31},{2,28},{3,29},{4,26},{5,27},{6,24},{7,25},{8,22},{9,... | collective-permute-start | bytes 589832 | tf_op jit(solution)/shard_map/ppermute | solution.py:329
  102.3 4.3 %collective-permute-start.17 = (f32[16,256]{1,0:T(8,128)S(1)}, f32[16,256]{1,0:T(8,128)S(1)}, u32[]{:S(2)}, u32[]{:S(2)}) collective-permute-start(f32[16,256]{1,0:T(8,128)S(1)} %slice_bitcast_fusion), channel_id=1, source_target_pairs={{0,16},{1,17},{2,18},{3,19},{4,20},{5,21},{6,22},{7,23},{8,24},{9,... | collective-permute-start | bytes 49160 | tf_op jit(solution)/shard_map/ppermute | solution.py:329
  106.6 5.7 %collective-permute-done.14.refs_1_.refs_16_ = f32[2,192,128]{2,1,0:T(8,128)S(1)} collective-permute-done((f32[2,192,128]{2,1,0:T(8,128)}, f32[2,192,128]{2,1,0:T(8,128)S(1)}, u32[]{:S(2)}, u32[]{:S(2)}) %collective-permute-start.14) | collective-permute-done | bytes 196640 | tf_op jit(solution)/shard_map/ppermute | solution.py:329
  112.9 1.6 %bundle.3 = f32[384,128]{1,0:T(8,128)} custom-call(s32[1]{0:T(128)} %bitcast.me_ref, f32[2,192,128]{2,1,0:T(8,128)} %copy-done.14, f32[2,192,128]{2,1,0:T(8,128)} %copy-done.15), custom_call_target="tpu_custom_call" | custom-call | tf_op jit(solution)/shard_map/bundle/pallas_call | solution.py:177
  114.6 5.6 %collective-permute-done.17 = f32[16,256]{1,0:T(8,128)S(1)} collective-permute-done((f32[16,256]{1,0:T(8,128)S(1)}, f32[16,256]{1,0:T(8,128)S(1)}, u32[]{:S(2)}, u32[]{:S(2)}) %collective-permute-start.17) | collective-permute-done | bytes 16416 | tf_op jit(solution)/shard_map/ppermute | solution.py:329
  120.2 4.5 %collective-permute-start.24 = (f32[16,256]{1,0:T(8,128)S(1)}, f32[16,256]{1,0:T(8,128)S(1)}, u32[]{:S(2)}, u32[]{:S(2)}) collective-permute-start(f32[16,256]{1,0:T(8,128)S(1)} %broadcast_select_fusion.refs_0_), channel_id=1, source_target_pairs={{0,14},{1,15},{2,12},{3,13},{4,10},{5,11},{6,8},{7,9},{8,6},{9,7},... | collective-permute-start | bytes 49160 | tf_op jit(solution)/shard_map/ppermute | solution.py:329
  124.7 2.9 %collective-permute-start.22 = (f32[16,256]{1,0:T(8,128)S(1)}, f32[16,256]{1,0:T(8,128)S(1)}, u32[]{:S(2)}, u32[]{:S(2)}) collective-permute-start(f32[16,256]{1,0:T(8,128)S(1)} %broadcast_select_fusion.refs_0_), channel_id=1, source_target_pairs={{0,10},{1,11},{2,8},{3,9},{4,14},{5,15},{6,12},{7,13},{8,2},{9,3},... | collective-permute-start | bytes 49160 | tf_op jit(solution)/shard_map/ppermute | solution.py:329
  127.6 1.7 %collective-permute-start.21 = (f32[16,256]{1,0:T(8,128)S(1)}, f32[16,256]{1,0:T(8,128)S(1)}, u32[]{:S(2)}, u32[]{:S(2)}) collective-permute-start(f32[16,256]{1,0:T(8,128)S(1)} %broadcast_select_fusion.refs_0_), channel_id=1, source_target_pairs={{0,8},{1,9},{2,10},{3,11},{4,12},{5,13},{6,14},{7,15},{8,0},{9,1},... | collective-permute-start | bytes 49160 | tf_op jit(solution)/shard_map/ppermute | solution.py:329
  131.4 1.5 collective-permute-start.18
  135.8 1.5 stack.1
  137.3 1.6 %collective-permute-done.25.refs_8_ = f32[128,256]{1,0:T(8,128)S(1)} collective-permute-done((f32[128,256]{1,0:T(8,128)}, f32[128,256]{1,0:T(8,128)S(1)}, u32[]{:S(2)}, u32[]{:S(2)}) %collective-permute-start.25) | collective-permute-done | bytes 131104 | tf_op jit(solution)/shard_map/ppermute | solution.py:329
  139.5 3.6 %mix.1 = (bf16[256,256]{1,0:T(8,128)(2,1)}, bf16[256,256]{1,0:T(8,128)(2,1)}, bf16[256,512]{1,0:T(8,128)(2,1)}, bf16[256,512]{1,0:T(8,128)(2,1)}) custom-call(s32[1]{0:T(128)} %bitcast.me_ref, s32[1,512]{1,0:T(1,128)} %constant.22.clone.spot_ref, s32[1,512]{1,0:T(1,128)} %constant.23.clone.mask_ref, f32[2,256,256]{2,1,0:T(8,128)} %inverse_ref.1, ...), custom_call_target="tpu_custom_call" | custom-call | tf_op jit(solution)/shard_map/mix/pallas_call | solution.py:227
  144.6 9.6 %solve.1 = f32[512,2048]{1,0:T(8,128)} custom-call(s32[1]{0:T(128)} %bitcast.me_ref, f32[2048,128]{1,0:T(8,128)} %bitcast.23, f32[2,192,128]{2,1,0:T(8,128)} %bitcast.25, f32[2,192,128]{2,1,0:T(8,128)} %copy-done.2, f32[2,192,128]{2,1,0:T(8,128)} %copy-done.3, f32[2,192,128]{2,1,0:T(8,128)} %copy-done.4, f32[2,192,128]{2,1,0:T(8,128)} %copy-done.5, ...), custom_call_target="tpu_custom_call" | custom-call | tf_op jit(solution)/shard_map/solve/pallas_call | solution.py:286
  (85 shorter events, 10.9 us)
Async XLA Ops:
  5.5 137.7 %all-to-all-start = ((f32[32,4,2,8,128]{4,3,2,1,0:T(8,128)}), f32[32,4,2,8,128]{4,3,2,1,0:T(8,128)S(1)}, u32[]{:S(2)}, u32[]{:S(2)}) async-start(f32[32,4,2,8,128]{4,3,2,1,0:T(8,128)} %whiten.2), calls=%async_computation | async-start | bytes 2097152 | tf_op jit(solution)/shard_map/all_to_all | solution.py:383
  12.8 89.5 %copy-start.26 = (f32[2,16,256]{2,1,0:T(8,128)S(1)}, f32[2,16,256]{2,1,0:T(8,128)}, u32[]{:S(2)}) copy-start(f32[2,16,256]{2,1,0:T(8,128)} %param.17) | copy-start | bytes 98308
  24.4 9.1 %collective-permute-start = (f32[2,192,128]{2,1,0:T(8,128)}, f32[2,192,128]{2,1,0:T(8,128)S(1)}, u32[]{:S(2)}, u32[]{:S(2)}) collective-permute-start(f32[2,192,128]{2,1,0:T(8,128)} %bitcast.42), channel_id=1, source_target_pairs={{0,2},{1,3},{2,0},{3,1},{4,6},{5,7},{6,4},{7,5},{8,10},{9,11},{10,... | collective-permute-start | bytes 589832 | tf_op jit(solution)/shard_map/ppermute | solution.py:329
  26.2 13.9 %collective-permute-start.1 = (f32[2,192,128]{2,1,0:T(8,128)}, f32[2,192,128]{2,1,0:T(8,128)S(1)}, u32[]{:S(2)}, u32[]{:S(2)}) collective-permute-start(f32[2,192,128]{2,1,0:T(8,128)} %bitcast.41), channel_id=1, source_target_pairs={{0,4},{1,5},{2,6},{3,7},{4,0},{5,1},{6,2},{7,3},{8,12},{9,13},{10,... | collective-permute-start | bytes 589832 | tf_op jit(solution)/shard_map/ppermute | solution.py:329
  27.7 12.4 %collective-permute-start.2 = (f32[2,192,128]{2,1,0:T(8,128)}, f32[2,192,128]{2,1,0:T(8,128)S(1)}, u32[]{:S(2)}, u32[]{:S(2)}) collective-permute-start(f32[2,192,128]{2,1,0:T(8,128)} %bitcast.40), channel_id=1, source_target_pairs={{0,6},{1,7},{2,4},{3,5},{4,2},{5,3},{6,0},{7,1},{8,14},{9,15},{10,... | collective-permute-start | bytes 589832 | tf_op jit(solution)/shard_map/ppermute | solution.py:329
  28.0 21.0 %collective-permute-start.3 = (f32[2,192,128]{2,1,0:T(8,128)}, f32[2,192,128]{2,1,0:T(8,128)S(1)}, u32[]{:S(2)}, u32[]{:S(2)}) collective-permute-start(f32[2,192,128]{2,1,0:T(8,128)} %bitcast.39), channel_id=1, source_target_pairs={{0,8},{1,9},{2,10},{3,11},{4,12},{5,13},{6,14},{7,15},{8,0},{9,1},... | collective-permute-start | bytes 589832 | tf_op jit(solution)/shard_map/ppermute | solution.py:329
  29.7 19.8 %collective-permute-start.4 = (f32[2,192,128]{2,1,0:T(8,128)}, f32[2,192,128]{2,1,0:T(8,128)S(1)}, u32[]{:S(2)}, u32[]{:S(2)}) collective-permute-start(f32[2,192,128]{2,1,0:T(8,128)} %bitcast.38), channel_id=1, source_target_pairs={{0,10},{1,11},{2,8},{3,9},{4,14},{5,15},{6,12},{7,13},{8,2},{9,3},... | collective-permute-start | bytes 589832 | tf_op jit(solution)/shard_map/ppermute | solution.py:329
  33.5 59.0 %copy-start.2 = (f32[2,192,128]{2,1,0:T(8,128)}, f32[2,192,128]{2,1,0:T(8,128)S(1)}, u32[]{:S(2)}) copy-start(f32[2,192,128]{2,1,0:T(8,128)S(1)} %collective-permute-done.refs_1_.refs_2_) | copy-start | bytes 589828
  33.5 18.3 %collective-permute-start.5 = (f32[2,192,128]{2,1,0:T(8,128)}, f32[2,192,128]{2,1,0:T(8,128)S(1)}, u32[]{:S(2)}, u32[]{:S(2)}) collective-permute-start(f32[2,192,128]{2,1,0:T(8,128)} %bitcast.37), channel_id=1, source_target_pairs={{0,12},{1,13},{2,14},{3,15},{4,8},{5,9},{6,10},{7,11},{8,4},{9,5},... | collective-permute-start | bytes 589832 | tf_op jit(solution)/shard_map/ppermute | solution.py:329
  40.1 52.4 %copy-start.3 = (f32[2,192,128]{2,1,0:T(8,128)}, f32[2,192,128]{2,1,0:T(8,128)S(1)}, u32[]{:S(2)}) copy-start(f32[2,192,128]{2,1,0:T(8,128)S(1)} %collective-permute-done.1.refs_2_.refs_3_) | copy-start | bytes 589828
  40.1 19.5 %collective-permute-start.6 = (f32[2,192,128]{2,1,0:T(8,128)}, f32[2,192,128]{2,1,0:T(8,128)S(1)}, u32[]{:S(2)}, u32[]{:S(2)}) collective-permute-start(f32[2,192,128]{2,1,0:T(8,128)} %bitcast.36), channel_id=1, source_target_pairs={{0,14},{1,15},{2,12},{3,13},{4,10},{5,11},{6,8},{7,9},{8,6},{9,7},... | collective-permute-start | bytes 589832 | tf_op jit(solution)/shard_map/ppermute | solution.py:329
  40.1 52.4 %copy-start.4 = (f32[2,192,128]{2,1,0:T(8,128)}, f32[2,192,128]{2,1,0:T(8,128)S(1)}, u32[]{:S(2)}) copy-start(f32[2,192,128]{2,1,0:T(8,128)S(1)} %collective-permute-done.2.refs_3_.refs_4_) | copy-start | bytes 589828
  40.1 36.5 %collective-permute-start.7 = (f32[2,192,128]{2,1,0:T(8,128)}, f32[2,192,128]{2,1,0:T(8,128)S(1)}, u32[]{:S(2)}, u32[]{:S(2)}) collective-permute-start(f32[2,192,128]{2,1,0:T(8,128)} %bitcast.35), channel_id=1, source_target_pairs={{0,16},{1,17},{2,18},{3,19},{4,20},{5,21},{6,22},{7,23},{8,24},{9,... | collective-permute-start | bytes 589832 | tf_op jit(solution)/shard_map/ppermute | solution.py:329
  49.0 43.6 %copy-start.5 = (f32[2,192,128]{2,1,0:T(8,128)}, f32[2,192,128]{2,1,0:T(8,128)S(1)}, u32[]{:S(2)}) copy-start(f32[2,192,128]{2,1,0:T(8,128)S(1)} %collective-permute-done.3.refs_4_.refs_5_) | copy-start | bytes 589828
  49.0 33.8 %collective-permute-start.8 = (f32[2,192,128]{2,1,0:T(8,128)}, f32[2,192,128]{2,1,0:T(8,128)S(1)}, u32[]{:S(2)}, u32[]{:S(2)}) collective-permute-start(f32[2,192,128]{2,1,0:T(8,128)} %bitcast.34), channel_id=1, source_target_pairs={{0,18},{1,19},{2,16},{3,17},{4,22},{5,23},{6,20},{7,21},{8,26},{9,... | collective-permute-start | bytes 589832 | tf_op jit(solution)/shard_map/ppermute | solution.py:329
  49.5 40.0 %collective-permute-start.9 = (f32[2,192,128]{2,1,0:T(8,128)}, f32[2,192,128]{2,1,0:T(8,128)S(1)}, u32[]{:S(2)}, u32[]{:S(2)}) collective-permute-start(f32[2,192,128]{2,1,0:T(8,128)} %bitcast.33), channel_id=1, source_target_pairs={{0,20},{1,21},{2,22},{3,23},{4,16},{5,17},{6,18},{7,19},{8,28},{9,... | collective-permute-start | bytes 589832 | tf_op jit(solution)/shard_map/ppermute | solution.py:329
  51.9 40.7 %collective-permute-start.10 = (f32[2,192,128]{2,1,0:T(8,128)}, f32[2,192,128]{2,1,0:T(8,128)S(1)}, u32[]{:S(2)}, u32[]{:S(2)}) collective-permute-start(f32[2,192,128]{2,1,0:T(8,128)} %bitcast.32), channel_id=1, source_target_pairs={{0,22},{1,23},{2,20},{3,21},{4,18},{5,19},{6,16},{7,17},{8,30},{9,... | collective-permute-start | bytes 589832 | tf_op jit(solution)/shard_map/ppermute | solution.py:329
  59.7 32.9 %collective-permute-start.11 = (f32[2,192,128]{2,1,0:T(8,128)}, f32[2,192,128]{2,1,0:T(8,128)S(1)}, u32[]{:S(2)}, u32[]{:S(2)}) collective-permute-start(f32[2,192,128]{2,1,0:T(8,128)} %bitcast.31), channel_id=1, source_target_pairs={{0,24},{1,25},{2,26},{3,27},{4,28},{5,29},{6,30},{7,31},{8,16},{9,... | collective-permute-start | bytes 589832 | tf_op jit(solution)/shard_map/ppermute | solution.py:329
  76.6 15.9 %collective-permute-start.12 = (f32[2,192,128]{2,1,0:T(8,128)}, f32[2,192,128]{2,1,0:T(8,128)}, u32[]{:S(2)}, u32[]{:S(2)}) collective-permute-start(f32[2,192,128]{2,1,0:T(8,128)} %bitcast.30), channel_id=1, source_target_pairs={{0,26},{1,27},{2,24},{3,25},{4,30},{5,31},{6,28},{7,29},{8,18},{9,... | collective-permute-start | bytes 589832 | tf_op jit(solution)/shard_map/ppermute | solution.py:329
  95.9 47.2 %collective-permute-start.15 = (f32[2688,128]{1,0:T(8,128)}, f32[2688,128]{1,0:T(8,128)S(1)}, u32[]{:S(2)}, u32[]{:S(2)}) collective-permute-start(f32[2688,128]{1,0:T(8,128)} %bundle.2), channel_id=1, source_target_pairs={{0,1},{1,0},{2,3},{3,2},{4,5},{5,4},{6,7},{7,6},{8,9},{9,8},{10,11... | collective-permute-start | bytes 4128776 | tf_op jit(solution)/shard_map/ppermute | solution.py:329
  95.9 10.7 %collective-permute-start.13 = (f32[2,192,128]{2,1,0:T(8,128)}, f32[2,192,128]{2,1,0:T(8,128)S(1)}, u32[]{:S(2)}, u32[]{:S(2)}) collective-permute-start(f32[2,192,128]{2,1,0:T(8,128)} %bitcast.29), channel_id=1, source_target_pairs={{0,28},{1,29},{2,30},{3,31},{4,24},{5,25},{6,26},{7,27},{8,20},{9,... | collective-permute-start | bytes 589832 | tf_op jit(solution)/shard_map/ppermute | solution.py:329
  97.3 15.0 %collective-permute-start.14 = (f32[2,192,128]{2,1,0:T(8,128)}, f32[2,192,128]{2,1,0:T(8,128)S(1)}, u32[]{:S(2)}, u32[]{:S(2)}) collective-permute-start(f32[2,192,128]{2,1,0:T(8,128)} %bitcast.28), channel_id=1, source_target_pairs={{0,30},{1,31},{2,28},{3,29},{4,26},{5,27},{6,24},{7,25},{8,22},{9,... | collective-permute-start | bytes 589832 | tf_op jit(solution)/shard_map/ppermute | solution.py:329
  102.3 17.9 %collective-permute-start.17 = (f32[16,256]{1,0:T(8,128)S(1)}, f32[16,256]{1,0:T(8,128)S(1)}, u32[]{:S(2)}, u32[]{:S(2)}) collective-permute-start(f32[16,256]{1,0:T(8,128)S(1)} %slice_bitcast_fusion), channel_id=1, source_target_pairs={{0,16},{1,17},{2,18},{3,19},{4,20},{5,21},{6,22},{7,23},{8,24},{9,... | collective-permute-start | bytes 49160 | tf_op jit(solution)/shard_map/ppermute | solution.py:329
  114.6 28.5 %collective-permute-start.16 = (f32[384,128]{1,0:T(8,128)}, f32[384,128]{1,0:T(8,128)S(1)}, u32[]{:S(2)}, u32[]{:S(2)}) collective-permute-start(f32[384,128]{1,0:T(8,128)} %bundle.3), channel_id=1, source_target_pairs={{0,1},{1,0},{2,3},{3,2},{4,5},{5,4},{6,7},{7,6},{8,9},{9,8},{10,11... | collective-permute-start | bytes 589832 | tf_op jit(solution)/shard_map/ppermute | solution.py:329
  120.2 7.4 %collective-permute-start.24 = (f32[16,256]{1,0:T(8,128)S(1)}, f32[16,256]{1,0:T(8,128)S(1)}, u32[]{:S(2)}, u32[]{:S(2)}) collective-permute-start(f32[16,256]{1,0:T(8,128)S(1)} %broadcast_select_fusion.refs_0_), channel_id=1, source_target_pairs={{0,14},{1,15},{2,12},{3,13},{4,10},{5,11},{6,8},{7,9},{8,6},{9,7},... | collective-permute-start | bytes 49160 | tf_op jit(solution)/shard_map/ppermute | solution.py:329
  124.7 4.6 %collective-permute-start.23 = (f32[16,256]{1,0:T(8,128)S(1)}, f32[16,256]{1,0:T(8,128)S(1)}, u32[]{:S(2)}, u32[]{:S(2)}) collective-permute-start(f32[16,256]{1,0:T(8,128)S(1)} %broadcast_select_fusion.refs_0_), channel_id=1, source_target_pairs={{0,12},{1,13},{2,14},{3,15},{4,8},{5,9},{6,10},{7,11},{8,4},{9,5},... | collective-permute-start | bytes 49160 | tf_op jit(solution)/shard_map/ppermute | solution.py:329
  124.7 6.1 %collective-permute-start.22 = (f32[16,256]{1,0:T(8,128)S(1)}, f32[16,256]{1,0:T(8,128)S(1)}, u32[]{:S(2)}, u32[]{:S(2)}) collective-permute-start(f32[16,256]{1,0:T(8,128)S(1)} %broadcast_select_fusion.refs_0_), channel_id=1, source_target_pairs={{0,10},{1,11},{2,8},{3,9},{4,14},{5,15},{6,12},{7,13},{8,2},{9,3},... | collective-permute-start | bytes 49160 | tf_op jit(solution)/shard_map/ppermute | solution.py:329
  127.6 3.7 %collective-permute-start.21 = (f32[16,256]{1,0:T(8,128)S(1)}, f32[16,256]{1,0:T(8,128)S(1)}, u32[]{:S(2)}, u32[]{:S(2)}) collective-permute-start(f32[16,256]{1,0:T(8,128)S(1)} %broadcast_select_fusion.refs_0_), channel_id=1, source_target_pairs={{0,8},{1,9},{2,10},{3,11},{4,12},{5,13},{6,14},{7,15},{8,0},{9,1},... | collective-permute-start | bytes 49160 | tf_op jit(solution)/shard_map/ppermute | solution.py:329
  129.3 4.6 %collective-permute-start.20 = (f32[16,256]{1,0:T(8,128)S(1)}, f32[16,256]{1,0:T(8,128)S(1)}, u32[]{:S(2)}, u32[]{:S(2)}) collective-permute-start(f32[16,256]{1,0:T(8,128)S(1)} %broadcast_select_fusion.refs_0_), channel_id=1, source_target_pairs={{0,6},{1,7},{2,4},{3,5},{4,2},{5,3},{6,0},{7,1},{8,14},{9,15},{10,... | collective-permute-start | bytes 49160 | tf_op jit(solution)/shard_map/ppermute | solution.py:329
  130.8 3.7 %collective-permute-start.19 = (f32[16,256]{1,0:T(8,128)S(1)}, f32[16,256]{1,0:T(8,128)S(1)}, u32[]{:S(2)}, u32[]{:S(2)}) collective-permute-start(f32[16,256]{1,0:T(8,128)S(1)} %broadcast_select_fusion.refs_0_), channel_id=1, source_target_pairs={{0,4},{1,5},{2,6},{3,7},{4,0},{5,1},{6,2},{7,3},{8,12},{9,13},{10,... | collective-permute-start | bytes 49160 | tf_op jit(solution)/shard_map/ppermute | solution.py:329
  131.4 3.7 %collective-permute-start.18 = (f32[16,256]{1,0:T(8,128)S(1)}, f32[16,256]{1,0:T(8,128)S(1)}, u32[]{:S(2)}, u32[]{:S(2)}) collective-permute-start(f32[16,256]{1,0:T(8,128)S(1)} %broadcast_select_fusion.refs_0_), channel_id=1, source_target_pairs={{0,2},{1,3},{2,0},{3,1},{4,6},{5,7},{6,4},{7,5},{8,10},{9,11},{10,... | collective-permute-start | bytes 49160 | tf_op jit(solution)/shard_map/ppermute | solution.py:329
  137.2 1.6 %collective-permute-start.25 = (f32[128,256]{1,0:T(8,128)}, f32[128,256]{1,0:T(8,128)S(1)}, u32[]{:S(2)}, u32[]{:S(2)}) collective-permute-start(f32[128,256]{1,0:T(8,128)} %stack.1), channel_id=1, source_target_pairs={{0,1},{1,0},{2,3},{3,2},{4,5},{5,4},{6,7},{7,6},{8,9},{9,8},{10,11... | collective-permute-start | bytes 393224 | tf_op jit(solution)/shard_map/ppermute | solution.py:329
  (22 other events, 196.2 us)

commit v5 on v3

--- a/solution.py
+++ b/solution.py
@@ -6,8 +6,6 @@
 from jax.experimental import pallas as pl
 from jax.experimental.pallas import tpu as pltpu
 from jax.sharding import PartitionSpec as P
-
-LIMIT = pltpu.CompilerParams(vmem_limit_bytes=32 << 20)
 
 
 def basis(length):
@@ -135,7 +133,6 @@
             scratch_shapes=scratch,
         ),
         out_shape=[jax.ShapeDtypeStruct((lead, count, parts, rows, LANES), jnp.float32) for lead in leads],
-        compiler_params=LIMIT,
         name="whiten",
     )(me, x, spectral_filter.T, fh, fl, fh.T, fl.T)
 
@@ -188,7 +185,6 @@
         grid_spec=pltpu.PrefetchScalarGridSpec(
             num_scalar_prefetch=1, grid=(1,), in_specs=[parity(a, True) for a in arrays], out_specs=whole(shape)),
         out_shape=jax.ShapeDtypeStruct(shape, jnp.float32),
-        compiler_params=LIMIT,
         name="bundle",
     )(me, *arrays)
 
@@ -201,7 +197,6 @@
         grid_spec=pltpu.PrefetchScalarGridSpec(
             num_scalar_prefetch=1, grid=(1,), in_specs=[whole(a.shape) for a in arrays], out_specs=whole(shape)),
         out_shape=jax.ShapeDtypeStruct(shape, jnp.float32),
-        compiler_params=LIMIT,
         name="stack",
     )(me, *arrays)
 
@@ -243,7 +238,6 @@
             out_specs=[whole(shape) for shape in shapes],
             scratch_shapes=[pltpu.VMEM((width, width), jnp.float32)]),
         out_shape=[jax.ShapeDtypeStruct(shape, jnp.bfloat16) for shape in shapes],
-        compiler_params=LIMIT,
         name="mix",
     )(me, *args)
 
@@ -299,7 +293,6 @@
             out_specs=pl.BlockSpec((2 * width, per * parts * LANES), lambda i, me: (0, i)),
             scratch_shapes=[pltpu.VMEM((2, 2, width, per * parts * LANES), jnp.bfloat16)]),
         out_shape=jax.ShapeDtypeStruct((2 * width, each * LANES), jnp.float32),
-        compiler_params=LIMIT,
         name="solve",
     )(me, *args)
 

time: 156 us -> 147 us (0.942)
  the two profiles are of different devices: /device:TPU:11 before, /device:TPU:9 now
where the time goes in v5:
time: 147 us
  starting transfers between devices  61.7 us (42%)
  waiting for transfers between devices  48.9 us (33%)
  Pallas kernels  33.9 us (23%)
  local copies, waits for them, and re-layouts  1.92 us (1%)
    ppermute x33, starting transfers between devices, exchange(): return lax.ppermute(x, 'dev', pairs)  55.4 us
    ppermute x33, waiting for transfers between devices, exchange(): return lax.ppermute(x, 'dev', pairs)  48.9 us
    pallas_call x2, Pallas kernels, whiten(): pl.pallas_call(functools.partial(whiten_kernel, rb=rb, groups=groups, out...  17.1 us
    pallas_call x1, Pallas kernels, solve(): pl.pallas_call(functools.partial(solve_kernel, rows=rows, parts=parts, pe...  9.42 us
    all_to_all x1, starting transfers between devices, per_device(): head = lax.all_to_all(head, 'dev', 0, 0, tiled=True)  6.32 us
    pallas_call x1, Pallas kernels, mix(): pl.pallas_call(functools.partial(mix_kernel, top=top, local=local), grid_...  3.62 us
  transfers between devices with their start and end apart: 34, of which 16 were waited for; matrix products, arithmetic and copies ran while one was open for 0% of the time, Pallas kernels for 13%

profile of v5, /device:TPU:9, one launch (start us, length us, event | category | flops | bytes accessed | tf_op | source)
XLA Modules:
  0.0 146.7 jit_solution(17928048161808678770)
XLA Ops:
  0.0 5.5 %whiten.2 = f32[32,4,2,8,128]{4,3,2,1,0:T(8,128)} custom-call(s32[1]{0:T(128)} %bitcast.me_ref, f32[16,256,256]{2,1,0:T(8,128)} %x_ref.3, f32[129,256]{1,0:T(8,128)} %bitcast.34, bf16[256,256]{1,0:T(8,128)(2,1)} %constant.18.clone.fh_ref, bf16[256,256]{1,0:T(8,128)(2,1)} %constant.19.clone.fl_ref, bf16[256,256]{1,0:T(8,128)(2,1)} %constant.20.clone.th_ref, ...), custom_call_target="tpu_custom_call" | custom-call | tf_op jit(solution)/shard_map/whiten/pallas_call | solution.py:125
  5.5 6.3 %all-to-all-start = ((f32[32,4,2,8,128]{4,3,2,1,0:T(8,128)}), f32[32,4,2,8,128]{4,3,2,1,0:T(8,128)S(1)}, u32[]{:S(2)}, u32[]{:S(2)}) async-start(f32[32,4,2,8,128]{4,3,2,1,0:T(8,128)} %whiten.2), calls=%async_computation | async-start | bytes 2097152 | tf_op jit(solution)/shard_map/all_to_all | solution.py:381
  11.8 11.7 %whiten.3 = (f32[2,12,2,8,128]{4,3,2,1,0:T(8,128)}, f32[2,12,2,8,128]{4,3,2,1,0:T(8,128)}, f32[2,12,2,8,128]{4,3,2,1,0:T(8,128)}, f32[2,12,2,8,128]{4,3,2,1,0:T(...) custom-call(s32[1]{0:T(128)} %bitcast.me_ref, ...), custom_call_target="tpu_custom_call" | custom-call | tf_op jit(solution)/shard_map/whiten/pallas_call | solution.py:125
  26.3 2.3 %collective-permute-start.4 = (f32[2,192,128]{2,1,0:T(8,128)}, f32[2,192,128]{2,1,0:T(8,128)S(1)}, u32[]{:S(2)}, u32[]{:S(2)}) collective-permute-start(f32[2,192,128]{2,1,0:T(8,128)} %bitcast.38), channel_id=1, source_target_pairs={{0,10},{1,11},{2,8},{3,9},{4,14},{5,15},{6,12},{7,13},{8,2},{9,3},... | collective-permute-start | bytes 589832 | tf_op jit(solution)/shard_map/ppermute | solution.py:331
  28.6 3.6 %collective-permute-done.refs_1_.refs_2_ = f32[2,192,128]{2,1,0:T(8,128)S(1)} collective-permute-done((f32[2,192,128]{2,1,0:T(8,128)}, f32[2,192,128]{2,1,0:T(8,128)S(1)}, u32[]{:S(2)}, u32[]{:S(2)}) %collective-permute-start) | collective-permute-done | bytes 196640 | tf_op jit(solution)/shard_map/ppermute | solution.py:331
  32.2 3.9 %collective-permute-done.1.refs_2_.refs_3_ = f32[2,192,128]{2,1,0:T(8,128)S(1)} collective-permute-done((f32[2,192,128]{2,1,0:T(8,128)}, f32[2,192,128]{2,1,0:T(8,128)S(1)}, u32[]{:S(2)}, u32[]{:S(2)}) %collective-permute-start.1) | collective-permute-done | bytes 196640 | tf_op jit(solution)/shard_map/ppermute | solution.py:331
  36.1 7.8 %collective-permute-done.2.refs_3_.refs_4_ = f32[2,192,128]{2,1,0:T(8,128)S(1)} collective-permute-done((f32[2,192,128]{2,1,0:T(8,128)}, f32[2,192,128]{2,1,0:T(8,128)S(1)}, u32[]{:S(2)}, u32[]{:S(2)}) %collective-permute-start.2) | collective-permute-done | bytes 196640 | tf_op jit(solution)/shard_map/ppermute | solution.py:331
  43.9 1.6 %collective-permute-done.5.refs_6_.refs_7_ = f32[2,192,128]{2,1,0:T(8,128)S(1)} collective-permute-done((f32[2,192,128]{2,1,0:T(8,128)}, f32[2,192,128]{2,1,0:T(8,128)S(1)}, u32[]{:S(2)}, u32[]{:S(2)}) %collective-permute-start.5) | collective-permute-done | bytes 196640 | tf_op jit(solution)/shard_map/ppermute | solution.py:331
  45.5 5.2 %collective-permute-done.6.refs_7_.refs_8_ = f32[2,192,128]{2,1,0:T(8,128)S(1)} collective-permute-done((f32[2,192,128]{2,1,0:T(8,128)}, f32[2,192,128]{2,1,0:T(8,128)S(1)}, u32[]{:S(2)}, u32[]{:S(2)}) %collective-permute-start.6) | collective-permute-done | bytes 196640 | tf_op jit(solution)/shard_map/ppermute | solution.py:331
  51.4 2.2 %bundle.1 = f32[1536,128]{1,0:T(8,128)} custom-call(s32[1]{0:T(128)} %bitcast.me_ref, f32[2,192,128]{2,1,0:T(8,128)} %bitcast.32, f32[2,192,128]{2,1,0:T(8,128)} %copy-done.2, f32[2,192,128]{2,1,0:T(8,128)} %copy-done.3, f32[2,192,128]{2,1,0:T(8,128)} %copy-done.4, f32[2,192,128]{2,1,0:T(8,128)} %copy-done.5, f32[2,192,128]{2,1,0:T(8,128)} %copy-done.6, ...), custom_call_target="tpu_custom_call" | custom-call | tf_op jit(solution)/shard_map/bundle/pallas_call | solution.py:183
  54.5 1.7 %collective-permute-start.24 = (f32[16,256]{1,0:T(8,128)S(1)}, f32[16,256]{1,0:T(8,128)S(1)}, u32[]{:S(2)}, u32[]{:S(2)}) collective-permute-start(f32[16,256]{1,0:T(8,128)S(1)} %slice_bitcast_fusion), channel_id=1, source_target_pairs={{0,16},{1,17},{2,18},{3,19},{4,20},{5,21},{6,22},{7,23},{8,24},{9,... | collective-permute-start | bytes 49160 | tf_op jit(solution)/shard_map/ppermute | solution.py:331
  60.5 2.1 %collective-permute-start.29 = (f32[16,256]{1,0:T(8,128)S(1)}, f32[16,256]{1,0:T(8,128)S(1)}, u32[]{:S(2)}, u32[]{:S(2)}) collective-permute-start(f32[16,256]{1,0:T(8,128)S(1)} %broadcast_select_fusion.refs_0_), channel_id=1, source_target_pairs={{0,10},{1,11},{2,8},{3,9},{4,14},{5,15},{6,12},{7,13},{8,2},{9,3},... | collective-permute-start | bytes 49160 | tf_op jit(solution)/shard_map/ppermute | solution.py:331
  62.6 3.0 %collective-permute-start.28 = (f32[16,256]{1,0:T(8,128)S(1)}, f32[16,256]{1,0:T(8,128)S(1)}, u32[]{:S(2)}, u32[]{:S(2)}) collective-permute-start(f32[16,256]{1,0:T(8,128)S(1)} %broadcast_select_fusion.refs_0_), channel_id=1, source_target_pairs={{0,8},{1,9},{2,10},{3,11},{4,12},{5,13},{6,14},{7,15},{8,0},{9,1},... | collective-permute-start | bytes 49160 | tf_op jit(solution)/shard_map/ppermute | solution.py:331
  65.6 3.7 %collective-permute-start.9 = (f32[192,128]{1,0:T(8,128)}, f32[192,128]{1,0:T(8,128)S(1)}, u32[]{:S(2)}, u32[]{:S(2)}) collective-permute-start(f32[192,128]{1,0:T(8,128)} %bitcast.57), channel_id=1, source_target_pairs={{0,17},{1,16},{2,19},{3,18},{4,21},{5,20},{6,23},{7,22},{8,25},{9,... | collective-permute-start | bytes 294920 | tf_op jit(solution)/shard_map/ppermute | solution.py:331
  70.8 1.5 %collective-permute-done.26.refs_2_ = f32[16,256]{1,0:T(8,128)S(1)} collective-permute-done((f32[16,256]{1,0:T(8,128)S(1)}, f32[16,256]{1,0:T(8,128)S(1)}, u32[]{:S(2)}, u32[]{:S(2)}) %collective-permute-start.26) | collective-permute-done | bytes 16416 | tf_op jit(solution)/shard_map/ppermute | solution.py:331
  72.3 1.7 %collective-permute-start.10 = (f32[192,128]{1,0:T(8,128)}, f32[192,128]{1,0:T(8,128)S(1)}, u32[]{:S(2)}, u32[]{:S(2)}) collective-permute-start(f32[192,128]{1,0:T(8,128)} %bitcast.56), channel_id=1, source_target_pairs={{0,18},{1,19},{2,16},{3,17},{4,22},{5,23},{6,20},{7,21},{8,26},{9,... | collective-permute-start | bytes 294920 | tf_op jit(solution)/shard_map/ppermute | solution.py:331
  74.0 2.2 %collective-permute-start.11 = (f32[192,128]{1,0:T(8,128)}, f32[192,128]{1,0:T(8,128)S(1)}, u32[]{:S(2)}, u32[]{:S(2)}) collective-permute-start(f32[192,128]{1,0:T(8,128)} %bitcast.55), channel_id=1, source_target_pairs={{0,19},{1,18},{2,17},{3,16},{4,23},{5,22},{6,21},{7,20},{8,27},{9,... | collective-permute-start | bytes 294920 | tf_op jit(solution)/shard_map/ppermute | solution.py:331
  76.3 2.5 %collective-permute-start.12 = (f32[192,128]{1,0:T(8,128)}, f32[192,128]{1,0:T(8,128)S(1)}, u32[]{:S(2)}, u32[]{:S(2)}) collective-permute-start(f32[192,128]{1,0:T(8,128)} %bitcast.54), channel_id=1, source_target_pairs={{0,20},{1,21},{2,22},{3,23},{4,16},{5,17},{6,18},{7,19},{8,28},{9,... | collective-permute-start | bytes 294920 | tf_op jit(solution)/shard_map/ppermute | solution.py:331
  79.4 5.1 %collective-permute-done.10.refs_12_ = f32[192,128]{1,0:T(8,128)S(1)} collective-permute-done((f32[192,128]{1,0:T(8,128)}, f32[192,128]{1,0:T(8,128)S(1)}, u32[]{:S(2)}, u32[]{:S(2)}) %collective-permute-start.10) | collective-permute-done | bytes 98336 | tf_op jit(solution)/shard_map/ppermute | solution.py:331
  84.5 2.1 %collective-permute-done.11.refs_13_ = f32[192,128]{1,0:T(8,128)S(1)} collective-permute-done((f32[192,128]{1,0:T(8,128)}, f32[192,128]{1,0:T(8,128)S(1)}, u32[]{:S(2)}, u32[]{:S(2)}) %collective-permute-start.11) | collective-permute-done | bytes 98336 | tf_op jit(solution)/shard_map/ppermute | solution.py:331
  86.6 3.7 %collective-permute-start.15 = (f32[192,128]{1,0:T(8,128)}, f32[192,128]{1,0:T(8,128)S(1)}, u32[]{:S(2)}, u32[]{:S(2)}) collective-permute-start(f32[192,128]{1,0:T(8,128)} %bitcast.51), channel_id=1, source_target_pairs={{0,23},{1,22},{2,21},{3,20},{4,19},{5,18},{6,17},{7,16},{8,31},{9,... | collective-permute-start | bytes 294920 | tf_op jit(solution)/shard_map/ppermute | solution.py:331
  91.5 1.5 %stack.1 = f32[128,256]{1,0:T(8,128)} custom-call(s32[1]{0:T(128)} %bitcast.me_ref, f32[16,256]{1,0:T(8,128)} %copy-done.9, f32[16,256]{1,0:T(8,128)} %copy-done.33, f32[16,256]{1,0:T(8,128)} %copy-done.32, f32[16,256]{1,0:T(8,128)} %copy-done.31, f32[16,256]{1,0:T(8,128)} %copy-done.30, f32[16,256]{1,0:T(8,128)} %copy-done.29, f32[16,256]{1,0:T(8,128)} %copy-done.28, ...), custom_call_target="tpu_custom_call" | custom-call | tf_op jit(solution)/shard_map/stack/pallas_call | solution.py:195
  93.0 4.3 %collective-permute-start.32 = (f32[128,256]{1,0:T(8,128)}, f32[128,256]{1,0:T(8,128)S(1)}, u32[]{:S(2)}, u32[]{:S(2)}) collective-permute-start(f32[128,256]{1,0:T(8,128)} %stack.1), channel_id=1, source_target_pairs={{0,1},{1,0},{2,3},{3,2},{4,5},{5,4},{6,7},{7,6},{8,9},{9,8},{10,11... | collective-permute-start | bytes 393224 | tf_op jit(solution)/shard_map/ppermute | solution.py:331
  98.0 2.1 %collective-permute-start.17 = (f32[192,128]{1,0:T(8,128)}, f32[192,128]{1,0:T(8,128)S(1)}, u32[]{:S(2)}, u32[]{:S(2)}) collective-permute-start(f32[192,128]{1,0:T(8,128)} %bitcast.49), channel_id=1, source_target_pairs={{0,25},{1,24},{2,27},{3,26},{4,29},{5,28},{6,31},{7,30},{8,17},{9,... | collective-permute-start | bytes 294920 | tf_op jit(solution)/shard_map/ppermute | solution.py:331
  102.5 2.1 %collective-permute-done.16.refs_18_ = f32[192,128]{1,0:T(8,128)S(1)} collective-permute-done((f32[192,128]{1,0:T(8,128)}, f32[192,128]{1,0:T(8,128)S(1)}, u32[]{:S(2)}, u32[]{:S(2)}) %collective-permute-start.16) | collective-permute-done | bytes 98336 | tf_op jit(solution)/shard_map/ppermute | solution.py:331
  104.6 2.5 %collective-permute-start.19 = (f32[192,128]{1,0:T(8,128)}, f32[192,128]{1,0:T(8,128)S(1)}, u32[]{:S(2)}, u32[]{:S(2)}) collective-permute-start(f32[192,128]{1,0:T(8,128)} %bitcast.47), channel_id=1, source_target_pairs={{0,27},{1,26},{2,25},{3,24},{4,31},{5,30},{6,29},{7,28},{8,19},{9,... | collective-permute-start | bytes 294920 | tf_op jit(solution)/shard_map/ppermute | solution.py:331
  107.1 8.9 %collective-permute-done.17.refs_19_ = f32[192,128]{1,0:T(8,128)S(1)} collective-permute-done((f32[192,128]{1,0:T(8,128)}, f32[192,128]{1,0:T(8,128)S(1)}, u32[]{:S(2)}, u32[]{:S(2)}) %collective-permute-start.17) | collective-permute-done | bytes 98336 | tf_op jit(solution)/shard_map/ppermute | solution.py:331
  117.9 8.8 %collective-permute-start.21 = (f32[192,128]{1,0:T(8,128)}, f32[192,128]{1,0:T(8,128)S(1)}, u32[]{:S(2)}, u32[]{:S(2)}) collective-permute-start(f32[192,128]{1,0:T(8,128)} %bitcast.45), channel_id=1, source_target_pairs={{0,29},{1,28},{2,31},{3,30},{4,25},{5,24},{6,27},{7,26},{8,21},{9,... | collective-permute-start | bytes 294920 | tf_op jit(solution)/shard_map/ppermute | solution.py:331
  128.8 1.3 collective-permute-start.23
  130.2 3.6 %mix.1 = (bf16[256,256]{1,0:T(8,128)(2,1)}, bf16[256,256]{1,0:T(8,128)(2,1)}, bf16[256,512]{1,0:T(8,128)(2,1)}, bf16[256,512]{1,0:T(8,128)(2,1)}) custom-call(s32[1]{0:T(128)} %bitcast.me_ref, s32[1,512]{1,0:T(1,128)} %constant.22.clone.spot_ref, s32[1,512]{1,0:T(1,128)} %constant.23.clone.mask_ref, f32[2,256,256]{2,1,0:T(8,128)} %inverse_ref.1, ...), custom_call_target="tpu_custom_call" | custom-call | tf_op jit(solution)/shard_map/mix/pallas_call | solution.py:233
  133.8 2.2 %collective-permute-done.23.refs_25_ = f32[192,128]{1,0:T(8,128)S(1)} collective-permute-done((f32[192,128]{1,0:T(8,128)}, f32[192,128]{1,0:T(8,128)S(1)}, u32[]{:S(2)}, u32[]{:S(2)}) %collective-permute-start.23) | collective-permute-done | bytes 98336 | tf_op jit(solution)/shard_map/ppermute | solution.py:331
  137.3 9.4 %solve.1 = f32[512,2048]{1,0:T(8,128)} custom-call(s32[1]{0:T(128)} %bitcast.me_ref, f32[2048,128]{1,0:T(8,128)} %bitcast.31, f32[2,192,128]{2,1,0:T(8,128)} %bitcast.33, f32[2,192,128]{2,1,0:T(8,128)} %copy-done.2, f32[2,192,128]{2,1,0:T(8,128)} %copy-done.3, f32[2,192,128]{2,1,0:T(8,128)} %copy-done.4, f32[2,192,128]{2,1,0:T(8,128)} %copy-done.5, ...), custom_call_target="tpu_custom_call" | custom-call | tf_op jit(solution)/shard_map/solve/pallas_call | solution.py:289
  (114 shorter events, 20.5 us)
Async XLA Ops:
  5.5 130.6 %all-to-all-start = ((f32[32,4,2,8,128]{4,3,2,1,0:T(8,128)}), f32[32,4,2,8,128]{4,3,2,1,0:T(8,128)S(1)}, u32[]{:S(2)}, u32[]{:S(2)}) async-start(f32[32,4,2,8,128]{4,3,2,1,0:T(8,128)} %whiten.2), calls=%async_computation | async-start | bytes 2097152 | tf_op jit(solution)/shard_map/all_to_all | solution.py:381
  23.5 8.7 %collective-permute-start = (f32[2,192,128]{2,1,0:T(8,128)}, f32[2,192,128]{2,1,0:T(8,128)S(1)}, u32[]{:S(2)}, u32[]{:S(2)}) collective-permute-start(f32[2,192,128]{2,1,0:T(8,128)} %bitcast.42), channel_id=1, source_target_pairs={{0,2},{1,3},{2,0},{3,1},{4,6},{5,7},{6,4},{7,5},{8,10},{9,11},{10,... | collective-permute-start | bytes 589832 | tf_op jit(solution)/shard_map/ppermute | solution.py:331
  24.7 11.4 %collective-permute-start.1 = (f32[2,192,128]{2,1,0:T(8,128)}, f32[2,192,128]{2,1,0:T(8,128)S(1)}, u32[]{:S(2)}, u32[]{:S(2)}) collective-permute-start(f32[2,192,128]{2,1,0:T(8,128)} %bitcast.41), channel_id=1, source_target_pairs={{0,4},{1,5},{2,6},{3,7},{4,0},{5,1},{6,2},{7,3},{8,12},{9,13},{10,... | collective-permute-start | bytes 589832 | tf_op jit(solution)/shard_map/ppermute | solution.py:331
  25.9 18.0 %collective-permute-start.2 = (f32[2,192,128]{2,1,0:T(8,128)}, f32[2,192,128]{2,1,0:T(8,128)S(1)}, u32[]{:S(2)}, u32[]{:S(2)}) collective-permute-start(f32[2,192,128]{2,1,0:T(8,128)} %bitcast.40), channel_id=1, source_target_pairs={{0,6},{1,7},{2,4},{3,5},{4,2},{5,3},{6,0},{7,1},{8,14},{9,15},{10,... | collective-permute-start | bytes 589832 | tf_op jit(solution)/shard_map/ppermute | solution.py:331
  26.2 17.7 %collective-permute-start.3 = (f32[2,192,128]{2,1,0:T(8,128)}, f32[2,192,128]{2,1,0:T(8,128)S(1)}, u32[]{:S(2)}, u32[]{:S(2)}) collective-permute-start(f32[2,192,128]{2,1,0:T(8,128)} %bitcast.39), channel_id=1, source_target_pairs={{0,8},{1,9},{2,10},{3,11},{4,12},{5,13},{6,14},{7,15},{8,0},{9,1},... | collective-permute-start | bytes 589832 | tf_op jit(solution)/shard_map/ppermute | solution.py:331
  26.3 17.6 %collective-permute-start.4 = (f32[2,192,128]{2,1,0:T(8,128)}, f32[2,192,128]{2,1,0:T(8,128)S(1)}, u32[]{:S(2)}, u32[]{:S(2)}) collective-permute-start(f32[2,192,128]{2,1,0:T(8,128)} %bitcast.38), channel_id=1, source_target_pairs={{0,10},{1,11},{2,8},{3,9},{4,14},{5,15},{6,12},{7,13},{8,2},{9,3},... | collective-permute-start | bytes 589832 | tf_op jit(solution)/shard_map/ppermute | solution.py:331
  32.2 13.3 %collective-permute-start.5 = (f32[2,192,128]{2,1,0:T(8,128)}, f32[2,192,128]{2,1,0:T(8,128)S(1)}, u32[]{:S(2)}, u32[]{:S(2)}) collective-permute-start(f32[2,192,128]{2,1,0:T(8,128)} %bitcast.37), channel_id=1, source_target_pairs={{0,12},{1,13},{2,14},{3,15},{4,8},{5,9},{6,10},{7,11},{8,4},{9,5},... | collective-permute-start | bytes 589832 | tf_op jit(solution)/shard_map/ppermute | solution.py:331
  36.1 14.6 %collective-permute-start.6 = (f32[2,192,128]{2,1,0:T(8,128)}, f32[2,192,128]{2,1,0:T(8,128)S(1)}, u32[]{:S(2)}, u32[]{:S(2)}) collective-permute-start(f32[2,192,128]{2,1,0:T(8,128)} %bitcast.36), channel_id=1, source_target_pairs={{0,14},{1,15},{2,12},{3,13},{4,10},{5,11},{6,8},{7,9},{8,6},{9,7},... | collective-permute-start | bytes 589832 | tf_op jit(solution)/shard_map/ppermute | solution.py:331
  53.6 82.4 %collective-permute-start.7 = (f32[1536,128]{1,0:T(8,128)}, f32[1536,128]{1,0:T(8,128)S(1)}, u32[]{:S(2)}, u32[]{:S(2)}) collective-permute-start(f32[1536,128]{1,0:T(8,128)} %bundle.1), channel_id=1, source_target_pairs={{0,1},{1,0},{2,3},{3,2},{4,5},{5,4},{6,7},{7,6},{8,9},{9,8},{10,11... | collective-permute-start | bytes 2359304 | tf_op jit(solution)/shard_map/ppermute | solution.py:331
  56.3 20.0 %collective-permute-start.8 = (f32[192,128]{1,0:T(8,128)}, f32[192,128]{1,0:T(8,128)S(1)}, u32[]{:S(2)}, u32[]{:S(2)}) collective-permute-start(f32[192,128]{1,0:T(8,128)} %bitcast.58), channel_id=1, source_target_pairs={{0,16},{1,17},{2,18},{3,19},{4,20},{5,21},{6,22},{7,23},{8,24},{9,... | collective-permute-start | bytes 294920 | tf_op jit(solution)/shard_map/ppermute | solution.py:331
  58.1 4.5 %collective-permute-start.31 = (f32[16,256]{1,0:T(8,128)S(1)}, f32[16,256]{1,0:T(8,128)S(1)}, u32[]{:S(2)}, u32[]{:S(2)}) collective-permute-start(f32[16,256]{1,0:T(8,128)S(1)} %broadcast_select_fusion.refs_0_), channel_id=1, source_target_pairs={{0,14},{1,15},{2,12},{3,13},{4,10},{5,11},{6,8},{7,9},{8,6},{9,7},... | collective-permute-start | bytes 49160 | tf_op jit(solution)/shard_map/ppermute | solution.py:331
  59.3 6.3 %collective-permute-start.30 = (f32[16,256]{1,0:T(8,128)S(1)}, f32[16,256]{1,0:T(8,128)S(1)}, u32[]{:S(2)}, u32[]{:S(2)}) collective-permute-start(f32[16,256]{1,0:T(8,128)S(1)} %broadcast_select_fusion.refs_0_), channel_id=1, source_target_pairs={{0,12},{1,13},{2,14},{3,15},{4,8},{5,9},{6,10},{7,11},{8,4},{9,5},... | collective-permute-start | bytes 49160 | tf_op jit(solution)/shard_map/ppermute | solution.py:331
  60.5 5.1 %collective-permute-start.29 = (f32[16,256]{1,0:T(8,128)S(1)}, f32[16,256]{1,0:T(8,128)S(1)}, u32[]{:S(2)}, u32[]{:S(2)}) collective-permute-start(f32[16,256]{1,0:T(8,128)S(1)} %broadcast_select_fusion.refs_0_), channel_id=1, source_target_pairs={{0,10},{1,11},{2,8},{3,9},{4,14},{5,15},{6,12},{7,13},{8,2},{9,3},... | collective-permute-start | bytes 49160 | tf_op jit(solution)/shard_map/ppermute | solution.py:331
  62.6 6.7 %collective-permute-start.28 = (f32[16,256]{1,0:T(8,128)S(1)}, f32[16,256]{1,0:T(8,128)S(1)}, u32[]{:S(2)}, u32[]{:S(2)}) collective-permute-start(f32[16,256]{1,0:T(8,128)S(1)} %broadcast_select_fusion.refs_0_), channel_id=1, source_target_pairs={{0,8},{1,9},{2,10},{3,11},{4,12},{5,13},{6,14},{7,15},{8,0},{9,1},... | collective-permute-start | bytes 49160 | tf_op jit(solution)/shard_map/ppermute | solution.py:331
  65.6 4.0 %collective-permute-start.27 = (f32[16,256]{1,0:T(8,128)S(1)}, f32[16,256]{1,0:T(8,128)S(1)}, u32[]{:S(2)}, u32[]{:S(2)}) collective-permute-start(f32[16,256]{1,0:T(8,128)S(1)} %broadcast_select_fusion.refs_0_), channel_id=1, source_target_pairs={{0,6},{1,7},{2,4},{3,5},{4,2},{5,3},{6,0},{7,1},{8,14},{9,15},{10,... | collective-permute-start | bytes 49160 | tf_op jit(solution)/shard_map/ppermute | solution.py:331
  65.6 13.2 %collective-permute-start.9 = (f32[192,128]{1,0:T(8,128)}, f32[192,128]{1,0:T(8,128)S(1)}, u32[]{:S(2)}, u32[]{:S(2)}) collective-permute-start(f32[192,128]{1,0:T(8,128)} %bitcast.57), channel_id=1, source_target_pairs={{0,17},{1,16},{2,19},{3,18},{4,21},{5,20},{6,23},{7,22},{8,25},{9,... | collective-permute-start | bytes 294920 | tf_op jit(solution)/shard_map/ppermute | solution.py:331
  69.6 4.4 %collective-permute-start.25 = (f32[16,256]{1,0:T(8,128)S(1)}, f32[16,256]{1,0:T(8,128)S(1)}, u32[]{:S(2)}, u32[]{:S(2)}) collective-permute-start(f32[16,256]{1,0:T(8,128)S(1)} %broadcast_select_fusion.refs_0_), channel_id=1, source_target_pairs={{0,2},{1,3},{2,0},{3,1},{4,6},{5,7},{6,4},{7,5},{8,10},{9,11},{10,... | collective-permute-start | bytes 49160 | tf_op jit(solution)/shard_map/ppermute | solution.py:331
  72.3 12.2 %collective-permute-start.10 = (f32[192,128]{1,0:T(8,128)}, f32[192,128]{1,0:T(8,128)S(1)}, u32[]{:S(2)}, u32[]{:S(2)}) collective-permute-start(f32[192,128]{1,0:T(8,128)} %bitcast.56), channel_id=1, source_target_pairs={{0,18},{1,19},{2,16},{3,17},{4,22},{5,23},{6,20},{7,21},{8,26},{9,... | collective-permute-start | bytes 294920 | tf_op jit(solution)/shard_map/ppermute | solution.py:331
  74.0 12.5 %collective-permute-start.11 = (f32[192,128]{1,0:T(8,128)}, f32[192,128]{1,0:T(8,128)S(1)}, u32[]{:S(2)}, u32[]{:S(2)}) collective-permute-start(f32[192,128]{1,0:T(8,128)} %bitcast.55), channel_id=1, source_target_pairs={{0,19},{1,18},{2,17},{3,16},{4,23},{5,22},{6,21},{7,20},{8,27},{9,... | collective-permute-start | bytes 294920 | tf_op jit(solution)/shard_map/ppermute | solution.py:331
  76.3 14.0 %collective-permute-start.12 = (f32[192,128]{1,0:T(8,128)}, f32[192,128]{1,0:T(8,128)S(1)}, u32[]{:S(2)}, u32[]{:S(2)}) collective-permute-start(f32[192,128]{1,0:T(8,128)} %bitcast.54), channel_id=1, source_target_pairs={{0,20},{1,21},{2,22},{3,23},{4,16},{5,17},{6,18},{7,19},{8,28},{9,... | collective-permute-start | bytes 294920 | tf_op jit(solution)/shard_map/ppermute | solution.py:331
  78.8 14.2 %collective-permute-start.13 = (f32[192,128]{1,0:T(8,128)}, f32[192,128]{1,0:T(8,128)S(1)}, u32[]{:S(2)}, u32[]{:S(2)}) collective-permute-start(f32[192,128]{1,0:T(8,128)} %bitcast.53), channel_id=1, source_target_pairs={{0,21},{1,20},{2,23},{3,22},{4,17},{5,16},{6,19},{7,18},{8,29},{9,... | collective-permute-start | bytes 294920 | tf_op jit(solution)/shard_map/ppermute | solution.py:331
  84.5 13.6 %collective-permute-start.14 = (f32[192,128]{1,0:T(8,128)}, f32[192,128]{1,0:T(8,128)S(1)}, u32[]{:S(2)}, u32[]{:S(2)}) collective-permute-start(f32[192,128]{1,0:T(8,128)} %bitcast.52), channel_id=1, source_target_pairs={{0,22},{1,23},{2,20},{3,21},{4,18},{5,19},{6,16},{7,17},{8,30},{9,... | collective-permute-start | bytes 294920 | tf_op jit(solution)/shard_map/ppermute | solution.py:331
  86.6 14.7 %collective-permute-start.15 = (f32[192,128]{1,0:T(8,128)}, f32[192,128]{1,0:T(8,128)S(1)}, u32[]{:S(2)}, u32[]{:S(2)}) collective-permute-start(f32[192,128]{1,0:T(8,128)} %bitcast.51), channel_id=1, source_target_pairs={{0,23},{1,22},{2,21},{3,20},{4,19},{5,18},{6,17},{7,16},{8,31},{9,... | collective-permute-start | bytes 294920 | tf_op jit(solution)/shard_map/ppermute | solution.py:331
  90.2 14.4 %collective-permute-start.16 = (f32[192,128]{1,0:T(8,128)}, f32[192,128]{1,0:T(8,128)S(1)}, u32[]{:S(2)}, u32[]{:S(2)}) collective-permute-start(f32[192,128]{1,0:T(8,128)} %bitcast.50), channel_id=1, source_target_pairs={{0,24},{1,25},{2,26},{3,27},{4,28},{5,29},{6,30},{7,31},{8,16},{9,... | collective-permute-start | bytes 294920 | tf_op jit(solution)/shard_map/ppermute | solution.py:331
  93.0 35.8 %collective-permute-start.32 = (f32[128,256]{1,0:T(8,128)}, f32[128,256]{1,0:T(8,128)S(1)}, u32[]{:S(2)}, u32[]{:S(2)}) collective-permute-start(f32[128,256]{1,0:T(8,128)} %stack.1), channel_id=1, source_target_pairs={{0,1},{1,0},{2,3},{3,2},{4,5},{5,4},{6,7},{7,6},{8,9},{9,8},{10,11... | collective-permute-start | bytes 393224 | tf_op jit(solution)/shard_map/ppermute | solution.py:331
  98.0 17.9 %collective-permute-start.17 = (f32[192,128]{1,0:T(8,128)}, f32[192,128]{1,0:T(8,128)S(1)}, u32[]{:S(2)}, u32[]{:S(2)}) collective-permute-start(f32[192,128]{1,0:T(8,128)} %bitcast.49), channel_id=1, source_target_pairs={{0,25},{1,24},{2,27},{3,26},{4,29},{5,28},{6,31},{7,30},{8,17},{9,... | collective-permute-start | bytes 294920 | tf_op jit(solution)/shard_map/ppermute | solution.py:331
  101.3 16.6 %collective-permute-start.18 = (f32[192,128]{1,0:T(8,128)}, f32[192,128]{1,0:T(8,128)S(1)}, u32[]{:S(2)}, u32[]{:S(2)}) collective-permute-start(f32[192,128]{1,0:T(8,128)} %bitcast.48), channel_id=1, source_target_pairs={{0,26},{1,27},{2,24},{3,25},{4,30},{5,31},{6,28},{7,29},{8,18},{9,... | collective-permute-start | bytes 294920 | tf_op jit(solution)/shard_map/ppermute | solution.py:331
  104.6 23.0 %collective-permute-start.19 = (f32[192,128]{1,0:T(8,128)}, f32[192,128]{1,0:T(8,128)S(1)}, u32[]{:S(2)}, u32[]{:S(2)}) collective-permute-start(f32[192,128]{1,0:T(8,128)} %bitcast.47), channel_id=1, source_target_pairs={{0,27},{1,26},{2,25},{3,24},{4,31},{5,30},{6,29},{7,28},{8,19},{9,... | collective-permute-start | bytes 294920 | tf_op jit(solution)/shard_map/ppermute | solution.py:331
  116.0 17.8 %collective-permute-start.20 = (f32[192,128]{1,0:T(8,128)}, f32[192,128]{1,0:T(8,128)S(1)}, u32[]{:S(2)}, u32[]{:S(2)}) collective-permute-start(f32[192,128]{1,0:T(8,128)} %bitcast.46), channel_id=1, source_target_pairs={{0,28},{1,29},{2,30},{3,31},{4,24},{5,25},{6,26},{7,27},{8,20},{9,... | collective-permute-start | bytes 294920 | tf_op jit(solution)/shard_map/ppermute | solution.py:331
  117.9 15.9 %collective-permute-start.21 = (f32[192,128]{1,0:T(8,128)}, f32[192,128]{1,0:T(8,128)S(1)}, u32[]{:S(2)}, u32[]{:S(2)}) collective-permute-start(f32[192,128]{1,0:T(8,128)} %bitcast.45), channel_id=1, source_target_pairs={{0,29},{1,28},{2,31},{3,30},{4,25},{5,24},{6,27},{7,26},{8,21},{9,... | collective-permute-start | bytes 294920 | tf_op jit(solution)/shard_map/ppermute | solution.py:331
  127.7 6.1 %collective-permute-start.22 = (f32[192,128]{1,0:T(8,128)}, f32[192,128]{1,0:T(8,128)S(1)}, u32[]{:S(2)}, u32[]{:S(2)}) collective-permute-start(f32[192,128]{1,0:T(8,128)} %bitcast.44), channel_id=1, source_target_pairs={{0,30},{1,31},{2,28},{3,29},{4,26},{5,27},{6,24},{7,25},{8,22},{9,... | collective-permute-start | bytes 294920 | tf_op jit(solution)/shard_map/ppermute | solution.py:331
  128.8 7.2 %collective-permute-start.23 = (f32[192,128]{1,0:T(8,128)}, f32[192,128]{1,0:T(8,128)S(1)}, u32[]{:S(2)}, u32[]{:S(2)}) collective-permute-start(f32[192,128]{1,0:T(8,128)} %bitcast.43), channel_id=1, source_target_pairs={{0,31},{1,30},{2,29},{3,28},{4,27},{5,26},{6,25},{7,24},{8,23},{9,... | collective-permute-start | bytes 294920 | tf_op jit(solution)/shard_map/ppermute | solution.py:331
  (37 other events, 778.8 us)

commit v6 on v5

--- a/solution.py
+++ b/solution.py
@@ -201,9 +201,9 @@
     )(me, *arrays)
 
 
-def mix_kernel(me_ref, spot_ref, mask_ref, inverse_ref, *refs, top, local):
-    papers, theirs_ref = refs[:-6], refs[-6]
-    th_ref, tl_ref, bh_ref, bl_ref, panel_ref = refs[-5:]
+def mix_kernel(me_ref, *refs, top, local, stages):
+    orders, (inverse_ref, *papers, theirs_ref) = refs[:2 * stages], refs[2 * stages:-2 * stages - 1]
+    o_refs, panel_ref = refs[-2 * stages - 1:-1], refs[-1]
     me = me_ref[0]
     for k, ref in enumerate(papers):
         for c in range(2):
@@ -212,26 +212,27 @@
     exact = functools.partial(jnp.dot, precision=lax.Precision.HIGHEST, preferred_element_type=jnp.float32)
     first, second = inverse_ref[0], inverse_ref[1]
     below = -exact(second, exact(panel_ref[...], first))
-    width = first.shape[0]
     table = jnp.concatenate([
         jnp.concatenate([first, jnp.zeros_like(first)], axis=1),
         jnp.concatenate([below, second], axis=1)], axis=0)
-    run = spot_ref[...] ^ ((me * local) & mask_ref[...])
-    order = lax.broadcasted_iota(jnp.int32, table.shape, 0) == jnp.broadcast_to(run, table.shape)
-    order = order.astype(jnp.float32).astype(jnp.bfloat16)
-    left = me < top
-    for piece, t_ref, b_ref in zip(split(table), (th_ref, tl_ref), (bh_ref, bl_ref)):
-        moved = mm(piece, order)
-        b_ref[...] = moved[width:].astype(jnp.bfloat16)
-        t_ref[...] = jnp.where(left, moved[:width, :width], moved[:width, width:]).astype(jnp.bfloat16)
-
-
-def mix(me, spots, masks, inverses, papers, theirs, top, local):
+    pieces = split(table)
+    for n in range(stages):
+        spot_ref, mask_ref = orders[2 * n:2 * n + 2]
+        run = spot_ref[...] ^ ((me * local) & mask_ref[...])
+        shape = (table.shape[0], run.shape[1])
+        order = lax.broadcasted_iota(jnp.int32, shape, 0) == jnp.broadcast_to(run, shape)
+        order = order.astype(jnp.float32).astype(jnp.bfloat16)
+        for piece, o_ref in zip(pieces, o_refs[2 * n:2 * n + 2]):
+            o_ref[...] = mm(piece, order).astype(jnp.bfloat16)
+
+
+def mix(me, orders, inverses, papers, theirs, top, local):
     width = inverses.shape[1]
-    shapes = [(width, width)] * 2 + [(width, 2 * width)] * 2
-    args = [spots, masks, inverses, *papers, theirs]
-    return pl.pallas_call(
-        functools.partial(mix_kernel, top=top, local=local),
+    flat = [table for order in orders for table in order]
+    args = [*flat, inverses, *papers, theirs]
+    shapes = [(2 * width, table.shape[1]) for table in flat]
+    return pl.pallas_call(
+        functools.partial(mix_kernel, top=top, local=local, stages=len(orders)),
         grid_spec=pltpu.PrefetchScalarGridSpec(
             num_scalar_prefetch=1, grid=(1,),
             in_specs=[whole(a.shape) for a in args],
@@ -242,57 +243,39 @@
     )(me, *args)
 
 
-def solve_kernel(me_ref, *refs, rows, parts, per, near, far, top):
-    count = len(refs) - 6
-    w_refs = refs[:count]
-    th_ref, tl_ref, bh_ref, bl_ref, o_ref, held_ref = refs[count:]
-    stride = rows * parts
-    width = th_ref.shape[0]
-    left = me_ref[0] // top
-    for block, picks in enumerate((near, far)):
-        columns = []
-        for g in range(per):
-            i = pl.program_id(0) * per + g
-            for p in range(parts):
-                at = p * rows + i
-                column = []
-                for n, start, size in picks:
-                    if start is None:
-                        start = (left ^ block) * (size * stride)
-                    column.append(w_refs[n][pl.ds(start + at, size, stride=stride), :])
-                columns.append(jnp.concatenate(column, axis=0))
-        high, low = split(jnp.concatenate(columns, axis=1))
-        held_ref[block, 0] = high
-        held_ref[block, 1] = low
-    th, tl = th_ref[...], tl_ref[...]
-    o_ref[:width] = mm(th, held_ref[left, 0]) + mm(th, held_ref[left, 1]) + mm(tl, held_ref[left, 0])
-    out = None
-    for block in range(2):
-        bh = bh_ref[:, block * width:(block + 1) * width]
-        bl = bl_ref[:, block * width:(block + 1) * width]
-        part = mm(bh, held_ref[block, 0]) + mm(bh, held_ref[block, 1]) + mm(bl, held_ref[block, 0])
-        out = part if out is None else out + part
-    o_ref[width:] = out
-
-
-def solve(me, head, got, load, direct, rest, tables, rows, parts, top):
+def solve_kernel(me_ref, *refs, rows, parts, per, sizes, acc):
+    n = len(sizes)
+    mh_ref, ml_ref = refs[n:n + 2]
+    o_ref = refs[-1]
+    columns = []
+    for g in range(per):
+        i = pl.program_id(0) * per + g
+        for p in range(parts):
+            column = [ref[pl.ds(p * rows + i, k, stride=rows * parts), :] for ref, k in zip(refs, sizes)]
+            columns.append(jnp.concatenate(column, axis=0))
+    wh, wl = split(jnp.concatenate(columns, axis=1))
+    mh, ml = mh_ref[...], ml_ref[...]
+    out = mm(mh, wh) + mm(mh, wl) + mm(ml, wh)
+    o_ref[...] = out + refs[n + 2][...] if acc else out
+
+
+def solve(me, pieces, tables, rows, parts, acc=None):
     each = rows * parts
-    per = 2 if rows % 2 == 0 else 1
-    args = [*outside([head]), *got, load, *outside([*direct, *tables])]
+    per = max(d for d in (4, 2, 1) if rows % d == 0)
+    width = tables[0].shape[0]
+    sizes = [a.shape[-2] // each for a in pieces]
+    args = [*pieces, *outside(tables)]
     specs = [parity(a, False) if a.ndim == 3 else whole(a.shape) for a in args]
-    pair = lambda n, size: (n, 0, size)
-    half_rows = head.shape[0] // each // 2
-    near = [(0, None, half_rows)] + [pair(1 + k, rest) for k in range(len(got))]
-    near += [pair(1 + len(got), len(got) * rest)]
-    far = [(0, None, half_rows)] + [pair(2 + len(got) + k, rest) for k in range(len(direct))]
-    width = tables[0].shape[0]
-    return pl.pallas_call(
-        functools.partial(solve_kernel, rows=rows, parts=parts, per=per, near=tuple(near), far=tuple(far), top=top),
-        grid_spec=pltpu.PrefetchScalarGridSpec(
-            num_scalar_prefetch=1, grid=(rows // per,), in_specs=specs,
-            out_specs=pl.BlockSpec((2 * width, per * parts * LANES), lambda i, me: (0, i)),
-            scratch_shapes=[pltpu.VMEM((2, 2, width, per * parts * LANES), jnp.bfloat16)]),
-        out_shape=jax.ShapeDtypeStruct((2 * width, each * LANES), jnp.float32),
+    tile = pl.BlockSpec((width, per * parts * LANES), lambda i, me: (0, i))
+    if acc is not None:
+        args.append(acc)
+        specs.append(tile)
+    return pl.pallas_call(
+        functools.partial(solve_kernel, rows=rows, parts=parts, per=per, sizes=tuple(sizes), acc=acc is not None),
+        grid_spec=pltpu.PrefetchScalarGridSpec(
+            num_scalar_prefetch=1, grid=(rows // per,), in_specs=specs, out_specs=tile),
+        out_shape=jax.ShapeDtypeStruct((width, each * LANES), jnp.float32),
+        input_output_aliases={} if acc is None else {len(args): 0},
         name="solve",
     )(me, *args)
 
@@ -324,6 +307,7 @@
 
 
 HEAD = 4
+SOON = 8
 
 
 def exchange(x, offset):
@@ -351,16 +335,11 @@
 def places(groups, local):
     top = groups // 2
     rest = range(HEAD, local)
-    ways = list(range(0, top, 2)) + list(range(1, top, 2)) + list(range(top, groups))
-    spots, masks = [], []
-    for far in range(2):
-        for source in range(top):
-            spots += [(source + far * top) * local + r for r in range(HEAD)]
-            masks += [top * local] * HEAD
-        for way in ways[far * top : (far + 1) * top]:
-            spots += [way * local + r for r in rest]
-            masks += [-1] * len(rest)
-    return np.array([spots], np.int32), np.array([masks], np.int32)
+    head = [(source * local + r, 0) for source in range(groups) for r in range(HEAD)]
+    ways = lambda picks: [(way * local + r, -1) for way in picks for r in rest]
+    soon = head + ways(range(0, top, 2)) + ways(range(top, top + SOON))
+    last = ways(range(1, top, 2)) + ways(range(top + SOON, groups))
+    return [np.array(stage, np.int32).T.reshape(2, 1, -1) for stage in (soon, last)]
 
 
 def per_device(runs_field, spectral_filter, block_inverses, factor_panels):
@@ -390,10 +369,11 @@
     for way in range(top, groups):
         direct.append(exchange(outs[way - chips // 2].reshape(-1, LANES), way))
     theirs = exchange(stack(me, papers), 1)
-    tables = mix(me, *places(groups, local), block_inverses, papers, theirs, top, local)
+    tables = mix(me, places(groups, local), block_inverses, papers, theirs, top, local)
     load = bundle(me, got)
     load = exchange(load, 1)
-    return solve(me, head.reshape(-1, LANES), got, load, direct, rest, tables, rows, parts, top)
+    out = solve(me, outside([head.reshape(-1, LANES), *got, *direct[:SOON]]), tables[:2], rows, parts)
+    return solve(me, [load, *outside(direct[SOON:])], tables[2:], rows, parts, out)
 
 
 def solution(mesh):

time: 147 us -> 148 us (level)
  the two profiles are of different devices: /device:TPU:9 before, /device:TPU:0 now
where the time goes in v6:
time: 148 us; the launch traced here: 147 us
  starting transfers between devices  64.8 us (44%)
  waiting for transfers between devices  40.8 us (28%)
  Pallas kernels  37.7 us (25%)
  local copies, waits for them, and re-layouts  3.24 us (2%)
    ppermute x33, starting transfers between devices, exchange(): return lax.ppermute(x, 'dev', pairs)  57.3 us
    ppermute x33, waiting for transfers between devices, exchange(): return lax.ppermute(x, 'dev', pairs)  40.8 us
    pallas_call x2, Pallas kernels, whiten(): pl.pallas_call(functools.partial(whiten_kernel, rb=rb, groups=groups, out...  17.1 us
    pallas_call x2, Pallas kernels, solve(): pl.pallas_call(functools.partial(solve_kernel, rows=rows, parts=parts, pe...  13 us
    all_to_all x1, starting transfers between devices, per_device(): head = lax.all_to_all(head, 'dev', 0, 0, tiled=True)  7.51 us
    pallas_call x1, Pallas kernels, mix(): pl.pallas_call(functools.partial(mix_kernel, top=top, local=local, stages...  3.89 us
  transfers between devices with their start and end apart: 34, of which 19 were waited for; matrix products, arithmetic and copies ran while one was open for 0% of the time, Pallas kernels for 18%

profile of v6, /device:TPU:0, one launch (start us, length us, event | category | flops | bytes accessed | tf_op | source)
XLA Modules:
  0.0 147.0 jit_solution(13226155968225056105)
XLA Ops:
  0.0 5.4 %whiten.3 = f32[32,4,2,8,128]{4,3,2,1,0:T(8,128)} custom-call(s32[1]{0:T(128)} %bitcast.me_ref, f32[16,256,256]{2,1,0:T(8,128)} %x_ref.3, f32[129,256]{1,0:T(8,128)} %bitcast.34, bf16[256,256]{1,0:T(8,128)(2,1)} %constant.22.clone.fh_ref, bf16[256,256]{1,0:T(8,128)(2,1)} %constant.23.clone.fl_ref, bf16[256,256]{1,0:T(8,128)(2,1)} %constant.24.clone.th_ref, ...), custom_call_target="tpu_custom_call" | custom-call | tf_op jit(solution)/shard_map/whiten/pallas_call | solution.py:125
  5.5 7.5 %all-to-all-start = ((f32[32,4,2,8,128]{4,3,2,1,0:T(8,128)}), f32[32,4,2,8,128]{4,3,2,1,0:T(8,128)S(1)}, u32[]{:S(2)}, u32[]{:S(2)}) async-start(f32[32,4,2,8,128]{4,3,2,1,0:T(8,128)} %whiten.3), calls=%async_computation | async-start | bytes 2097152 | tf_op jit(solution)/shard_map/all_to_all | solution.py:360
  13.0 11.7 %whiten.2 = (f32[2,12,2,8,128]{4,3,2,1,0:T(8,128)}, f32[2,12,2,8,128]{4,3,2,1,0:T(8,128)}, f32[2,12,2,8,128]{4,3,2,1,0:T(8,128)}, f32[2,12,2,8,128]{4,3,2,1,0:T(...) custom-call(s32[1]{0:T(128)} %bitcast.me_ref, ...), custom_call_target="tpu_custom_call" | custom-call | tf_op jit(solution)/shard_map/whiten/pallas_call | solution.py:125
  24.7 1.7 %collective-permute-start = (f32[2,192,128]{2,1,0:T(8,128)}, f32[2,192,128]{2,1,0:T(8,128)S(1)}, u32[]{:S(2)}, u32[]{:S(2)}) collective-permute-start(f32[2,192,128]{2,1,0:T(8,128)} %bitcast.42), channel_id=1, source_target_pairs={{0,2},{1,3},{2,0},{3,1},{4,6},{5,7},{6,4},{7,5},{8,10},{9,11},{10,... | collective-permute-start | bytes 589832 | tf_op jit(solution)/shard_map/ppermute | solution.py:315
  28.2 1.6 %collective-permute-start.3 = (f32[2,192,128]{2,1,0:T(8,128)}, f32[2,192,128]{2,1,0:T(8,128)S(1)}, u32[]{:S(2)}, u32[]{:S(2)}) collective-permute-start(f32[2,192,128]{2,1,0:T(8,128)} %bitcast.39), channel_id=1, source_target_pairs={{0,8},{1,9},{2,10},{3,11},{4,12},{5,13},{6,14},{7,15},{8,0},{9,1},... | collective-permute-start | bytes 589832 | tf_op jit(solution)/shard_map/ppermute | solution.py:315
  31.3 2.4 %collective-permute-done.refs_1_.refs_2_ = f32[2,192,128]{2,1,0:T(8,128)S(1)} collective-permute-done((f32[2,192,128]{2,1,0:T(8,128)}, f32[2,192,128]{2,1,0:T(8,128)S(1)}, u32[]{:S(2)}, u32[]{:S(2)}) %collective-permute-start) | collective-permute-done | bytes 196640 | tf_op jit(solution)/shard_map/ppermute | solution.py:315
  33.7 2.6 %collective-permute-start.5 = (f32[2,192,128]{2,1,0:T(8,128)}, f32[2,192,128]{2,1,0:T(8,128)S(1)}, u32[]{:S(2)}, u32[]{:S(2)}) collective-permute-start(f32[2,192,128]{2,1,0:T(8,128)} %bitcast.37), channel_id=1, source_target_pairs={{0,12},{1,13},{2,14},{3,15},{4,8},{5,9},{6,10},{7,11},{8,4},{9,5},... | collective-permute-start | bytes 589832 | tf_op jit(solution)/shard_map/ppermute | solution.py:315
  36.3 3.9 %collective-permute-done.1.refs_2_.refs_3_ = f32[2,192,128]{2,1,0:T(8,128)S(1)} collective-permute-done((f32[2,192,128]{2,1,0:T(8,128)}, f32[2,192,128]{2,1,0:T(8,128)S(1)}, u32[]{:S(2)}, u32[]{:S(2)}) %collective-permute-start.1) | collective-permute-done | bytes 196640 | tf_op jit(solution)/shard_map/ppermute | solution.py:315
  40.2 4.6 %collective-permute-done.4.refs_5_.refs_6_ = f32[2,192,128]{2,1,0:T(8,128)S(1)} collective-permute-done((f32[2,192,128]{2,1,0:T(8,128)}, f32[2,192,128]{2,1,0:T(8,128)S(1)}, u32[]{:S(2)}, u32[]{:S(2)}) %collective-permute-start.4) | collective-permute-done | bytes 196640 | tf_op jit(solution)/shard_map/ppermute | solution.py:315
  44.8 4.3 %collective-permute-done.5.refs_6_.refs_7_ = f32[2,192,128]{2,1,0:T(8,128)S(1)} collective-permute-done((f32[2,192,128]{2,1,0:T(8,128)}, f32[2,192,128]{2,1,0:T(8,128)S(1)}, u32[]{:S(2)}, u32[]{:S(2)}) %collective-permute-start.5) | collective-permute-done | bytes 196640 | tf_op jit(solution)/shard_map/ppermute | solution.py:315
  49.2 4.3 %collective-permute-done.6.refs_7_.refs_8_ = f32[2,192,128]{2,1,0:T(8,128)S(1)} collective-permute-done((f32[2,192,128]{2,1,0:T(8,128)}, f32[2,192,128]{2,1,0:T(8,128)S(1)}, u32[]{:S(2)}, u32[]{:S(2)}) %collective-permute-start.6) | collective-permute-done | bytes 196640 | tf_op jit(solution)/shard_map/ppermute | solution.py:315
  54.1 2.1 %bundle.1 = f32[1536,128]{1,0:T(8,128)} custom-call(s32[1]{0:T(128)} %bitcast.me_ref, f32[2,192,128]{2,1,0:T(8,128)} %bitcast.32, f32[2,192,128]{2,1,0:T(8,128)} %copy-done.1, f32[2,192,128]{2,1,0:T(8,128)} %copy-done.2, f32[2,192,128]{2,1,0:T(8,128)} %copy-done.3, f32[2,192,128]{2,1,0:T(8,128)} %copy-done.4, f32[2,192,128]{2,1,0:T(8,128)} %copy-done.5, ...), custom_call_target="tpu_custom_call" | custom-call | tf_op jit(solution)/shard_map/bundle/pallas_call | solution.py:183
  56.3 2.0 %collective-permute-start.16 = (f32[16,256]{1,0:T(8,128)S(1)}, f32[16,256]{1,0:T(8,128)S(1)}, u32[]{:S(2)}, u32[]{:S(2)}) collective-permute-start(f32[16,256]{1,0:T(8,128)S(1)} %slice_bitcast_fusion), channel_id=1, source_target_pairs={{0,16},{1,17},{2,18},{3,19},{4,20},{5,21},{6,22},{7,23},{8,24},{9,... | collective-permute-start | bytes 49160 | tf_op jit(solution)/shard_map/ppermute | solution.py:315
  59.3 1.9 %collective-permute-done.16 = f32[16,256]{1,0:T(8,128)S(1)} collective-permute-done((f32[16,256]{1,0:T(8,128)S(1)}, f32[16,256]{1,0:T(8,128)S(1)}, u32[]{:S(2)}, u32[]{:S(2)}) %collective-permute-start.16) | collective-permute-done | bytes 16416 | tf_op jit(solution)/shard_map/ppermute | solution.py:315
  62.0 2.1 %collective-permute-start.22 = (f32[16,256]{1,0:T(8,128)S(1)}, f32[16,256]{1,0:T(8,128)S(1)}, u32[]{:S(2)}, u32[]{:S(2)}) collective-permute-start(f32[16,256]{1,0:T(8,128)S(1)} %broadcast_select_fusion.refs_0_.refs_5_), channel_id=1, source_target_pairs={{0,12},{1,13},{2,14},{3,15},{4,8},{5,9},{6,10},{7,11},{8,4},{9,5},... | collective-permute-start | bytes 49160 | tf_op jit(solution)/shard_map/ppermute | solution.py:315
  69.0 1.5 %collective-permute-done.20.refs_4_.refs_9_ = f32[16,256]{1,0:T(8,128)S(1)} collective-permute-done((f32[16,256]{1,0:T(8,128)S(1)}, f32[16,256]{1,0:T(8,128)S(1)}, u32[]{:S(2)}, u32[]{:S(2)}) %collective-permute-start.20) | collective-permute-done | bytes 16416 | tf_op jit(solution)/shard_map/ppermute | solution.py:315
  72.7 1.6 %collective-permute-done.18.refs_2_.refs_7_ = f32[16,256]{1,0:T(8,128)S(1)} collective-permute-done((f32[16,256]{1,0:T(8,128)S(1)}, f32[16,256]{1,0:T(8,128)S(1)}, u32[]{:S(2)}, u32[]{:S(2)}) %collective-permute-start.18) | collective-permute-done | bytes 16416 | tf_op jit(solution)/shard_map/ppermute | solution.py:315
  74.3 2.8 %collective-permute-start.10 = (f32[192,128]{1,0:T(8,128)}, f32[192,128]{1,0:T(8,128)S(1)}, u32[]{:S(2)}, u32[]{:S(2)}) collective-permute-start(f32[192,128]{1,0:T(8,128)} %bitcast.56), channel_id=1, source_target_pairs={{0,26},{1,27},{2,24},{3,25},{4,30},{5,31},{6,28},{7,29},{8,18},{9,... | collective-permute-start | bytes 294920 | tf_op jit(solution)/shard_map/ppermute | solution.py:315
  78.6 2.8 %collective-permute-start.26 = (f32[192,128]{1,0:T(8,128)}, f32[192,128]{1,0:T(8,128)S(1)}, u32[]{:S(2)}, u32[]{:S(2)}) collective-permute-start(f32[192,128]{1,0:T(8,128)} %bitcast.53), channel_id=1, source_target_pairs={{0,17},{1,16},{2,19},{3,18},{4,21},{5,20},{6,23},{7,22},{8,25},{9,... | collective-permute-start | bytes 294920 | tf_op jit(solution)/shard_map/ppermute | solution.py:315
  82.3 9.1 %collective-permute-start.27 = (f32[192,128]{1,0:T(8,128)}, f32[192,128]{1,0:T(8,128)S(1)}, u32[]{:S(2)}, u32[]{:S(2)}) collective-permute-start(f32[192,128]{1,0:T(8,128)} %bitcast.52), channel_id=1, source_target_pairs={{0,18},{1,19},{2,16},{3,17},{4,22},{5,23},{6,20},{7,21},{8,26},{9,... | collective-permute-start | bytes 294920 | tf_op jit(solution)/shard_map/ppermute | solution.py:315
  91.4 1.5 %collective-permute-start.28 = (f32[192,128]{1,0:T(8,128)}, f32[192,128]{1,0:T(8,128)S(1)}, u32[]{:S(2)}, u32[]{:S(2)}) collective-permute-start(f32[192,128]{1,0:T(8,128)} %bitcast.51), channel_id=1, source_target_pairs={{0,19},{1,18},{2,17},{3,16},{4,23},{5,22},{6,21},{7,20},{8,27},{9,... | collective-permute-start | bytes 294920 | tf_op jit(solution)/shard_map/ppermute | solution.py:315
  95.9 5.2 %collective-permute-start.24 = (f32[128,256]{1,0:T(8,128)}, f32[128,256]{1,0:T(8,128)S(1)}, u32[]{:S(2)}, u32[]{:S(2)}) collective-permute-start(f32[128,256]{1,0:T(8,128)} %stack.1), channel_id=1, source_target_pairs={{0,1},{1,0},{2,3},{3,2},{4,5},{5,4},{6,7},{7,6},{8,9},{9,8},{10,11... | collective-permute-start | bytes 393224 | tf_op jit(solution)/shard_map/ppermute | solution.py:315
  101.1 2.1 %collective-permute-done.27.refs_11_ = f32[192,128]{1,0:T(8,128)S(1)} collective-permute-done((f32[192,128]{1,0:T(8,128)}, f32[192,128]{1,0:T(8,128)S(1)}, u32[]{:S(2)}, u32[]{:S(2)}) %collective-permute-start.27) | collective-permute-done | bytes 98336 | tf_op jit(solution)/shard_map/ppermute | solution.py:315
  103.2 2.2 %collective-permute-done.28.refs_12_ = f32[192,128]{1,0:T(8,128)S(1)} collective-permute-done((f32[192,128]{1,0:T(8,128)}, f32[192,128]{1,0:T(8,128)S(1)}, u32[]{:S(2)}, u32[]{:S(2)}) %collective-permute-start.28) | collective-permute-done | bytes 98336 | tf_op jit(solution)/shard_map/ppermute | solution.py:315
  106.6 2.8 %collective-permute-done.29.refs_13_ = f32[192,128]{1,0:T(8,128)S(1)} collective-permute-done((f32[192,128]{1,0:T(8,128)}, f32[192,128]{1,0:T(8,128)S(1)}, u32[]{:S(2)}, u32[]{:S(2)}) %collective-permute-start.29) | collective-permute-done | bytes 98336 | tf_op jit(solution)/shard_map/ppermute | solution.py:315
  109.5 4.2 %collective-permute-done.30.refs_14_ = f32[192,128]{1,0:T(8,128)S(1)} collective-permute-done((f32[192,128]{1,0:T(8,128)}, f32[192,128]{1,0:T(8,128)S(1)}, u32[]{:S(2)}, u32[]{:S(2)}) %collective-permute-start.30) | collective-permute-done | bytes 98336 | tf_op jit(solution)/shard_map/ppermute | solution.py:315
  113.7 4.7 %collective-permute-start.12 = (f32[192,128]{1,0:T(8,128)}, f32[192,128]{1,0:T(8,128)S(1)}, u32[]{:S(2)}, u32[]{:S(2)}) collective-permute-start(f32[192,128]{1,0:T(8,128)} %bitcast.46), channel_id=1, source_target_pairs={{0,28},{1,29},{2,30},{3,31},{4,24},{5,25},{6,26},{7,27},{8,20},{9,... | collective-permute-start | bytes 294920 | tf_op jit(solution)/shard_map/ppermute | solution.py:315
  120.6 2.8 %collective-permute-start.14 = (f32[192,128]{1,0:T(8,128)}, f32[192,128]{1,0:T(8,128)S(1)}, u32[]{:S(2)}, u32[]{:S(2)}) collective-permute-start(f32[192,128]{1,0:T(8,128)} %bitcast.44), channel_id=1, source_target_pairs={{0,30},{1,31},{2,28},{3,29},{4,26},{5,27},{6,24},{7,25},{8,22},{9,... | collective-permute-start | bytes 294920 | tf_op jit(solution)/shard_map/ppermute | solution.py:315
  123.5 3.8 %collective-permute-start.15 = (f32[192,128]{1,0:T(8,128)}, f32[192,128]{1,0:T(8,128)S(1)}, u32[]{:S(2)}, u32[]{:S(2)}) collective-permute-start(f32[192,128]{1,0:T(8,128)} %bitcast.43), channel_id=1, source_target_pairs={{0,31},{1,30},{2,29},{3,28},{4,27},{5,26},{6,25},{7,24},{8,23},{9,... | collective-permute-start | bytes 294920 | tf_op jit(solution)/shard_map/ppermute | solution.py:315
  127.9 3.9 %mix.1 = (bf16[512,320]{1,0:T(8,128)(2,1)}, bf16[512,320]{1,0:T(8,128)(2,1)}, bf16[512,192]{1,0:T(8,128)(2,1)}, bf16[512,192]{1,0:T(8,128)(2,1)}) custom-call(s32[1]{0:T(128)} %bitcast.me_ref, s32[1,320]{1,0:T(1,128)} %constant.26.clone.refs_0_, s32[1,320]{1,0:T(1,128)} %constant.27.clone.refs_1_, s32[1,192]{1,0:T(1,128)} %constant.28.clone.refs_2_, ...), custom_call_target="tpu_custom_call" | custom-call | tf_op jit(solution)/shard_map/mix/pallas_call | solution.py:234
  132.8 7.3 %solve.2.refs_11_ = f32[512,2048]{1,0:T(8,128)} custom-call(s32[1]{0:T(128)} %bitcast.me_ref, f32[2048,128]{1,0:T(8,128)} %bitcast.31, f32[2,192,128]{2,1,0:T(8,128)} %bitcast.33, f32[2,192,128]{2,1,0:T(8,128)} %copy-done.1, f32[2,192,128]{2,1,0:T(8,128)} %copy-done.2, f32[2,192,128]{2,1,0:T(8,128)} %copy-done.3, f32[2,192,128]{2,1,0:T(8,128)} %copy-done.4, ...), custom_call_target="tpu_custom_call" | custom-call | tf_op jit(solution)/shard_map/solve/pallas_call | solution.py:273
  141.3 5.7 %solve.3 = f32[512,2048]{1,0:T(8,128)} custom-call(s32[1]{0:T(128)} %bitcast.me_ref, f32[1536,128]{1,0:T(8,128)} %copy-done.8, f32[192,128]{1,0:T(8,128)} %copy-done.11, f32[192,128]{1,0:T(8,128)} %copy-done.12, f32[192,128]{1,0:T(8,128)} %copy-done.13, f32[192,128]{1,0:T(8,128)} %copy-done.14, ...), custom_call_target="tpu_custom_call", output_to_operand_aliasing={{}: (12, {})} | custom-call | tf_op jit(solution)/shard_map/solve/pallas_call | solution.py:273
  (116 shorter events, 24.3 us)
Async XLA Ops:
  5.5 126.3 %all-to-all-start = ((f32[32,4,2,8,128]{4,3,2,1,0:T(8,128)}), f32[32,4,2,8,128]{4,3,2,1,0:T(8,128)S(1)}, u32[]{:S(2)}, u32[]{:S(2)}) async-start(f32[32,4,2,8,128]{4,3,2,1,0:T(8,128)} %whiten.3), calls=%async_computation | async-start | bytes 2097152 | tf_op jit(solution)/shard_map/all_to_all | solution.py:360
  24.7 9.0 %collective-permute-start = (f32[2,192,128]{2,1,0:T(8,128)}, f32[2,192,128]{2,1,0:T(8,128)S(1)}, u32[]{:S(2)}, u32[]{:S(2)}) collective-permute-start(f32[2,192,128]{2,1,0:T(8,128)} %bitcast.42), channel_id=1, source_target_pairs={{0,2},{1,3},{2,0},{3,1},{4,6},{5,7},{6,4},{7,5},{8,10},{9,11},{10,... | collective-permute-start | bytes 589832 | tf_op jit(solution)/shard_map/ppermute | solution.py:315
  26.3 13.9 %collective-permute-start.1 = (f32[2,192,128]{2,1,0:T(8,128)}, f32[2,192,128]{2,1,0:T(8,128)S(1)}, u32[]{:S(2)}, u32[]{:S(2)}) collective-permute-start(f32[2,192,128]{2,1,0:T(8,128)} %bitcast.41), channel_id=1, source_target_pairs={{0,4},{1,5},{2,6},{3,7},{4,0},{5,1},{6,2},{7,3},{8,12},{9,13},{10,... | collective-permute-start | bytes 589832 | tf_op jit(solution)/shard_map/ppermute | solution.py:315
  27.8 12.4 %collective-permute-start.2 = (f32[2,192,128]{2,1,0:T(8,128)}, f32[2,192,128]{2,1,0:T(8,128)S(1)}, u32[]{:S(2)}, u32[]{:S(2)}) collective-permute-start(f32[2,192,128]{2,1,0:T(8,128)} %bitcast.40), channel_id=1, source_target_pairs={{0,6},{1,7},{2,4},{3,5},{4,2},{5,3},{6,0},{7,1},{8,14},{9,15},{10,... | collective-permute-start | bytes 589832 | tf_op jit(solution)/shard_map/ppermute | solution.py:315
  28.2 12.0 %collective-permute-start.3 = (f32[2,192,128]{2,1,0:T(8,128)}, f32[2,192,128]{2,1,0:T(8,128)S(1)}, u32[]{:S(2)}, u32[]{:S(2)}) collective-permute-start(f32[2,192,128]{2,1,0:T(8,128)} %bitcast.39), channel_id=1, source_target_pairs={{0,8},{1,9},{2,10},{3,11},{4,12},{5,13},{6,14},{7,15},{8,0},{9,1},... | collective-permute-start | bytes 589832 | tf_op jit(solution)/shard_map/ppermute | solution.py:315
  29.8 15.0 %collective-permute-start.4 = (f32[2,192,128]{2,1,0:T(8,128)}, f32[2,192,128]{2,1,0:T(8,128)S(1)}, u32[]{:S(2)}, u32[]{:S(2)}) collective-permute-start(f32[2,192,128]{2,1,0:T(8,128)} %bitcast.38), channel_id=1, source_target_pairs={{0,10},{1,11},{2,8},{3,9},{4,14},{5,15},{6,12},{7,13},{8,2},{9,3},... | collective-permute-start | bytes 589832 | tf_op jit(solution)/shard_map/ppermute | solution.py:315
  33.7 15.5 %collective-permute-start.5 = (f32[2,192,128]{2,1,0:T(8,128)}, f32[2,192,128]{2,1,0:T(8,128)S(1)}, u32[]{:S(2)}, u32[]{:S(2)}) collective-permute-start(f32[2,192,128]{2,1,0:T(8,128)} %bitcast.37), channel_id=1, source_target_pairs={{0,12},{1,13},{2,14},{3,15},{4,8},{5,9},{6,10},{7,11},{8,4},{9,5},... | collective-permute-start | bytes 589832 | tf_op jit(solution)/shard_map/ppermute | solution.py:315
  40.2 13.2 %collective-permute-start.6 = (f32[2,192,128]{2,1,0:T(8,128)}, f32[2,192,128]{2,1,0:T(8,128)S(1)}, u32[]{:S(2)}, u32[]{:S(2)}) collective-permute-start(f32[2,192,128]{2,1,0:T(8,128)} %bitcast.36), channel_id=1, source_target_pairs={{0,14},{1,15},{2,12},{3,13},{4,10},{5,11},{6,8},{7,9},{8,6},{9,7},... | collective-permute-start | bytes 589832 | tf_op jit(solution)/shard_map/ppermute | solution.py:315
  56.3 84.0 %collective-permute-start.7 = (f32[1536,128]{1,0:T(8,128)}, f32[1536,128]{1,0:T(8,128)S(1)}, u32[]{:S(2)}, u32[]{:S(2)}) collective-permute-start(f32[1536,128]{1,0:T(8,128)} %bundle.1), channel_id=1, source_target_pairs={{0,1},{1,0},{2,3},{3,2},{4,5},{5,4},{6,7},{7,6},{8,9},{9,8},{10,11... | collective-permute-start | bytes 2359304 | tf_op jit(solution)/shard_map/ppermute | solution.py:315
  56.3 4.9 %collective-permute-start.16 = (f32[16,256]{1,0:T(8,128)S(1)}, f32[16,256]{1,0:T(8,128)S(1)}, u32[]{:S(2)}, u32[]{:S(2)}) collective-permute-start(f32[16,256]{1,0:T(8,128)S(1)} %slice_bitcast_fusion), channel_id=1, source_target_pairs={{0,16},{1,17},{2,18},{3,19},{4,20},{5,21},{6,22},{7,23},{8,24},{9,... | collective-permute-start | bytes 49160 | tf_op jit(solution)/shard_map/ppermute | solution.py:315
  58.3 20.3 %collective-permute-start.8 = (f32[192,128]{1,0:T(8,128)}, f32[192,128]{1,0:T(8,128)S(1)}, u32[]{:S(2)}, u32[]{:S(2)}) collective-permute-start(f32[192,128]{1,0:T(8,128)} %bitcast.58), channel_id=1, source_target_pairs={{0,24},{1,25},{2,26},{3,27},{4,28},{5,29},{6,30},{7,31},{8,16},{9,... | collective-permute-start | bytes 294920 | tf_op jit(solution)/shard_map/ppermute | solution.py:315
  61.2 5.6 %collective-permute-start.23 = (f32[16,256]{1,0:T(8,128)S(1)}, f32[16,256]{1,0:T(8,128)S(1)}, u32[]{:S(2)}, u32[]{:S(2)}) collective-permute-start(f32[16,256]{1,0:T(8,128)S(1)} %broadcast_select_fusion.refs_0_.refs_5_), channel_id=1, source_target_pairs={{0,14},{1,15},{2,12},{3,13},{4,10},{5,11},{6,8},{7,9},{8,6},{9,7},... | collective-permute-start | bytes 49160 | tf_op jit(solution)/shard_map/ppermute | solution.py:315
  62.0 5.2 %collective-permute-start.22 = (f32[16,256]{1,0:T(8,128)S(1)}, f32[16,256]{1,0:T(8,128)S(1)}, u32[]{:S(2)}, u32[]{:S(2)}) collective-permute-start(f32[16,256]{1,0:T(8,128)S(1)} %broadcast_select_fusion.refs_0_.refs_5_), channel_id=1, source_target_pairs={{0,12},{1,13},{2,14},{3,15},{4,8},{5,9},{6,10},{7,11},{8,4},{9,5},... | collective-permute-start | bytes 49160 | tf_op jit(solution)/shard_map/ppermute | solution.py:315
  64.1 4.8 %collective-permute-start.21 = (f32[16,256]{1,0:T(8,128)S(1)}, f32[16,256]{1,0:T(8,128)S(1)}, u32[]{:S(2)}, u32[]{:S(2)}) collective-permute-start(f32[16,256]{1,0:T(8,128)S(1)} %broadcast_select_fusion.refs_0_.refs_5_), channel_id=1, source_target_pairs={{0,10},{1,11},{2,8},{3,9},{4,14},{5,15},{6,12},{7,13},{8,2},{9,3},... | collective-permute-start | bytes 49160 | tf_op jit(solution)/shard_map/ppermute | solution.py:315
  67.2 4.6 %collective-permute-start.19 = (f32[16,256]{1,0:T(8,128)S(1)}, f32[16,256]{1,0:T(8,128)S(1)}, u32[]{:S(2)}, u32[]{:S(2)}) collective-permute-start(f32[16,256]{1,0:T(8,128)S(1)} %broadcast_select_fusion.refs_0_.refs_5_), channel_id=1, source_target_pairs={{0,6},{1,7},{2,4},{3,5},{4,2},{5,3},{6,0},{7,1},{8,14},{9,15},{10,... | collective-permute-start | bytes 49160 | tf_op jit(solution)/shard_map/ppermute | solution.py:315
  68.9 9.7 %collective-permute-start.9 = (f32[192,128]{1,0:T(8,128)}, f32[192,128]{1,0:T(8,128)S(1)}, u32[]{:S(2)}, u32[]{:S(2)}) collective-permute-start(f32[192,128]{1,0:T(8,128)} %bitcast.57), channel_id=1, source_target_pairs={{0,25},{1,24},{2,27},{3,26},{4,29},{5,28},{6,31},{7,30},{8,17},{9,... | collective-permute-start | bytes 294920 | tf_op jit(solution)/shard_map/ppermute | solution.py:315
  71.8 5.3 %collective-permute-start.17 = (f32[16,256]{1,0:T(8,128)S(1)}, f32[16,256]{1,0:T(8,128)S(1)}, u32[]{:S(2)}, u32[]{:S(2)}) collective-permute-start(f32[16,256]{1,0:T(8,128)S(1)} %broadcast_select_fusion.refs_0_.refs_5_), channel_id=1, source_target_pairs={{0,2},{1,3},{2,0},{3,1},{4,6},{5,7},{6,4},{7,5},{8,10},{9,11},{10,... | collective-permute-start | bytes 49160 | tf_op jit(solution)/shard_map/ppermute | solution.py:315
  74.3 8.0 %collective-permute-start.10 = (f32[192,128]{1,0:T(8,128)}, f32[192,128]{1,0:T(8,128)S(1)}, u32[]{:S(2)}, u32[]{:S(2)}) collective-permute-start(f32[192,128]{1,0:T(8,128)} %bitcast.56), channel_id=1, source_target_pairs={{0,26},{1,27},{2,24},{3,25},{4,30},{5,31},{6,28},{7,29},{8,18},{9,... | collective-permute-start | bytes 294920 | tf_op jit(solution)/shard_map/ppermute | solution.py:315
  77.1 14.3 %collective-permute-start.11 = (f32[192,128]{1,0:T(8,128)}, f32[192,128]{1,0:T(8,128)S(1)}, u32[]{:S(2)}, u32[]{:S(2)}) collective-permute-start(f32[192,128]{1,0:T(8,128)} %bitcast.55), channel_id=1, source_target_pairs={{0,27},{1,26},{2,25},{3,24},{4,31},{5,30},{6,29},{7,28},{8,19},{9,... | collective-permute-start | bytes 294920 | tf_op jit(solution)/shard_map/ppermute | solution.py:315
  78.6 15.0 %collective-permute-start.25 = (f32[192,128]{1,0:T(8,128)}, f32[192,128]{1,0:T(8,128)S(1)}, u32[]{:S(2)}, u32[]{:S(2)}) collective-permute-start(f32[192,128]{1,0:T(8,128)} %bitcast.54), channel_id=1, source_target_pairs={{0,16},{1,17},{2,18},{3,19},{4,20},{5,21},{6,22},{7,23},{8,24},{9,... | collective-permute-start | bytes 294920 | tf_op jit(solution)/shard_map/ppermute | solution.py:315
  78.6 17.2 %collective-permute-start.26 = (f32[192,128]{1,0:T(8,128)}, f32[192,128]{1,0:T(8,128)S(1)}, u32[]{:S(2)}, u32[]{:S(2)}) collective-permute-start(f32[192,128]{1,0:T(8,128)} %bitcast.53), channel_id=1, source_target_pairs={{0,17},{1,16},{2,19},{3,18},{4,21},{5,20},{6,23},{7,22},{8,25},{9,... | collective-permute-start | bytes 294920 | tf_op jit(solution)/shard_map/ppermute | solution.py:315
  82.3 20.9 %collective-permute-start.27 = (f32[192,128]{1,0:T(8,128)}, f32[192,128]{1,0:T(8,128)S(1)}, u32[]{:S(2)}, u32[]{:S(2)}) collective-permute-start(f32[192,128]{1,0:T(8,128)} %bitcast.52), channel_id=1, source_target_pairs={{0,18},{1,19},{2,16},{3,17},{4,22},{5,23},{6,20},{7,21},{8,26},{9,... | collective-permute-start | bytes 294920 | tf_op jit(solution)/shard_map/ppermute | solution.py:315
  91.4 14.0 %collective-permute-start.28 = (f32[192,128]{1,0:T(8,128)}, f32[192,128]{1,0:T(8,128)S(1)}, u32[]{:S(2)}, u32[]{:S(2)}) collective-permute-start(f32[192,128]{1,0:T(8,128)} %bitcast.51), channel_id=1, source_target_pairs={{0,19},{1,18},{2,17},{3,16},{4,23},{5,22},{6,21},{7,20},{8,27},{9,... | collective-permute-start | bytes 294920 | tf_op jit(solution)/shard_map/ppermute | solution.py:315
  93.6 15.8 %collective-permute-start.29 = (f32[192,128]{1,0:T(8,128)}, f32[192,128]{1,0:T(8,128)S(1)}, u32[]{:S(2)}, u32[]{:S(2)}) collective-permute-start(f32[192,128]{1,0:T(8,128)} %bitcast.50), channel_id=1, source_target_pairs={{0,20},{1,21},{2,22},{3,23},{4,16},{5,17},{6,18},{7,19},{8,28},{9,... | collective-permute-start | bytes 294920 | tf_op jit(solution)/shard_map/ppermute | solution.py:315
  95.9 27.6 %collective-permute-start.24 = (f32[128,256]{1,0:T(8,128)}, f32[128,256]{1,0:T(8,128)S(1)}, u32[]{:S(2)}, u32[]{:S(2)}) collective-permute-start(f32[128,256]{1,0:T(8,128)} %stack.1), channel_id=1, source_target_pairs={{0,1},{1,0},{2,3},{3,2},{4,5},{5,4},{6,7},{7,6},{8,9},{9,8},{10,11... | collective-permute-start | bytes 393224 | tf_op jit(solution)/shard_map/ppermute | solution.py:315
  103.2 10.5 %collective-permute-start.30 = (f32[192,128]{1,0:T(8,128)}, f32[192,128]{1,0:T(8,128)S(1)}, u32[]{:S(2)}, u32[]{:S(2)}) collective-permute-start(f32[192,128]{1,0:T(8,128)} %bitcast.49), channel_id=1, source_target_pairs={{0,21},{1,20},{2,23},{3,22},{4,17},{5,16},{6,19},{7,18},{8,29},{9,... | collective-permute-start | bytes 294920 | tf_op jit(solution)/shard_map/ppermute | solution.py:315
  105.4 13.4 %collective-permute-start.31 = (f32[192,128]{1,0:T(8,128)}, f32[192,128]{1,0:T(8,128)S(1)}, u32[]{:S(2)}, u32[]{:S(2)}) collective-permute-start(f32[192,128]{1,0:T(8,128)} %bitcast.48), channel_id=1, source_target_pairs={{0,22},{1,23},{2,20},{3,21},{4,18},{5,19},{6,16},{7,17},{8,30},{9,... | collective-permute-start | bytes 294920 | tf_op jit(solution)/shard_map/ppermute | solution.py:315
  109.4 11.2 %collective-permute-start.32 = (f32[192,128]{1,0:T(8,128)}, f32[192,128]{1,0:T(8,128)S(1)}, u32[]{:S(2)}, u32[]{:S(2)}) collective-permute-start(f32[192,128]{1,0:T(8,128)} %bitcast.47), channel_id=1, source_target_pairs={{0,23},{1,22},{2,21},{3,20},{4,19},{5,18},{6,17},{7,16},{8,31},{9,... | collective-permute-start | bytes 294920 | tf_op jit(solution)/shard_map/ppermute | solution.py:315
  113.7 26.5 %collective-permute-start.12 = (f32[192,128]{1,0:T(8,128)}, f32[192,128]{1,0:T(8,128)S(1)}, u32[]{:S(2)}, u32[]{:S(2)}) collective-permute-start(f32[192,128]{1,0:T(8,128)} %bitcast.46), channel_id=1, source_target_pairs={{0,28},{1,29},{2,30},{3,31},{4,24},{5,25},{6,26},{7,27},{8,20},{9,... | collective-permute-start | bytes 294920 | tf_op jit(solution)/shard_map/ppermute | solution.py:315
  118.8 21.4 %collective-permute-start.13 = (f32[192,128]{1,0:T(8,128)}, f32[192,128]{1,0:T(8,128)S(1)}, u32[]{:S(2)}, u32[]{:S(2)}) collective-permute-start(f32[192,128]{1,0:T(8,128)} %bitcast.45), channel_id=1, source_target_pairs={{0,29},{1,28},{2,31},{3,30},{4,25},{5,24},{6,27},{7,26},{8,21},{9,... | collective-permute-start | bytes 294920 | tf_op jit(solution)/shard_map/ppermute | solution.py:315
  120.6 19.6 %collective-permute-start.14 = (f32[192,128]{1,0:T(8,128)}, f32[192,128]{1,0:T(8,128)S(1)}, u32[]{:S(2)}, u32[]{:S(2)}) collective-permute-start(f32[192,128]{1,0:T(8,128)} %bitcast.44), channel_id=1, source_target_pairs={{0,30},{1,31},{2,28},{3,29},{4,26},{5,27},{6,24},{7,25},{8,22},{9,... | collective-permute-start | bytes 294920 | tf_op jit(solution)/shard_map/ppermute | solution.py:315
  123.5 16.8 %collective-permute-start.15 = (f32[192,128]{1,0:T(8,128)}, f32[192,128]{1,0:T(8,128)S(1)}, u32[]{:S(2)}, u32[]{:S(2)}) collective-permute-start(f32[192,128]{1,0:T(8,128)} %bitcast.43), channel_id=1, source_target_pairs={{0,31},{1,30},{2,29},{3,28},{4,27},{5,26},{6,25},{7,24},{8,23},{9,... | collective-permute-start | bytes 294920 | tf_op jit(solution)/shard_map/ppermute | solution.py:315
  (37 other events, 761.3 us)

commit v7 on v6

--- a/solution.py
+++ b/solution.py
@@ -276,6 +276,7 @@
             num_scalar_prefetch=1, grid=(rows // per,), in_specs=specs, out_specs=tile),
         out_shape=jax.ShapeDtypeStruct((width, each * LANES), jnp.float32),
         input_output_aliases={} if acc is None else {len(args): 0},
+        compiler_params=None if acc is None else pltpu.CompilerParams(vmem_limit_bytes=24 << 20),
         name="solve",
     )(me, *args)
 
@@ -307,7 +308,8 @@
 
 
 HEAD = 4
-SOON = 8
+SOON = 6
+NEAR_SOON = 5
 
 
 def exchange(x, offset):
@@ -337,8 +339,9 @@
     rest = range(HEAD, local)
     head = [(source * local + r, 0) for source in range(groups) for r in range(HEAD)]
     ways = lambda picks: [(way * local + r, -1) for way in picks for r in rest]
-    soon = head + ways(range(0, top, 2)) + ways(range(top, top + SOON))
-    last = ways(range(1, top, 2)) + ways(range(top + SOON, groups))
+    near, far = list(range(0, top, 2)), list(range(top, groups))
+    soon = head + ways(near[:NEAR_SOON]) + ways(far[:SOON])
+    last = ways(range(1, top, 2)) + ways(near[NEAR_SOON:]) + ways(far[SOON:])
     return [np.array(stage, np.int32).T.reshape(2, 1, -1) for stage in (soon, last)]
 
 
@@ -372,8 +375,8 @@
     tables = mix(me, places(groups, local), block_inverses, papers, theirs, top, local)
     load = bundle(me, got)
     load = exchange(load, 1)
-    out = solve(me, outside([head.reshape(-1, LANES), *got, *direct[:SOON]]), tables[:2], rows, parts)
-    return solve(me, [load, *outside(direct[SOON:])], tables[2:], rows, parts, out)
+    out = solve(me, outside([head.reshape(-1, LANES), *got[:NEAR_SOON], *direct[:SOON]]), tables[:2], rows, parts)
+    return solve(me, [load, *outside(got[NEAR_SOON:]), *direct[SOON:]], tables[2:], rows, parts, out)
 
 
 def solution(mesh):

time: 148 us -> 146 us (0.986)
  starting transfers between devices: 64.8 us -> 54.1 us
  waiting for transfers between devices: 40.8 us -> 51.4 us
    ppermute x33, starting transfers between devices: 57.3 us -> 46.5 us  [exchange(): return lax.ppermute(x, 'dev', pairs)]
    ppermute x33, waiting for transfers between devices: 40.8 us -> 51.4 us  [exchange(): return lax.ppermute(x, 'dev', pairs)]
  transfers between devices with their start and end apart: 34 -> 34, of which waited for: 19 -> 17; matrix products, arithmetic and copies ran while one was open for 0% -> 0% of each run, Pallas kernels for 18% -> 18%
where the time goes in v7:
time: 146 us; the launch traced here: 145 us
  starting transfers between devices  54.1 us (37%)
  waiting for transfers between devices  51.4 us (35%)
  Pallas kernels  37.4 us (26%)
  local copies, waits for them, and re-layouts  2.25 us (2%)
    ppermute x33, waiting for transfers between devices, exchange(): return lax.ppermute(x, 'dev', pairs)  51.4 us
    ppermute x33, starting transfers between devices, exchange(): return lax.ppermute(x, 'dev', pairs)  46.5 us
    pallas_call x2, Pallas kernels, whiten(): pl.pallas_call(functools.partial(whiten_kernel, rb=rb, groups=groups, out...  17.2 us
    pallas_call x2, Pallas kernels, solve(): pl.pallas_call(functools.partial(solve_kernel, rows=rows, parts=parts, pe...  12.6 us
    all_to_all x1, starting transfers between devices, per_device(): head = lax.all_to_all(head, 'dev', 0, 0, tiled=True)  7.51 us
    pallas_call x1, Pallas kernels, mix(): pl.pallas_call(functools.partial(mix_kernel, top=top, local=local, stages...  3.92 us
  transfers between devices with their start and end apart: 34, of which 17 were waited for; matrix products, arithmetic and copies ran while one was open for 0% of the time, Pallas kernels for 18%

profile of v7, /device:TPU:0, one launch (start us, length us, event | category | flops | bytes accessed | tf_op | source)
XLA Modules:
  0.0 145.4 jit_solution(11729074628139459794)
XLA Ops:
  0.0 5.4 %whiten.3 = f32[32,4,2,8,128]{4,3,2,1,0:T(8,128)} custom-call(s32[1]{0:T(128)} %bitcast.me_ref, f32[16,256,256]{2,1,0:T(8,128)} %x_ref.3, f32[129,256]{1,0:T(8,128)} %bitcast.34, bf16[256,256]{1,0:T(8,128)(2,1)} %constant.22.clone.fh_ref, bf16[256,256]{1,0:T(8,128)(2,1)} %constant.23.clone.fl_ref, bf16[256,256]{1,0:T(8,128)(2,1)} %constant.24.clone.th_ref, ...), custom_call_target="tpu_custom_call" | custom-call | tf_op jit(solution)/shard_map/whiten/pallas_call | solution.py:125
  5.5 7.5 %all-to-all-start = ((f32[32,4,2,8,128]{4,3,2,1,0:T(8,128)}), f32[32,4,2,8,128]{4,3,2,1,0:T(8,128)S(1)}, u32[]{:S(2)}, u32[]{:S(2)}) async-start(f32[32,4,2,8,128]{4,3,2,1,0:T(8,128)} %whiten.3), calls=%async_computation | async-start | bytes 2097152 | tf_op jit(solution)/shard_map/all_to_all | solution.py:363
  13.0 11.7 %whiten.2 = (f32[2,12,2,8,128]{4,3,2,1,0:T(8,128)}, f32[2,12,2,8,128]{4,3,2,1,0:T(8,128)}, f32[2,12,2,8,128]{4,3,2,1,0:T(8,128)}, f32[2,12,2,8,128]{4,3,2,1,0:T(...) custom-call(s32[1]{0:T(128)} %bitcast.me_ref, ...), custom_call_target="tpu_custom_call" | custom-call | tf_op jit(solution)/shard_map/whiten/pallas_call | solution.py:125
  24.7 1.7 %collective-permute-start = (f32[2,192,128]{2,1,0:T(8,128)}, f32[2,192,128]{2,1,0:T(8,128)S(1)}, u32[]{:S(2)}, u32[]{:S(2)}) collective-permute-start(f32[2,192,128]{2,1,0:T(8,128)} %bitcast.42), channel_id=1, source_target_pairs={{0,2},{1,3},{2,0},{3,1},{4,6},{5,7},{6,4},{7,5},{8,10},{9,11},{10,... | collective-permute-start | bytes 589832 | tf_op jit(solution)/shard_map/ppermute | solution.py:317
  31.3 2.4 %collective-permute-done.refs_1_.refs_2_ = f32[2,192,128]{2,1,0:T(8,128)S(1)} collective-permute-done((f32[2,192,128]{2,1,0:T(8,128)}, f32[2,192,128]{2,1,0:T(8,128)S(1)}, u32[]{:S(2)}, u32[]{:S(2)}) %collective-permute-start) | collective-permute-done | bytes 196640 | tf_op jit(solution)/shard_map/ppermute | solution.py:317
  33.7 2.6 %collective-permute-start.5 = (f32[2,192,128]{2,1,0:T(8,128)}, f32[2,192,128]{2,1,0:T(8,128)S(1)}, u32[]{:S(2)}, u32[]{:S(2)}) collective-permute-start(f32[2,192,128]{2,1,0:T(8,128)} %bitcast.37), channel_id=1, source_target_pairs={{0,12},{1,13},{2,14},{3,15},{4,8},{5,9},{6,10},{7,11},{8,4},{9,5},... | collective-permute-start | bytes 589832 | tf_op jit(solution)/shard_map/ppermute | solution.py:317
  36.3 3.9 %collective-permute-done.1.refs_2_.refs_3_ = f32[2,192,128]{2,1,0:T(8,128)S(1)} collective-permute-done((f32[2,192,128]{2,1,0:T(8,128)}, f32[2,192,128]{2,1,0:T(8,128)S(1)}, u32[]{:S(2)}, u32[]{:S(2)}) %collective-permute-start.1) | collective-permute-done | bytes 196640 | tf_op jit(solution)/shard_map/ppermute | solution.py:317
  40.3 4.5 %collective-permute-done.4.refs_5_.refs_1_ = f32[2,192,128]{2,1,0:T(8,128)S(1)} collective-permute-done((f32[2,192,128]{2,1,0:T(8,128)}, f32[2,192,128]{2,1,0:T(8,128)S(1)}, u32[]{:S(2)}, u32[]{:S(2)}) %collective-permute-start.4) | collective-permute-done | bytes 196640 | tf_op jit(solution)/shard_map/ppermute | solution.py:317
  44.8 4.4 %collective-permute-done.5.refs_6_.refs_2_ = f32[2,192,128]{2,1,0:T(8,128)S(1)} collective-permute-done((f32[2,192,128]{2,1,0:T(8,128)}, f32[2,192,128]{2,1,0:T(8,128)S(1)}, u32[]{:S(2)}, u32[]{:S(2)}) %collective-permute-start.5) | collective-permute-done | bytes 196640 | tf_op jit(solution)/shard_map/ppermute | solution.py:317
  49.2 4.3 %collective-permute-done.6.refs_7_.refs_3_ = f32[2,192,128]{2,1,0:T(8,128)S(1)} collective-permute-done((f32[2,192,128]{2,1,0:T(8,128)}, f32[2,192,128]{2,1,0:T(8,128)S(1)}, u32[]{:S(2)}, u32[]{:S(2)}) %collective-permute-start.6) | collective-permute-done | bytes 196640 | tf_op jit(solution)/shard_map/ppermute | solution.py:317
  54.2 2.2 %bundle.1 = f32[1536,128]{1,0:T(8,128)} custom-call(s32[1]{0:T(128)} %bitcast.me_ref, f32[2,192,128]{2,1,0:T(8,128)} %bitcast.32, f32[2,192,128]{2,1,0:T(8,128)} %copy-done.4, f32[2,192,128]{2,1,0:T(8,128)} %copy-done.5, f32[2,192,128]{2,1,0:T(8,128)} %copy-done.6, f32[2,192,128]{2,1,0:T(8,128)} %copy-done.7, f32[2,192,128]{2,1,0:T(8,128)} %copy-done.1, ...), custom_call_target="tpu_custom_call" | custom-call | tf_op jit(solution)/shard_map/bundle/pallas_call | solution.py:183
  56.3 2.0 %collective-permute-start.18 = (f32[16,256]{1,0:T(8,128)S(1)}, f32[16,256]{1,0:T(8,128)S(1)}, u32[]{:S(2)}, u32[]{:S(2)}) collective-permute-start(f32[16,256]{1,0:T(8,128)S(1)} %slice_bitcast_fusion), channel_id=1, source_target_pairs={{0,16},{1,17},{2,18},{3,19},{4,20},{5,21},{6,22},{7,23},{8,24},{9,... | collective-permute-start | bytes 49160 | tf_op jit(solution)/shard_map/ppermute | solution.py:317
  59.5 1.7 %collective-permute-done.18 = f32[16,256]{1,0:T(8,128)S(1)} collective-permute-done((f32[16,256]{1,0:T(8,128)S(1)}, f32[16,256]{1,0:T(8,128)S(1)}, u32[]{:S(2)}, u32[]{:S(2)}) %collective-permute-start.18) | collective-permute-done | bytes 16416 | tf_op jit(solution)/shard_map/ppermute | solution.py:317
  62.0 2.2 %collective-permute-start.24 = (f32[16,256]{1,0:T(8,128)S(1)}, f32[16,256]{1,0:T(8,128)S(1)}, u32[]{:S(2)}, u32[]{:S(2)}) collective-permute-start(f32[16,256]{1,0:T(8,128)S(1)} %broadcast_select_fusion.refs_0_.refs_5_), channel_id=1, source_target_pairs={{0,12},{1,13},{2,14},{3,15},{4,8},{5,9},{6,10},{7,11},{8,4},{9,5},... | collective-permute-start | bytes 49160 | tf_op jit(solution)/shard_map/ppermute | solution.py:317
  65.5 3.1 %collective-permute-done.25.refs_7_.refs_12_ = f32[16,256]{1,0:T(8,128)S(1)} collective-permute-done((f32[16,256]{1,0:T(8,128)S(1)}, f32[16,256]{1,0:T(8,128)S(1)}, u32[]{:S(2)}, u32[]{:S(2)}) %collective-permute-start.25) | collective-permute-done | bytes 16416 | tf_op jit(solution)/shard_map/ppermute | solution.py:317
  69.1 3.2 %collective-permute-done.22.refs_4_.refs_9_ = f32[16,256]{1,0:T(8,128)S(1)} collective-permute-done((f32[16,256]{1,0:T(8,128)S(1)}, f32[16,256]{1,0:T(8,128)S(1)}, u32[]{:S(2)}, u32[]{:S(2)}) %collective-permute-start.22) | collective-permute-done | bytes 16416 | tf_op jit(solution)/shard_map/ppermute | solution.py:317
  74.1 2.6 %collective-permute-done.20.refs_2_.refs_7_ = f32[16,256]{1,0:T(8,128)S(1)} collective-permute-done((f32[16,256]{1,0:T(8,128)S(1)}, f32[16,256]{1,0:T(8,128)S(1)}, u32[]{:S(2)}, u32[]{:S(2)}) %collective-permute-start.20) | collective-permute-done | bytes 16416 | tf_op jit(solution)/shard_map/ppermute | solution.py:317
  78.9 2.0 %collective-permute-start.12 = (f32[192,128]{1,0:T(8,128)}, f32[192,128]{1,0:T(8,128)S(1)}, u32[]{:S(2)}, u32[]{:S(2)}) collective-permute-start(f32[192,128]{1,0:T(8,128)} %bitcast.54), channel_id=1, source_target_pairs={{0,26},{1,27},{2,24},{3,25},{4,30},{5,31},{6,28},{7,29},{8,18},{9,... | collective-permute-start | bytes 294920 | tf_op jit(solution)/shard_map/ppermute | solution.py:317
  80.9 3.8 %collective-permute-start.13 = (f32[192,128]{1,0:T(8,128)}, f32[192,128]{1,0:T(8,128)S(1)}, u32[]{:S(2)}, u32[]{:S(2)}) collective-permute-start(f32[192,128]{1,0:T(8,128)} %bitcast.53), channel_id=1, source_target_pairs={{0,27},{1,26},{2,25},{3,24},{4,31},{5,30},{6,29},{7,28},{8,19},{9,... | collective-permute-start | bytes 294920 | tf_op jit(solution)/shard_map/ppermute | solution.py:317
  84.7 7.2 %collective-permute-start.27 = (f32[192,128]{1,0:T(8,128)}, f32[192,128]{1,0:T(8,128)S(1)}, u32[]{:S(2)}, u32[]{:S(2)}) collective-permute-start(f32[192,128]{1,0:T(8,128)} %bitcast.52), channel_id=1, source_target_pairs={{0,16},{1,17},{2,18},{3,19},{4,20},{5,21},{6,22},{7,23},{8,24},{9,... | collective-permute-start | bytes 294920 | tf_op jit(solution)/shard_map/ppermute | solution.py:317
  93.4 3.6 %collective-permute-start.29 = (f32[192,128]{1,0:T(8,128)}, f32[192,128]{1,0:T(8,128)S(1)}, u32[]{:S(2)}, u32[]{:S(2)}) collective-permute-start(f32[192,128]{1,0:T(8,128)} %bitcast.50), channel_id=1, source_target_pairs={{0,18},{1,19},{2,16},{3,17},{4,22},{5,23},{6,20},{7,21},{8,26},{9,... | collective-permute-start | bytes 294920 | tf_op jit(solution)/shard_map/ppermute | solution.py:317
  98.6 5.2 %collective-permute-done.27.refs_6_ = f32[192,128]{1,0:T(8,128)S(1)} collective-permute-done((f32[192,128]{1,0:T(8,128)}, f32[192,128]{1,0:T(8,128)S(1)}, u32[]{:S(2)}, u32[]{:S(2)}) %collective-permute-start.27) | collective-permute-done | bytes 98336 | tf_op jit(solution)/shard_map/ppermute | solution.py:317
  104.0 2.6 %collective-permute-done.28.refs_7_ = f32[192,128]{1,0:T(8,128)S(1)} collective-permute-done((f32[192,128]{1,0:T(8,128)}, f32[192,128]{1,0:T(8,128)S(1)}, u32[]{:S(2)}, u32[]{:S(2)}) %collective-permute-start.28) | collective-permute-done | bytes 98336 | tf_op jit(solution)/shard_map/ppermute | solution.py:317
  106.9 6.9 %collective-permute-done.29.refs_8_ = f32[192,128]{1,0:T(8,128)S(1)} collective-permute-done((f32[192,128]{1,0:T(8,128)}, f32[192,128]{1,0:T(8,128)S(1)}, u32[]{:S(2)}, u32[]{:S(2)}) %collective-permute-start.29) | collective-permute-done | bytes 98336 | tf_op jit(solution)/shard_map/ppermute | solution.py:317
  113.8 2.1 %collective-permute-done.30.refs_9_ = f32[192,128]{1,0:T(8,128)S(1)} collective-permute-done((f32[192,128]{1,0:T(8,128)}, f32[192,128]{1,0:T(8,128)S(1)}, u32[]{:S(2)}, u32[]{:S(2)}) %collective-permute-start.30) | collective-permute-done | bytes 98336 | tf_op jit(solution)/shard_map/ppermute | solution.py:317
  116.9 2.4 %collective-permute-done.31.refs_10_ = f32[192,128]{1,0:T(8,128)S(1)} collective-permute-done((f32[192,128]{1,0:T(8,128)}, f32[192,128]{1,0:T(8,128)S(1)}, u32[]{:S(2)}, u32[]{:S(2)}) %collective-permute-start.31) | collective-permute-done | bytes 98336 | tf_op jit(solution)/shard_map/ppermute | solution.py:317
  119.2 2.1 %collective-permute-start.15 = (f32[192,128]{1,0:T(8,128)}, f32[192,128]{1,0:T(8,128)S(1)}, u32[]{:S(2)}, u32[]{:S(2)}) collective-permute-start(f32[192,128]{1,0:T(8,128)} %bitcast.45), channel_id=1, source_target_pairs={{0,29},{1,28},{2,31},{3,30},{4,25},{5,24},{6,27},{7,26},{8,21},{9,... | collective-permute-start | bytes 294920 | tf_op jit(solution)/shard_map/ppermute | solution.py:317
  121.6 2.2 %collective-permute-start.16 = (f32[192,128]{1,0:T(8,128)}, f32[192,128]{1,0:T(8,128)S(1)}, u32[]{:S(2)}, u32[]{:S(2)}) collective-permute-start(f32[192,128]{1,0:T(8,128)} %bitcast.44), channel_id=1, source_target_pairs={{0,30},{1,31},{2,28},{3,29},{4,26},{5,27},{6,24},{7,25},{8,22},{9,... | collective-permute-start | bytes 294920 | tf_op jit(solution)/shard_map/ppermute | solution.py:317
  123.8 3.4 %collective-permute-start.17 = (f32[192,128]{1,0:T(8,128)}, f32[192,128]{1,0:T(8,128)S(1)}, u32[]{:S(2)}, u32[]{:S(2)}) collective-permute-start(f32[192,128]{1,0:T(8,128)} %bitcast.43), channel_id=1, source_target_pairs={{0,31},{1,30},{2,29},{3,28},{4,27},{5,26},{6,25},{7,24},{8,23},{9,... | collective-permute-start | bytes 294920 | tf_op jit(solution)/shard_map/ppermute | solution.py:317
  127.8 3.9 %mix.1 = (bf16[512,260]{1,0:T(8,128)(2,1)}, bf16[512,260]{1,0:T(8,128)(2,1)}, bf16[512,252]{1,0:T(8,128)(2,1)}, bf16[512,252]{1,0:T(8,128)(2,1)}) custom-call(s32[1]{0:T(128)} %bitcast.me_ref, s32[1,260]{1,0:T(1,128)} %constant.26.clone.refs_0_, s32[1,260]{1,0:T(1,128)} %constant.27.clone.refs_1_, s32[1,252]{1,0:T(1,128)} %constant.28.clone.refs_2_, ...), custom_call_target="tpu_custom_call" | custom-call | tf_op jit(solution)/shard_map/mix/pallas_call | solution.py:234
  132.7 7.1 %solve.2.refs_16_ = f32[512,2048]{1,0:T(8,128)} custom-call(s32[1]{0:T(128)} %bitcast.me_ref, f32[2048,128]{1,0:T(8,128)} %bitcast.31, f32[2,192,128]{2,1,0:T(8,128)} %bitcast.33, f32[2,192,128]{2,1,0:T(8,128)} %copy-done.4, f32[2,192,128]{2,1,0:T(8,128)} %copy-done.5, f32[2,192,128]{2,1,0:T(8,128)} %copy-done.6, f32[2,192,128]{2,1,0:T(8,128)} %copy-done.7, ...), custom_call_target="tpu_custom_call" | custom-call | tf_op jit(solution)/shard_map/solve/pallas_call | solution.py:273
  139.9 5.5 %solve.3 = f32[512,2048]{1,0:T(8,128)} custom-call(s32[1]{0:T(128)} %bitcast.me_ref, f32[1536,128]{1,0:T(8,128)S(1)} %collective-permute-done.7.refs_0_, f32[2,192,128]{2,1,0:T(8,128)} %copy-done.1, f32[2,192,128]{2,1,0:T(8,128)} %copy-done.2, f32[2,192,128]{2,1,0:T(8,128)} %copy-done.3, ...), custom_call_target="tpu_custom_call", output_to_operand_aliasing={{}: (17, {})} | custom-call | tf_op jit(solution)/shard_map/solve/pallas_call | solution.py:273
  (94 shorter events, 19.6 us)
Async XLA Ops:
  5.5 126.3 %all-to-all-start = ((f32[32,4,2,8,128]{4,3,2,1,0:T(8,128)}), f32[32,4,2,8,128]{4,3,2,1,0:T(8,128)S(1)}, u32[]{:S(2)}, u32[]{:S(2)}) async-start(f32[32,4,2,8,128]{4,3,2,1,0:T(8,128)} %whiten.3), calls=%async_computation | async-start | bytes 2097152 | tf_op jit(solution)/shard_map/all_to_all | solution.py:363
  24.7 9.0 %collective-permute-start = (f32[2,192,128]{2,1,0:T(8,128)}, f32[2,192,128]{2,1,0:T(8,128)S(1)}, u32[]{:S(2)}, u32[]{:S(2)}) collective-permute-start(f32[2,192,128]{2,1,0:T(8,128)} %bitcast.42), channel_id=1, source_target_pairs={{0,2},{1,3},{2,0},{3,1},{4,6},{5,7},{6,4},{7,5},{8,10},{9,11},{10,... | collective-permute-start | bytes 589832 | tf_op jit(solution)/shard_map/ppermute | solution.py:317
  26.4 13.9 %collective-permute-start.1 = (f32[2,192,128]{2,1,0:T(8,128)}, f32[2,192,128]{2,1,0:T(8,128)S(1)}, u32[]{:S(2)}, u32[]{:S(2)}) collective-permute-start(f32[2,192,128]{2,1,0:T(8,128)} %bitcast.41), channel_id=1, source_target_pairs={{0,4},{1,5},{2,6},{3,7},{4,0},{5,1},{6,2},{7,3},{8,12},{9,13},{10,... | collective-permute-start | bytes 589832 | tf_op jit(solution)/shard_map/ppermute | solution.py:317
  27.8 12.4 %collective-permute-start.2 = (f32[2,192,128]{2,1,0:T(8,128)}, f32[2,192,128]{2,1,0:T(8,128)S(1)}, u32[]{:S(2)}, u32[]{:S(2)}) collective-permute-start(f32[2,192,128]{2,1,0:T(8,128)} %bitcast.40), channel_id=1, source_target_pairs={{0,6},{1,7},{2,4},{3,5},{4,2},{5,3},{6,0},{7,1},{8,14},{9,15},{10,... | collective-permute-start | bytes 589832 | tf_op jit(solution)/shard_map/ppermute | solution.py:317
  28.3 12.0 %collective-permute-start.3 = (f32[2,192,128]{2,1,0:T(8,128)}, f32[2,192,128]{2,1,0:T(8,128)S(1)}, u32[]{:S(2)}, u32[]{:S(2)}) collective-permute-start(f32[2,192,128]{2,1,0:T(8,128)} %bitcast.39), channel_id=1, source_target_pairs={{0,8},{1,9},{2,10},{3,11},{4,12},{5,13},{6,14},{7,15},{8,0},{9,1},... | collective-permute-start | bytes 589832 | tf_op jit(solution)/shard_map/ppermute | solution.py:317
  29.9 15.0 %collective-permute-start.4 = (f32[2,192,128]{2,1,0:T(8,128)}, f32[2,192,128]{2,1,0:T(8,128)S(1)}, u32[]{:S(2)}, u32[]{:S(2)}) collective-permute-start(f32[2,192,128]{2,1,0:T(8,128)} %bitcast.38), channel_id=1, source_target_pairs={{0,10},{1,11},{2,8},{3,9},{4,14},{5,15},{6,12},{7,13},{8,2},{9,3},... | collective-permute-start | bytes 589832 | tf_op jit(solution)/shard_map/ppermute | solution.py:317
  33.7 15.5 %collective-permute-start.5 = (f32[2,192,128]{2,1,0:T(8,128)}, f32[2,192,128]{2,1,0:T(8,128)S(1)}, u32[]{:S(2)}, u32[]{:S(2)}) collective-permute-start(f32[2,192,128]{2,1,0:T(8,128)} %bitcast.37), channel_id=1, source_target_pairs={{0,12},{1,13},{2,14},{3,15},{4,8},{5,9},{6,10},{7,11},{8,4},{9,5},... | collective-permute-start | bytes 589832 | tf_op jit(solution)/shard_map/ppermute | solution.py:317
  40.2 13.2 %collective-permute-start.6 = (f32[2,192,128]{2,1,0:T(8,128)}, f32[2,192,128]{2,1,0:T(8,128)S(1)}, u32[]{:S(2)}, u32[]{:S(2)}) collective-permute-start(f32[2,192,128]{2,1,0:T(8,128)} %bitcast.36), channel_id=1, source_target_pairs={{0,14},{1,15},{2,12},{3,13},{4,10},{5,11},{6,8},{7,9},{8,6},{9,7},... | collective-permute-start | bytes 589832 | tf_op jit(solution)/shard_map/ppermute | solution.py:317
  56.3 83.6 %collective-permute-start.7 = (f32[1536,128]{1,0:T(8,128)}, f32[1536,128]{1,0:T(8,128)S(1)}, u32[]{:S(2)}, u32[]{:S(2)}) collective-permute-start(f32[1536,128]{1,0:T(8,128)} %bundle.1), channel_id=1, source_target_pairs={{0,1},{1,0},{2,3},{3,2},{4,5},{5,4},{6,7},{7,6},{8,9},{9,8},{10,11... | collective-permute-start | bytes 2359304 | tf_op jit(solution)/shard_map/ppermute | solution.py:317
  56.3 4.9 %collective-permute-start.18 = (f32[16,256]{1,0:T(8,128)S(1)}, f32[16,256]{1,0:T(8,128)S(1)}, u32[]{:S(2)}, u32[]{:S(2)}) collective-permute-start(f32[16,256]{1,0:T(8,128)S(1)} %slice_bitcast_fusion), channel_id=1, source_target_pairs={{0,16},{1,17},{2,18},{3,19},{4,20},{5,21},{6,22},{7,23},{8,24},{9,... | collective-permute-start | bytes 49160 | tf_op jit(solution)/shard_map/ppermute | solution.py:317
  58.4 20.5 %collective-permute-start.8 = (f32[192,128]{1,0:T(8,128)}, f32[192,128]{1,0:T(8,128)S(1)}, u32[]{:S(2)}, u32[]{:S(2)}) collective-permute-start(f32[192,128]{1,0:T(8,128)} %bitcast.58), channel_id=1, source_target_pairs={{0,22},{1,23},{2,20},{3,21},{4,18},{5,19},{6,16},{7,17},{8,30},{9,... | collective-permute-start | bytes 294920 | tf_op jit(solution)/shard_map/ppermute | solution.py:317
  61.2 7.4 %collective-permute-start.25 = (f32[16,256]{1,0:T(8,128)S(1)}, f32[16,256]{1,0:T(8,128)S(1)}, u32[]{:S(2)}, u32[]{:S(2)}) collective-permute-start(f32[16,256]{1,0:T(8,128)S(1)} %broadcast_select_fusion.refs_0_.refs_5_), channel_id=1, source_target_pairs={{0,14},{1,15},{2,12},{3,13},{4,10},{5,11},{6,8},{7,9},{8,6},{9,7},... | collective-permute-start | bytes 49160 | tf_op jit(solution)/shard_map/ppermute | solution.py:317
  62.0 6.6 %collective-permute-start.24 = (f32[16,256]{1,0:T(8,128)S(1)}, f32[16,256]{1,0:T(8,128)S(1)}, u32[]{:S(2)}, u32[]{:S(2)}) collective-permute-start(f32[16,256]{1,0:T(8,128)S(1)} %broadcast_select_fusion.refs_0_.refs_5_), channel_id=1, source_target_pairs={{0,12},{1,13},{2,14},{3,15},{4,8},{5,9},{6,10},{7,11},{8,4},{9,5},... | collective-permute-start | bytes 49160 | tf_op jit(solution)/shard_map/ppermute | solution.py:317
  64.2 4.9 %collective-permute-start.23 = (f32[16,256]{1,0:T(8,128)S(1)}, f32[16,256]{1,0:T(8,128)S(1)}, u32[]{:S(2)}, u32[]{:S(2)}) collective-permute-start(f32[16,256]{1,0:T(8,128)S(1)} %broadcast_select_fusion.refs_0_.refs_5_), channel_id=1, source_target_pairs={{0,10},{1,11},{2,8},{3,9},{4,14},{5,15},{6,12},{7,13},{8,2},{9,3},... | collective-permute-start | bytes 49160 | tf_op jit(solution)/shard_map/ppermute | solution.py:317
  68.6 4.7 %collective-permute-start.21 = (f32[16,256]{1,0:T(8,128)S(1)}, f32[16,256]{1,0:T(8,128)S(1)}, u32[]{:S(2)}, u32[]{:S(2)}) collective-permute-start(f32[16,256]{1,0:T(8,128)S(1)} %broadcast_select_fusion.refs_0_.refs_5_), channel_id=1, source_target_pairs={{0,6},{1,7},{2,4},{3,5},{4,2},{5,3},{6,0},{7,1},{8,14},{9,15},{10,... | collective-permute-start | bytes 49160 | tf_op jit(solution)/shard_map/ppermute | solution.py:317
  69.1 11.8 %collective-permute-start.9 = (f32[192,128]{1,0:T(8,128)}, f32[192,128]{1,0:T(8,128)S(1)}, u32[]{:S(2)}, u32[]{:S(2)}) collective-permute-start(f32[192,128]{1,0:T(8,128)} %bitcast.57), channel_id=1, source_target_pairs={{0,23},{1,22},{2,21},{3,20},{4,19},{5,18},{6,17},{7,16},{8,31},{9,... | collective-permute-start | bytes 294920 | tf_op jit(solution)/shard_map/ppermute | solution.py:317
  73.3 4.5 %collective-permute-start.19 = (f32[16,256]{1,0:T(8,128)S(1)}, f32[16,256]{1,0:T(8,128)S(1)}, u32[]{:S(2)}, u32[]{:S(2)}) collective-permute-start(f32[16,256]{1,0:T(8,128)S(1)} %broadcast_select_fusion.refs_0_.refs_5_), channel_id=1, source_target_pairs={{0,2},{1,3},{2,0},{3,1},{4,6},{5,7},{6,4},{7,5},{8,10},{9,11},{10,... | collective-permute-start | bytes 49160 | tf_op jit(solution)/shard_map/ppermute | solution.py:317
  76.7 8.0 %collective-permute-start.10 = (f32[192,128]{1,0:T(8,128)}, f32[192,128]{1,0:T(8,128)S(1)}, u32[]{:S(2)}, u32[]{:S(2)}) collective-permute-start(f32[192,128]{1,0:T(8,128)} %bitcast.56), channel_id=1, source_target_pairs={{0,24},{1,25},{2,26},{3,27},{4,28},{5,29},{6,30},{7,31},{8,16},{9,... | collective-permute-start | bytes 294920 | tf_op jit(solution)/shard_map/ppermute | solution.py:317
  77.9 14.0 %collective-permute-start.11 = (f32[192,128]{1,0:T(8,128)}, f32[192,128]{1,0:T(8,128)S(1)}, u32[]{:S(2)}, u32[]{:S(2)}) collective-permute-start(f32[192,128]{1,0:T(8,128)} %bitcast.55), channel_id=1, source_target_pairs={{0,25},{1,24},{2,27},{3,26},{4,29},{5,28},{6,31},{7,30},{8,17},{9,... | collective-permute-start | bytes 294920 | tf_op jit(solution)/shard_map/ppermute | solution.py:317
  78.9 14.6 %collective-permute-start.12 = (f32[192,128]{1,0:T(8,128)}, f32[192,128]{1,0:T(8,128)S(1)}, u32[]{:S(2)}, u32[]{:S(2)}) collective-permute-start(f32[192,128]{1,0:T(8,128)} %bitcast.54), channel_id=1, source_target_pairs={{0,26},{1,27},{2,24},{3,25},{4,30},{5,31},{6,28},{7,29},{8,18},{9,... | collective-permute-start | bytes 294920 | tf_op jit(solution)/shard_map/ppermute | solution.py:317
  80.9 17.7 %collective-permute-start.13 = (f32[192,128]{1,0:T(8,128)}, f32[192,128]{1,0:T(8,128)S(1)}, u32[]{:S(2)}, u32[]{:S(2)}) collective-permute-start(f32[192,128]{1,0:T(8,128)} %bitcast.53), channel_id=1, source_target_pairs={{0,27},{1,26},{2,25},{3,24},{4,31},{5,30},{6,29},{7,28},{8,19},{9,... | collective-permute-start | bytes 294920 | tf_op jit(solution)/shard_map/ppermute | solution.py:317
  84.7 19.1 %collective-permute-start.27 = (f32[192,128]{1,0:T(8,128)}, f32[192,128]{1,0:T(8,128)S(1)}, u32[]{:S(2)}, u32[]{:S(2)}) collective-permute-start(f32[192,128]{1,0:T(8,128)} %bitcast.52), channel_id=1, source_target_pairs={{0,16},{1,17},{2,18},{3,19},{4,20},{5,21},{6,22},{7,23},{8,24},{9,... | collective-permute-start | bytes 294920 | tf_op jit(solution)/shard_map/ppermute | solution.py:317
  91.9 14.7 %collective-permute-start.28 = (f32[192,128]{1,0:T(8,128)}, f32[192,128]{1,0:T(8,128)S(1)}, u32[]{:S(2)}, u32[]{:S(2)}) collective-permute-start(f32[192,128]{1,0:T(8,128)} %bitcast.51), channel_id=1, source_target_pairs={{0,17},{1,16},{2,19},{3,18},{4,21},{5,20},{6,23},{7,22},{8,25},{9,... | collective-permute-start | bytes 294920 | tf_op jit(solution)/shard_map/ppermute | solution.py:317
  93.4 20.3 %collective-permute-start.29 = (f32[192,128]{1,0:T(8,128)}, f32[192,128]{1,0:T(8,128)S(1)}, u32[]{:S(2)}, u32[]{:S(2)}) collective-permute-start(f32[192,128]{1,0:T(8,128)} %bitcast.50), channel_id=1, source_target_pairs={{0,18},{1,19},{2,16},{3,17},{4,22},{5,23},{6,20},{7,21},{8,26},{9,... | collective-permute-start | bytes 294920 | tf_op jit(solution)/shard_map/ppermute | solution.py:317
  98.6 25.2 %collective-permute-start.26 = (f32[128,256]{1,0:T(8,128)}, f32[128,256]{1,0:T(8,128)S(1)}, u32[]{:S(2)}, u32[]{:S(2)}) collective-permute-start(f32[128,256]{1,0:T(8,128)} %stack.1), channel_id=1, source_target_pairs={{0,1},{1,0},{2,3},{3,2},{4,5},{5,4},{6,7},{7,6},{8,9},{9,8},{10,11... | collective-permute-start | bytes 393224 | tf_op jit(solution)/shard_map/ppermute | solution.py:317
  103.8 12.1 %collective-permute-start.30 = (f32[192,128]{1,0:T(8,128)}, f32[192,128]{1,0:T(8,128)S(1)}, u32[]{:S(2)}, u32[]{:S(2)}) collective-permute-start(f32[192,128]{1,0:T(8,128)} %bitcast.49), channel_id=1, source_target_pairs={{0,19},{1,18},{2,17},{3,16},{4,23},{5,22},{6,21},{7,20},{8,27},{9,... | collective-permute-start | bytes 294920 | tf_op jit(solution)/shard_map/ppermute | solution.py:317
  106.6 12.6 %collective-permute-start.31 = (f32[192,128]{1,0:T(8,128)}, f32[192,128]{1,0:T(8,128)S(1)}, u32[]{:S(2)}, u32[]{:S(2)}) collective-permute-start(f32[192,128]{1,0:T(8,128)} %bitcast.48), channel_id=1, source_target_pairs={{0,20},{1,21},{2,22},{3,23},{4,16},{5,17},{6,18},{7,19},{8,28},{9,... | collective-permute-start | bytes 294920 | tf_op jit(solution)/shard_map/ppermute | solution.py:317
  113.8 7.9 %collective-permute-start.32 = (f32[192,128]{1,0:T(8,128)}, f32[192,128]{1,0:T(8,128)S(1)}, u32[]{:S(2)}, u32[]{:S(2)}) collective-permute-start(f32[192,128]{1,0:T(8,128)} %bitcast.47), channel_id=1, source_target_pairs={{0,21},{1,20},{2,23},{3,22},{4,17},{5,16},{6,19},{7,18},{8,29},{9,... | collective-permute-start | bytes 294920 | tf_op jit(solution)/shard_map/ppermute | solution.py:317
  115.9 24.0 %collective-permute-start.14 = (f32[192,128]{1,0:T(8,128)}, f32[192,128]{1,0:T(8,128)S(1)}, u32[]{:S(2)}, u32[]{:S(2)}) collective-permute-start(f32[192,128]{1,0:T(8,128)} %bitcast.46), channel_id=1, source_target_pairs={{0,28},{1,29},{2,30},{3,31},{4,24},{5,25},{6,26},{7,27},{8,20},{9,... | collective-permute-start | bytes 294920 | tf_op jit(solution)/shard_map/ppermute | solution.py:317
  119.2 20.6 %collective-permute-start.15 = (f32[192,128]{1,0:T(8,128)}, f32[192,128]{1,0:T(8,128)S(1)}, u32[]{:S(2)}, u32[]{:S(2)}) collective-permute-start(f32[192,128]{1,0:T(8,128)} %bitcast.45), channel_id=1, source_target_pairs={{0,29},{1,28},{2,31},{3,30},{4,25},{5,24},{6,27},{7,26},{8,21},{9,... | collective-permute-start | bytes 294920 | tf_op jit(solution)/shard_map/ppermute | solution.py:317
  121.6 18.3 %collective-permute-start.16 = (f32[192,128]{1,0:T(8,128)}, f32[192,128]{1,0:T(8,128)S(1)}, u32[]{:S(2)}, u32[]{:S(2)}) collective-permute-start(f32[192,128]{1,0:T(8,128)} %bitcast.44), channel_id=1, source_target_pairs={{0,30},{1,31},{2,28},{3,29},{4,26},{5,27},{6,24},{7,25},{8,22},{9,... | collective-permute-start | bytes 294920 | tf_op jit(solution)/shard_map/ppermute | solution.py:317
  123.8 16.1 %collective-permute-start.17 = (f32[192,128]{1,0:T(8,128)}, f32[192,128]{1,0:T(8,128)S(1)}, u32[]{:S(2)}, u32[]{:S(2)}) collective-permute-start(f32[192,128]{1,0:T(8,128)} %bitcast.43), channel_id=1, source_target_pairs={{0,31},{1,30},{2,29},{3,28},{4,27},{5,26},{6,25},{7,24},{8,23},{9,... | collective-permute-start | bytes 294920 | tf_op jit(solution)/shard_map/ppermute | solution.py:317
  (26 other events, 455.3 us)
